TPU v7x, 32 devices: a whole 2x2x4 slice. The times are simulated.
32 devices in a mesh: grp: 8 (over z, y), mem: 4 (over x, core).
Axes of the slice: x: 2, y: 2, z: 4, core: 2. Of those that a mesh axis runs over, the one named last changes fastest.
Arguments:
- codes: bfloat16 [8192, 1024], P(('grp', 'mem')), as said below
- scales: float32 [8192, 8], P(('grp', 'mem')), may hold values from 0.2 to 2
- cluster_id: int32 [8192], P(('grp', 'mem')), may hold values from 0 to 63, as said below
Outputs:
- smoothed: bfloat16 [8192, 1024], P(('grp', 'mem'))
- dup_mass: bfloat16 [8192], P(('grp', 'mem'))
Inputs may be any that keep to these rules, and one draw needn't show every extreme that they name: `cluster_id`: cluster c belongs to owner group c mod 8. Among the 256 documents of one device, at most 40 belong to clusters of any one owner group, and at most 20 to any one cluster; for each index along mem, some owner group gets exactly 40 from every device of that index, and some cluster of that group exactly 20 from every device of that index. `codes`: documents of one cluster lie near a common direction.
All inputs are finite; a program needn't handle non-finite values.
Results may differ from a plain program's by a relative error of at most 0.0034.
Values may be sent and summed in bfloat16 or wider, within the bound.
No kernel may reach another device: no remote copies, remote signals or barrier semaphores. Data moves between devices by JAX's collectives and lax.ppermute only.
A program may use at most 64 MiB of HBM per device.

v0:
```python
import jax
import jax.numpy as jnp
from jax import lax
from jax.sharding import PartitionSpec as P

CAP = 40


def embed(codes, scales):
    rows, width = codes.shape
    nblk = scales.shape[1]
    x = (codes.astype(jnp.float32).reshape(rows, nblk, width // nblk) * scales[:, :, None]).reshape(
        rows, width
    )
    inv = lax.rsqrt(jnp.mean(x * x, axis=1, keepdims=True) + 1e-06)
    return (x * inv).astype(jnp.bfloat16)


def make_fold(queries, qtags, query_index):
    width = queries.shape[1]

    def accumulate(carry, piece, start):
        keys, ktags = piece
        member_count = keys.shape[0]
        sims = (
            lax.dot_general(
                queries, keys, (((1,), (1,)), ((), ())), preferred_element_type=jnp.float32
            )
            / width
        )
        key_index = jnp.arange(member_count, dtype=jnp.int32)
        keep = (
            (qtags[:, None] == ktags[None, :])
            & (qtags[:, None] >= 0)
            & (query_index[:, None] != key_index[None, :])
        )
        weights = jnp.where(keep, jnp.exp(8.0 * (sims - 1.0)), jnp.float32(0.0))
        den_sum = jnp.sum(weights, axis=1)
        numerator_sum = jnp.dot(
            weights.astype(jnp.bfloat16), keys, preferred_element_type=jnp.float32
        )
        return (den_sum, numerator_sum)

    return accumulate


def local(codes, scales, cluster_id):
    rows, width = codes.shape
    groups = lax.axis_size("grp")
    member = lax.axis_index("mem")
    embedding_rows = embed(codes, scales)
    owner = cluster_id % groups
    onehot = (owner[:, None] == jnp.arange(groups, dtype=jnp.int32)[None, :]).astype(jnp.int32)
    ranks = jnp.cumsum(onehot, axis=0) - 1
    slot = jnp.sum(ranks * onehot, axis=1)
    target = owner * CAP + slot
    outbox = (
        jnp.zeros((groups * CAP, width), jnp.bfloat16)
        .at[target]
        .set(embedding_rows)
        .reshape(groups, CAP, width)
    )
    outtags = (
        jnp.full((groups * CAP,), -1.0, jnp.float32)
        .at[target]
        .set(cluster_id.astype(jnp.float32))
        .astype(jnp.bfloat16)
        .reshape(groups, CAP)
    )
    slots = groups * CAP
    inbox, incoming_tags = (
        lax.all_to_all(outbox, "grp", split_axis=0, concat_axis=0, tiled=True),
        lax.all_to_all(outtags, "grp", split_axis=0, concat_axis=0, tiled=True),
    )
    queries = inbox.reshape(slots, width)
    qtags = incoming_tags.reshape(slots)
    start_carry = (jnp.zeros((slots,), jnp.float32), jnp.zeros((slots, width), jnp.float32))
    query_index = member * slots + jnp.arange(slots, dtype=jnp.int32)
    accumulate = make_fold(queries, qtags, query_index)
    den_sum, numerator_sum = accumulate(
        start_carry,
        (
            lax.all_gather(queries, "mem", axis=0, tiled=True),
            lax.all_gather(qtags, "mem", axis=0, tiled=True),
        ),
        jnp.int32(0),
    )
    den = 1.0 + den_sum
    result = ((queries.astype(jnp.float32) + numerator_sum) / den[:, None]).astype(jnp.bfloat16)
    mass = jnp.log(den).astype(jnp.bfloat16)
    back_rows, back_mass = (
        lax.all_to_all(
            result.reshape(groups, CAP, width), "grp", split_axis=0, concat_axis=0, tiled=True
        ),
        lax.all_to_all(mass.reshape(groups, CAP), "grp", split_axis=0, concat_axis=0, tiled=True),
    )
    smoothed = back_rows.reshape(slots, width)[target]
    dup_mass = back_mass.reshape(slots)[target]
    return (smoothed, dup_mass)


def solution(mesh):
    placed = (P(("grp", "mem"), None), P(("grp", "mem"), None), P(("grp", "mem")))
    return jax.shard_map(
        local,
        mesh=mesh,
        in_specs=placed,
        out_specs=(P(("grp", "mem"), None), P(("grp", "mem"))),
        check_vma=False,
    )
```

profile of v0, /device:TPU:0, one launch (start us, length us, event | category | flops | bytes accessed | tf_op | source)
XLA Modules:
  0.0 107.8 jit_solution(3126384838830802530)
XLA Ops:
  7.2 0.8 fusion.14
  8.0 0.6 reduce-window.6
  8.9 0.8 copy.7
  9.8 0.3 mul.43
  10.1 0.3 multiply_reduce_fusion
  10.4 2.0 %scatter_custom_fusion = bf16[320,1024]{1,0:T(8,128)(2,1)S(1)} fusion(s32[256]{0:T(256)S(1)} %compare_select_fusion, f32[32,8,8,128]{3,2,1,0:T(8,128)S(1)} %bitcast.26, bf16[256,1024]{1,0:T(8,128)(2,1)S(1)} %copy-done.1, f32[256]{0:T(256)S(1)} %add_rsqrt_fusion, bf16[]{:T(256)} %constant.16.clone.1), kind=kCustom, calls=%fused_computation.17 | custom fusion | flops 1048576 | bytes 2229250 | tf_op jit(solution)/shard_map/scatter | solution.py:60
  12.4 24.9 %all_to_all.26 = bf16[8,40,1024]{2,1,0:T(8,128)(2,1)} all-to-all(bf16[8,40,1024]{2,1,0:T(8,128)(2,1)S(1)} %bitcast.30), channel_id=1, replica_groups=mesh['grp'=8,'mem'=4] {'grp'}, dimensions={0} | all-to-all | bytes 1310720 | tf_op jit(solution)/shard_map/all_to_all | solution.py:72
  37.3 1.4 %scatter_custom_fusion.1 = f32[320]{0:T(512)S(1)} fusion(s32[256]{0:T(256)S(1)} %compare_select_fusion, f32[256]{0:T(256)S(1)} %get-tuple-element.4, f32[]{:T(128)} %constant.49.clone.1), kind=kCustom, calls=%fused_computation.35 | custom fusion | bytes 1284 | tf_op jit(solution)/shard_map/scatter | solution.py:66
  38.7 0.7 all_to_all.21
  39.4 3.3 %all-to-all-start.1 = ((bf16[8,1,40]{2,1,0:T(2,128)(2,1)}), bf16[8,1,40]{2,1,0:T(2,128)(2,1)S(1)}, u32[]{:S(2)}, u32[]{:S(2)}) async-start(bf16[8,1,40]{2,1,0:T(2,128)(2,1)} %all_to_all.21), calls=%async_computation.1 | async-start | bytes 8192 | tf_op jit(solution)/shard_map/all_to_all | solution.py:73
  42.8 0.6 dynamic-slice
  44.0 5.1 %all-to-all-done.1 = bf16[8,1,40]{2,1,0:T(2,128)(2,1)S(1)} async-done(((bf16[8,1,40]{2,1,0:T(2,128)(2,1)}), bf16[8,1,40]{2,1,0:T(2,128)(2,1)S(1)}, u32[]{:S(2)}, u32[]{:S(2)}) %all-to-all-start.1) | async-done | bytes 672 | tf_op jit(solution)/shard_map/all_to_all | solution.py:73
  49.2 0.3 dynamic-update-slice
  49.4 6.1 %all-reduce = bf16[1280]{0:T(1024)(128)(2,1)S(1)} all-reduce(bf16[1280]{0:T(1024)(128)(2,1)S(1)} %dynamic-update-slice), channel_id=1, replica_groups=mesh['grp'=8,'mem'=4] {'mem'}, use_global_device_ids=true, to_apply=%add | all-reduce | flops 1280 | bytes 5120
  55.6 6.2 %all-gather.2.cloned.1.call-done = bf16[1280,1024]{1,0:T(8,128)(2,1)} async-done(((bf16[320,1024]{1,0:T(8,128)(2,1)}), bf16[1280,1024]{1,0:T(8,128)(2,1)}) %all-gather.2.cloned.1.call-update) | async-done | bytes 2621456 | tf_op jit(solution)/shard_map/all_gather | solution.py:83
  61.8 4.5 %fusion.15 = (f32[320]{0:T(512)S(1)}, bf16[320,1280]{1,0:T(8,128)(2,1)}) fusion(bf16[320,1024]{1,0:T(8,128)(2,1)} %bitcast.28, bf16[1280,1024]{1,0:T(8,128)(2,1)} %all-gather.2.cloned.1.call-done, s32[320]{0:T(512)S(1)} %iota_add_fusion, pred[320]{0:T(512)(128)(4,1)S(1)} %broadcast_compare_fusion, bf16[1280]{0:T(1024)(128)(2,1)S(1)} %all-reduce, ...), kind=kOutput, calls=%fused_computation.40 | convolution fusion | flops 843775680 | bytes 4102080 | tf_op jit(solution)/shard_map/dot_general | solution.py:26
  66.3 0.7 convert_element_type.50
  67.0 5.5 %all-to-all-start.3 = ((bf16[8,1,40]{2,1,0:T(2,128)(2,1)}), bf16[8,1,40]{2,1,0:T(2,128)(2,1)S(1)}, u32[]{:S(2)}, u32[]{:S(2)}) async-start(bf16[8,1,40]{2,1,0:T(2,128)(2,1)} %convert_element_type.50), calls=%async_computation.3 | async-start | bytes 8192 | tf_op jit(solution)/shard_map/all_to_all | solution.py:95
  72.5 3.1 %divide_convert_fusion = bf16[320,1024]{1,0:T(8,128)(2,1)} fusion(bf16[1280,1024]{1,0:T(8,128)(2,1)S(1)} %copy-done.2, bf16[320,1024]{1,0:T(8,128)(2,1)S(1)} %bitcast.29, bf16[320,1280]{1,0:T(8,128)(2,1)} %get-tuple-element.7, f32[320]{0:T(512)S(1)} %get-tuple-element.3), kind=kOutput, calls=%fused_computation.12 | convolution fusion | flops 840171520 | bytes 4752640 | tf_op jit(solution)/shard_map/dot_general | solution.py:39
  75.6 3.3 %all-to-all-done.3 = bf16[8,1,40]{2,1,0:T(2,128)(2,1)S(1)} async-done(((bf16[8,1,40]{2,1,0:T(2,128)(2,1)}), bf16[8,1,40]{2,1,0:T(2,128)(2,1)S(1)}, u32[]{:S(2)}, u32[]{:S(2)}) %all-to-all-start.3) | async-done | bytes 672 | tf_op jit(solution)/shard_map/all_to_all | solution.py:95
  78.9 3.5 %all-to-all-start.2 = ((bf16[8,40,1024]{2,1,0:T(8,128)(2,1)}), bf16[8,40,1024]{2,1,0:T(8,128)(2,1)S(1)}, u32[]{:S(2)}, u32[]{:S(2)}) async-start(bf16[8,40,1024]{2,1,0:T(8,128)(2,1)} %bitcast.6), calls=%async_computation.2 | async-start | bytes 1310720 | tf_op jit(solution)/shard_map/all_to_all | solution.py:92
  82.6 2.5 %gather_fusion.1 = bf16[256]{0:T(256)(128)(2,1)} fusion(bf16[320]{0:T(512)(128)(2,1)S(1)} %reshape.103, s32[1024]{0:T(1024)S(1)} %pad_clamp_fusion), kind=kCustom, calls=%fused_computation.1 | custom fusion | bytes 2048 | tf_op jit(solution)/shard_map/gather | solution.py:98
  85.0 13.9 %all-to-all-done.2 = bf16[8,40,1024]{2,1,0:T(8,128)(2,1)S(1)} async-done(((bf16[8,40,1024]{2,1,0:T(8,128)(2,1)}), bf16[8,40,1024]{2,1,0:T(8,128)(2,1)S(1)}, u32[]{:S(2)}, u32[]{:S(2)}) %all-to-all-start.2) | async-done | bytes 655392 | tf_op jit(solution)/shard_map/all_to_all | solution.py:92
  98.9 2.0 %gather_fusion = bf16[256,1024]{1,0:T(8,128)(2,1)} fusion(bf16[320,1024]{1,0:T(8,128)(2,1)S(1)} %bitcast.24, s32[1024]{0:T(1024)S(1)} %pad_clamp_fusion), kind=kCustom, calls=%fused_computation | custom fusion | bytes 1049600 | tf_op jit(solution)/shard_map/gather | solution.py:97
  (27 shorter events, 0.7 us)
Async XLA Ops:
  7.2 2.9 %copy-start.1 = (bf16[256,1024]{1,0:T(8,128)(2,1)S(1)}, bf16[256,1024]{1,0:T(8,128)(2,1)}, u32[]{:S(2)}) copy-start(bf16[256,1024]{1,0:T(8,128)(2,1)} %param.3) | copy-start | bytes 1572868
  7.2 54.6 %all-gather.2.cloned.1.call-start = ((), (), s32[]{:S(2)}) async-start(), calls=%async_computation.4 | async-start | bytes 3276800 | tf_op jit(solution)/shard_map/all_gather | solution.py:83
  10.4 32.4 %copy-start.3 = (u32[32]{0:T(128)S(1)}, u32[32]{0:T(128)}, u32[]{:S(2)}) copy-start(u32[32]{0:T(128)} %constant.55) | copy-start | bytes 388
  39.4 9.6 %all-to-all-start.1 = ((bf16[8,1,40]{2,1,0:T(2,128)(2,1)}), bf16[8,1,40]{2,1,0:T(2,128)(2,1)S(1)}, u32[]{:S(2)}, u32[]{:S(2)}) async-start(bf16[8,1,40]{2,1,0:T(2,128)(2,1)} %all_to_all.21), calls=%async_computation.1 | async-start | bytes 8192 | tf_op jit(solution)/shard_map/all_to_all | solution.py:73
  55.6 16.9 %copy-start = (bf16[8,40,1024]{2,1,0:T(8,128)(2,1)S(1)}, bf16[8,40,1024]{2,1,0:T(8,128)(2,1)}, u32[]{:S(2)}) copy-start(bf16[8,40,1024]{2,1,0:T(8,128)(2,1)} %all_to_all.26) | copy-start | bytes 1966084
  61.8 10.7 %copy-start.2 = (bf16[1280,1024]{1,0:T(8,128)(2,1)S(1)}, bf16[1280,1024]{1,0:T(8,128)(2,1)}, u32[]{:S(2)}) copy-start(bf16[1280,1024]{1,0:T(8,128)(2,1)} %all-gather.2.cloned.1.call-done) | copy-start | bytes 7864324
  67.0 11.9 %all-to-all-start.3 = ((bf16[8,1,40]{2,1,0:T(2,128)(2,1)}), bf16[8,1,40]{2,1,0:T(2,128)(2,1)S(1)}, u32[]{:S(2)}, u32[]{:S(2)}) async-start(bf16[8,1,40]{2,1,0:T(2,128)(2,1)} %convert_element_type.50), calls=%async_computation.3 | async-start | bytes 8192 | tf_op jit(solution)/shard_map/all_to_all | solution.py:95
  78.9 20.1 %all-to-all-start.2 = ((bf16[8,40,1024]{2,1,0:T(8,128)(2,1)}), bf16[8,40,1024]{2,1,0:T(8,128)(2,1)S(1)}, u32[]{:S(2)}, u32[]{:S(2)}) async-start(bf16[8,40,1024]{2,1,0:T(8,128)(2,1)} %bitcast.6), calls=%async_computation.2 | async-start | bytes 1310720 | tf_op jit(solution)/shard_map/all_to_all | solution.py:92
Sparse Core Ops, SparseCore 0:
  37.4 24.3 all-gather.1
where the time goes:
time: 108 us
  blocking collectives  31 us (29%)
  waiting for transfers between devices  28.5 us (26%)
  between operations  14.8 us (14%)
  starting transfers between devices  12.4 us (11%)
  local copies, waits for them, and re-layouts  9.58 us (9%)
  matrix products  7.54 us (7%)
  other arithmetic  3.82 us (4%)
    all_to_all x1, blocking collectives, local(): lax.all_to_all(outbox, 'grp', split_axis=0, concat_axis=0, tiled=True)  24.9 us
    all_to_all x1, waiting for transfers between devices, local(): lax.all_to_all(result.reshape(groups, CAP, width), 'grp', split_axis=0, c...  13.9 us
    all_gather x1, waiting for transfers between devices, local(): lax.all_gather(queries, 'mem', axis=0, tiled=True)  6.2 us
    unnamed x1, blocking collectives  6.14 us
    all_to_all x1, starting transfers between devices, local(): lax.all_to_all(mass.reshape(groups, CAP), 'grp', split_axis=0, concat_axi...  5.52 us
    all_to_all x1, waiting for transfers between devices, local(): lax.all_to_all(outtags, 'grp', split_axis=0, concat_axis=0, tiled=True)  5.05 us
    dot_general x1, matrix products, accumulate(): lax.dot_general(queries, keys, (((1,), (1,)), ((), ())), preferred_elemen...  4.49 us
    all_to_all x1, starting transfers between devices, local(): lax.all_to_all(result.reshape(groups, CAP, width), 'grp', split_axis=0, c...  3.54 us
  transfers between devices with their start and end apart: 4, of which 4 were waited for; matrix products, arithmetic and copies ran while one was open for 7% of the time, Pallas kernels for 0%

commit v1 on v0

v1 whole, which is shorter than its diff:
```python
import functools

import jax
import jax.numpy as jnp
from jax import lax
from jax.experimental import pallas as pl
from jax.experimental.pallas import tpu as pltpu
from jax.sharding import PartitionSpec as P

CAP = 40
LANES = 128
VMEM = pl.BlockSpec(memory_space=pltpu.VMEM)


def as_column(row):
    n = row.shape[1]
    same = lax.broadcasted_iota(jnp.int32, (n, n), 0) == lax.broadcasted_iota(jnp.int32, (n, n), 1)
    return jnp.sum(jnp.where(same, jnp.broadcast_to(row, (n, n)), 0.0), axis=1, keepdims=True)


def pack_kernel(groups, codes_ref, scales_ref, cluster_ref, select_ref, *out_refs):
    rows, width = codes_ref.shape
    nblk = scales_ref.shape[0]
    step = width // nblk
    scales = scales_ref[...].T
    parts = []
    total = None
    for b in range(nblk):
        x = codes_ref[:, b * step : (b + 1) * step].astype(jnp.float32) * scales[:, b : b + 1]
        parts.append(x)
        square = x * x
        total = square if total is None else total + square
    inv = lax.rsqrt(jnp.sum(total, axis=1, keepdims=True) / width + 1e-06)
    cluster = cluster_ref[...]
    owner = lax.rem(cluster, groups)
    step_row = lax.bitwise_xor(owner, lax.axis_index("grp"))
    step_f = step_row.astype(jnp.float32)
    step_col = as_column(step_f)
    before = lax.broadcasted_iota(jnp.int32, (rows, rows), 0) < lax.broadcasted_iota(
        jnp.int32, (rows, rows), 1
    )
    rank = jnp.sum(
        jnp.where(before & (step_col == step_f), 1.0, 0.0), axis=0, keepdims=True
    ).astype(jnp.int32)
    target = step_row * CAP + rank
    slots = groups * CAP
    hit = lax.broadcasted_iota(jnp.int32, (slots, rows), 0) == target
    select = jnp.where(hit, 1.0, 0.0).astype(jnp.bfloat16)
    select_ref[...] = select
    tags = jnp.sum(jnp.where(hit, cluster.astype(jnp.float32) + 1.0, 0.0), axis=1, keepdims=True) - 1.0
    tags = jnp.broadcast_to(tags, (slots, LANES)).astype(jnp.bfloat16)
    for s in range(groups):
        out_refs[s][:, width:] = tags[s * CAP : (s + 1) * CAP]
    for b in range(nblk):
        e = (parts[b] * inv).astype(jnp.bfloat16)
        packed = jnp.dot(select, e, preferred_element_type=jnp.float32).astype(jnp.bfloat16)
        for s in range(groups):
            out_refs[s][:, b * step : (b + 1) * step] = packed[s * CAP : (s + 1) * CAP]


def smooth_kernel(groups, pieces, *refs):
    in_refs, out_refs, keys = refs[:pieces], refs[pieces : pieces + groups], refs[-1]
    width = in_refs[0].shape[1] - LANES
    for p in range(pieces):
        keys[p * CAP : (p + 1) * CAP, :] = in_refs[p][...]
    slots, count = groups * CAP, pieces * CAP
    queries = keys[:slots, :width]
    first = jnp.where(lax.broadcasted_iota(jnp.int32, (8, LANES), 1) == 0, 1.0, 0.0).astype(jnp.bfloat16)
    ktags = lax.dot_general(
        first, keys[:, width:], (((1,), (1,)), ((), ())), preferred_element_type=jnp.float32
    )[:1]
    qtags = keys[:slots, width : width + 1].astype(jnp.float32)
    sims = (
        lax.dot_general(
            queries, keys[:, :width], (((1,), (1,)), ((), ())), preferred_element_type=jnp.float32
        )
        / width
    )
    keep = (
        (qtags == ktags)
        & (qtags >= 0.0)
        & (
            lax.broadcasted_iota(jnp.int32, (slots, count), 0)
            != lax.broadcasted_iota(jnp.int32, (slots, count), 1)
        )
    )
    weights = jnp.where(keep, jnp.exp(8.0 * (sims - 1.0)), 0.0)
    den = 1.0 + jnp.sum(weights, axis=1, keepdims=True)
    num = jnp.dot(
        weights.astype(jnp.bfloat16), keys[:, :width], preferred_element_type=jnp.float32
    )
    result = ((queries.astype(jnp.float32) + num) / den).astype(jnp.bfloat16)
    mass = jnp.broadcast_to(jnp.log(den), (slots, LANES)).astype(jnp.bfloat16)
    for s in range(groups):
        out_refs[s][:, :width] = result[s * CAP : (s + 1) * CAP]
        out_refs[s][:, width:] = mass[s * CAP : (s + 1) * CAP]


def unpack_kernel(groups, select_ref, *refs):
    in_refs, (smoothed_ref, mass_ref, back) = refs[:groups], refs[groups:]
    width = smoothed_ref.shape[1]
    for s in range(groups):
        back[s * CAP : (s + 1) * CAP, :] = in_refs[s][...]
    select = select_ref[...]
    over_slots = (((0,), (0,)), ((), ()))
    smoothed_ref[...] = lax.dot_general(
        select, back[:, :width], over_slots, preferred_element_type=jnp.float32
    ).astype(jnp.bfloat16)
    mass_ref[...] = lax.dot_general(
        back[:, width:], select, over_slots, preferred_element_type=jnp.float32
    )[:1].astype(jnp.bfloat16)


def local(codes, scales, cluster_id):
    rows, width = codes.shape
    groups, members = lax.axis_size("grp"), lax.axis_size("mem")
    slots = groups * CAP
    piece = jax.ShapeDtypeStruct((CAP, width + LANES), jnp.bfloat16)

    def swap(value, axis, step):
        size = lax.axis_size(axis)
        return lax.ppermute(value, axis, [(i, i ^ step) for i in range(size)])

    select, *outbox = pl.pallas_call(
        functools.partial(pack_kernel, groups),
        out_shape=[jax.ShapeDtypeStruct((slots, rows), jnp.bfloat16)] + [piece] * groups,
        in_specs=[VMEM] * 3,
        out_specs=[VMEM] * (1 + groups),
        name="pack",
    )(codes, scales.T, cluster_id.reshape(1, rows))
    inbox = [outbox[0]] + [swap(outbox[s], "grp", s) for s in range(1, groups)]
    held = list(inbox)
    for step in range(2, members, 2):
        held += [swap(p, "mem", step) for p in inbox]
    held += [swap(p, "mem", 1) for p in held]
    results = pl.pallas_call(
        functools.partial(smooth_kernel, groups, len(held)),
        out_shape=[piece] * groups,
        in_specs=[VMEM] * len(held),
        out_specs=[VMEM] * groups,
        scratch_shapes=[pltpu.VMEM((len(held) * CAP, width + LANES), jnp.bfloat16)],
        name="smooth",
    )(*held)
    back = [results[0]] + [swap(results[s], "grp", s) for s in range(1, groups)]
    smoothed, mass = pl.pallas_call(
        functools.partial(unpack_kernel, groups),
        out_shape=[
            jax.ShapeDtypeStruct((rows, width), jnp.bfloat16),
            jax.ShapeDtypeStruct((1, rows), jnp.bfloat16),
        ],
        in_specs=[VMEM] * (1 + groups),
        out_specs=[VMEM] * 2,
        scratch_shapes=[pltpu.VMEM((slots, width + LANES), jnp.bfloat16)],
        name="unpack",
    )(select, *back)
    return (smoothed, mass.reshape(rows))


def solution(mesh):
    placed = (P(("grp", "mem"), None), P(("grp", "mem"), None), P(("grp", "mem")))
    return jax.shard_map(
        local,
        mesh=mesh,
        in_specs=placed,
        out_specs=(P(("grp", "mem"), None), P(("grp", "mem"))),
        check_vma=False,
    )
```

time: 108 us -> 76.6 us (0.71)
  blocking collectives: 31 us -> 0 us
  starting transfers between devices: 12.4 us -> 37.3 us
  between operations: 14.8 us -> 1.05 us
  Pallas kernels: 0 us -> 10.5 us
  matrix products: 7.54 us -> 0 us
  local copies, waits for them, and re-layouts: 9.58 us -> 2.28 us
  waiting for transfers between devices: 28.5 us -> 24.1 us
  other arithmetic: 3.82 us -> 0.53 us
    ppermute x0 -> x38, starting transfers between devices: none -> 37.3 us  [swap(): return lax.ppermute(value, axis, [(i, i ^ step) for i in range(size)])]
    all_to_all x1 -> x0, blocking collectives: 24.9 us -> none  [local(): lax.all_to_all(outbox, 'grp', split_axis=0, concat_axis=0, tiled=True)]
    ppermute x0 -> x38, waiting for transfers between devices: none -> 24.1 us  [swap(): return lax.ppermute(value, axis, [(i, i ^ step) for i in range(size)])]
    all_to_all x3 -> x0, waiting for transfers between devices: 22.3 us -> none  [the longest x1 13.9 us: local(): lax.all_to_all(result.reshape(groups, CAP, width), 'grp', split_axis=0, c...]
    all_to_all x3 -> x0, starting transfers between devices: 12.4 us -> none  [the longest x1 5.52 us: local(): lax.all_to_all(mass.reshape(groups, CAP), 'grp', split_axis=0, concat_axi...]
    pallas_call x0 -> x3, Pallas kernels: none -> 10.5 us  [the longest x1 4.81 us: local(): pl.pallas_call(functools.partial(smooth_kernel, groups, len(held)), out_s...]
    dot_general x2 -> x0, matrix products: 7.54 us -> none  [the longest x1 4.49 us: accumulate(): lax.dot_general(queries, keys, (((1,), (1,)), ((), ())), preferred_elemen...]
    all_gather x1 -> x0, waiting for transfers between devices: 6.2 us -> none  [local(): lax.all_gather(queries, 'mem', axis=0, tiled=True)]
  transfers between devices with their start and end apart: 4 -> 38, of which waited for: 4 -> 13; matrix products, arithmetic and copies ran while one was open for 7% -> 0% of each run, Pallas kernels for 0% -> 0%
where the time goes in v1:
time: 76.6 us; the launch traced here: 75.8 us
  starting transfers between devices  37.3 us (49%)
  waiting for transfers between devices  24.1 us (31%)
  Pallas kernels  10.5 us (14%)
  local copies, waits for them, and re-layouts  2.28 us (3%)
  between operations  1.05 us (1%)
    ppermute x38, starting transfers between devices, swap(): return lax.ppermute(value, axis, [(i, i ^ step) for i in range(size)])  37.3 us
    ppermute x38, waiting for transfers between devices, swap(): return lax.ppermute(value, axis, [(i, i ^ step) for i in range(size)])  24.1 us
    pallas_call x1, Pallas kernels, local(): pl.pallas_call(functools.partial(smooth_kernel, groups, len(held)), out_s...  4.81 us
    pallas_call x1, Pallas kernels, local(): pl.pallas_call(functools.partial(pack_kernel, groups), out_shape=[jax.Sha...  3.14 us
    pallas_call x1, Pallas kernels, local(): pl.pallas_call(functools.partial(unpack_kernel, groups), out_shape=[jax.S...  2.53 us
    unnamed x78, local copies, waits for them, and re-layouts  2.28 us
  transfers between devices with their start and end apart: 38, of which 13 were waited for; matrix products, arithmetic and copies ran while one was open for 0% of the time, Pallas kernels for 0%

profile of v1, /device:TPU:0, one launch (start us, length us, event | category | flops | bytes accessed | tf_op | source)
XLA Modules:
  0.0 75.8 jit_solution(6930637204304954705)
XLA Ops:
  0.6 3.1 %pack.1 = (bf16[320,256]{1,0:T(8,128)(2,1)}, bf16[40,1152]{1,0:T(8,128)(2,1)}, bf16[40,1152]{1,0:T(8,128)(2,1)}, bf16[40,1152]{1,0:T(8,128)(2,1)}, bf16[40,1152]...) custom-call(bf16[256,1024]{1,0:T(8,128)(2,1)} %codes_ref.1, ...), custom_call_target="tpu_custom_call" | custom-call | tf_op jit(solution)/shard_map/pack/pallas_call | solution.py:124
  3.8 3.0 %collective-permute-start = (bf16[40,1152]{1,0:T(8,128)(2,1)}, bf16[40,1152]{1,0:T(8,128)(2,1)S(1)}, u32[]{:S(2)}, u32[]{:S(2)}) collective-permute-start(bf16[40,1152]{1,0:T(8,128)(2,1)} %get-tuple-element.23), channel_id=1, source_target_pairs={{0,4},{4,0},{8,12},{12,8},{16,20},{20,16},{24,28},{28,24},{1,5},{5... | collective-permute-start | bytes 276488 | tf_op jit(solution)/shard_map/ppermute | solution.py:122
  6.7 1.6 %collective-permute-start.1 = (bf16[40,1152]{1,0:T(8,128)(2,1)}, bf16[40,1152]{1,0:T(8,128)(2,1)S(1)}, u32[]{:S(2)}, u32[]{:S(2)}) collective-permute-start(bf16[40,1152]{1,0:T(8,128)(2,1)} %get-tuple-element.24), channel_id=1, source_target_pairs={{0,8},{4,12},{8,0},{12,4},{16,24},{20,28},{24,16},{28,20},{1,9},{5... | collective-permute-start | bytes 276488 | tf_op jit(solution)/shard_map/ppermute | solution.py:122
  8.3 3.0 %collective-permute-start.3 = (bf16[40,1152]{1,0:T(8,128)(2,1)}, bf16[40,1152]{1,0:T(8,128)(2,1)S(1)}, u32[]{:S(2)}, u32[]{:S(2)}) collective-permute-start(bf16[40,1152]{1,0:T(8,128)(2,1)} %get-tuple-element.26), channel_id=1, source_target_pairs={{0,16},{4,20},{8,24},{12,28},{16,0},{20,4},{24,8},{28,12},{1,17},{... | collective-permute-start | bytes 276488 | tf_op jit(solution)/shard_map/ppermute | solution.py:122
  11.3 1.3 %collective-permute-start.4 = (bf16[40,1152]{1,0:T(8,128)(2,1)}, bf16[40,1152]{1,0:T(8,128)(2,1)S(1)}, u32[]{:S(2)}, u32[]{:S(2)}) collective-permute-start(bf16[40,1152]{1,0:T(8,128)(2,1)} %get-tuple-element.27), channel_id=1, source_target_pairs={{0,20},{4,16},{8,28},{12,24},{16,4},{20,0},{24,12},{28,8},{1,21},{... | collective-permute-start | bytes 276488 | tf_op jit(solution)/shard_map/ppermute | solution.py:122
  12.6 3.6 %collective-permute-start.5 = (bf16[40,1152]{1,0:T(8,128)(2,1)}, bf16[40,1152]{1,0:T(8,128)(2,1)S(1)}, u32[]{:S(2)}, u32[]{:S(2)}) collective-permute-start(bf16[40,1152]{1,0:T(8,128)(2,1)} %get-tuple-element.28), channel_id=1, source_target_pairs={{0,24},{4,28},{8,16},{12,20},{16,8},{20,12},{24,0},{28,4},{1,25},{... | collective-permute-start | bytes 276488 | tf_op jit(solution)/shard_map/ppermute | solution.py:122
  16.3 1.6 %collective-permute-start.7 = (bf16[40,1152]{1,0:T(8,128)(2,1)}, bf16[40,1152]{1,0:T(8,128)(2,1)S(1)}, u32[]{:S(2)}, u32[]{:S(2)}) collective-permute-start(bf16[40,1152]{1,0:T(8,128)(2,1)} %get-tuple-element.22.refs_0_), channel_id=1, source_target_pairs={{0,2},{1,3},{2,0},{3,1},{4,6},{5,7},{6,4},{7,5},{8,10},{9,11},{10,... | collective-permute-start | bytes 276488 | tf_op jit(solution)/shard_map/ppermute | solution.py:122
  18.0 8.0 %collective-permute-done.4.refs_5_ = bf16[40,1152]{1,0:T(8,128)(2,1)S(1)} collective-permute-done((bf16[40,1152]{1,0:T(8,128)(2,1)}, bf16[40,1152]{1,0:T(8,128)(2,1)S(1)}, u32[]{:S(2)}, u32[]{:S(2)}) %collective-permute-start.4) | collective-permute-done | bytes 92192 | tf_op jit(solution)/shard_map/ppermute | solution.py:122
  26.0 1.6 %collective-permute-start.8 = (bf16[40,1152]{1,0:T(8,128)(2,1)S(1)}, bf16[40,1152]{1,0:T(8,128)(2,1)S(1)}, u32[]{:S(2)}, u32[]{:S(2)}) collective-permute-start(bf16[40,1152]{1,0:T(8,128)(2,1)S(1)} %collective-permute-done.refs_1_), channel_id=1, source_target_pairs={{0,2},{1,3},{2,0},{3,1},{4,6},{5,7},{6,4},{7,5},{8,10},{9,11},{10,... | collective-permute-start | bytes 276488 | tf_op jit(solution)/shard_map/ppermute | solution.py:122
  28.3 1.5 %collective-permute-start.10 = (bf16[40,1152]{1,0:T(8,128)(2,1)S(1)}, bf16[40,1152]{1,0:T(8,128)(2,1)S(1)}, u32[]{:S(2)}, u32[]{:S(2)}) collective-permute-start(bf16[40,1152]{1,0:T(8,128)(2,1)S(1)} %collective-permute-done.2.refs_3_), channel_id=1, source_target_pairs={{0,2},{1,3},{2,0},{3,1},{4,6},{5,7},{6,4},{7,5},{8,10},{9,11},{10,... | collective-permute-start | bytes 276488 | tf_op jit(solution)/shard_map/ppermute | solution.py:122
  29.8 1.6 %collective-permute-done.8.refs_9_ = bf16[40,1152]{1,0:T(8,128)(2,1)S(1)} collective-permute-done((bf16[40,1152]{1,0:T(8,128)(2,1)S(1)}, bf16[40,1152]{1,0:T(8,128)(2,1)S(1)}, u32[]{:S(2)}, u32[]{:S(2)}) %collective-permute-start.8) | collective-permute-done | bytes 92192 | tf_op jit(solution)/shard_map/ppermute | solution.py:122
  31.5 1.6 %collective-permute-start.11 = (bf16[40,1152]{1,0:T(8,128)(2,1)S(1)}, bf16[40,1152]{1,0:T(8,128)(2,1)S(1)}, u32[]{:S(2)}, u32[]{:S(2)}) collective-permute-start(bf16[40,1152]{1,0:T(8,128)(2,1)S(1)} %collective-permute-done.3.refs_4_), channel_id=1, source_target_pairs={{0,2},{1,3},{2,0},{3,1},{4,6},{5,7},{6,4},{7,5},{8,10},{9,11},{10,... | collective-permute-start | bytes 276488 | tf_op jit(solution)/shard_map/ppermute | solution.py:122
  33.5 1.6 %collective-permute-start.12 = (bf16[40,1152]{1,0:T(8,128)(2,1)S(1)}, bf16[40,1152]{1,0:T(8,128)(2,1)S(1)}, u32[]{:S(2)}, u32[]{:S(2)}) collective-permute-start(bf16[40,1152]{1,0:T(8,128)(2,1)S(1)} %collective-permute-done.4.refs_5_), channel_id=1, source_target_pairs={{0,2},{1,3},{2,0},{3,1},{4,6},{5,7},{6,4},{7,5},{8,10},{9,11},{10,... | collective-permute-start | bytes 276488 | tf_op jit(solution)/shard_map/ppermute | solution.py:122
  35.4 1.5 %collective-permute-start.13 = (bf16[40,1152]{1,0:T(8,128)(2,1)S(1)}, bf16[40,1152]{1,0:T(8,128)(2,1)S(1)}, u32[]{:S(2)}, u32[]{:S(2)}) collective-permute-start(bf16[40,1152]{1,0:T(8,128)(2,1)S(1)} %collective-permute-done.5.refs_6_), channel_id=1, source_target_pairs={{0,2},{1,3},{2,0},{3,1},{4,6},{5,7},{6,4},{7,5},{8,10},{9,11},{10,... | collective-permute-start | bytes 276488 | tf_op jit(solution)/shard_map/ppermute | solution.py:122
  37.4 1.5 %collective-permute-start.14 = (bf16[40,1152]{1,0:T(8,128)(2,1)S(1)}, bf16[40,1152]{1,0:T(8,128)(2,1)S(1)}, u32[]{:S(2)}, u32[]{:S(2)}) collective-permute-start(bf16[40,1152]{1,0:T(8,128)(2,1)S(1)} %collective-permute-done.6.refs_7_), channel_id=1, source_target_pairs={{0,2},{1,3},{2,0},{3,1},{4,6},{5,7},{6,4},{7,5},{8,10},{9,11},{10,... | collective-permute-start | bytes 276488 | tf_op jit(solution)/shard_map/ppermute | solution.py:122
  39.9 1.5 %collective-permute-done.13.refs_14_ = bf16[40,1152]{1,0:T(8,128)(2,1)S(1)} collective-permute-done((bf16[40,1152]{1,0:T(8,128)(2,1)S(1)}, bf16[40,1152]{1,0:T(8,128)(2,1)S(1)}, u32[]{:S(2)}, u32[]{:S(2)}) %collective-permute-start.13) | collective-permute-done | bytes 92192 | tf_op jit(solution)/shard_map/ppermute | solution.py:122
  41.9 1.1 %collective-permute-done.14.refs_15_ = bf16[40,1152]{1,0:T(8,128)(2,1)S(1)} collective-permute-done((bf16[40,1152]{1,0:T(8,128)(2,1)S(1)}, bf16[40,1152]{1,0:T(8,128)(2,1)S(1)}, u32[]{:S(2)}, u32[]{:S(2)}) %collective-permute-start.14) | collective-permute-done | bytes 92192 | tf_op jit(solution)/shard_map/ppermute | solution.py:122
  46.0 4.8 %smooth.1 = (bf16[40,1152]{1,0:T(8,128)(2,1)}, bf16[40,1152]{1,0:T(8,128)(2,1)}, bf16[40,1152]{1,0:T(8,128)(2,1)}, bf16[40,1152]{1,0:T(8,128)(2,1)}, bf16[40,115...) custom-call(bf16[40,1152]{1,0:T(8,128)(2,1)} %get-tuple-element.22.refs_0_, ...), custom_call_target="tpu_custom_call" | custom-call | tf_op jit(solution)/shard_map/smooth/pallas_call | solution.py:136
  51.7 1.8 %collective-permute-start.32 = (bf16[40,1152]{1,0:T(8,128)(2,1)}, bf16[40,1152]{1,0:T(8,128)(2,1)S(1)}, u32[]{:S(2)}, u32[]{:S(2)}) collective-permute-start(bf16[40,1152]{1,0:T(8,128)(2,1)} %get-tuple-element.32), channel_id=1, source_target_pairs={{0,8},{4,12},{8,0},{12,4},{16,24},{20,28},{24,16},{28,20},{1,9},{5... | collective-permute-start | bytes 276488 | tf_op jit(solution)/shard_map/ppermute | solution.py:122
  54.4 2.9 %collective-permute-start.34 = (bf16[40,1152]{1,0:T(8,128)(2,1)}, bf16[40,1152]{1,0:T(8,128)(2,1)S(1)}, u32[]{:S(2)}, u32[]{:S(2)}) collective-permute-start(bf16[40,1152]{1,0:T(8,128)(2,1)} %get-tuple-element.34), channel_id=1, source_target_pairs={{0,16},{4,20},{8,24},{12,28},{16,0},{20,4},{24,8},{28,12},{1,17},{... | collective-permute-start | bytes 276488 | tf_op jit(solution)/shard_map/ppermute | solution.py:122
  57.6 2.5 %collective-permute-start.36 = (bf16[40,1152]{1,0:T(8,128)(2,1)}, bf16[40,1152]{1,0:T(8,128)(2,1)S(1)}, u32[]{:S(2)}, u32[]{:S(2)}) collective-permute-start(bf16[40,1152]{1,0:T(8,128)(2,1)} %get-tuple-element.36), channel_id=1, source_target_pairs={{0,24},{4,28},{8,16},{12,20},{16,8},{20,12},{24,0},{28,4},{1,25},{... | collective-permute-start | bytes 276488 | tf_op jit(solution)/shard_map/ppermute | solution.py:122
  60.1 1.9 %collective-permute-start.37 = (bf16[40,1152]{1,0:T(8,128)(2,1)}, bf16[40,1152]{1,0:T(8,128)(2,1)S(1)}, u32[]{:S(2)}, u32[]{:S(2)}) collective-permute-start(bf16[40,1152]{1,0:T(8,128)(2,1)} %get-tuple-element.37), channel_id=1, source_target_pairs={{0,28},{4,24},{8,20},{12,16},{16,12},{20,8},{24,4},{28,0},{1,29},{... | collective-permute-start | bytes 276488 | tf_op jit(solution)/shard_map/ppermute | solution.py:122
  62.0 9.3 %collective-permute-done.35.refs_5_ = bf16[40,1152]{1,0:T(8,128)(2,1)S(1)} collective-permute-done((bf16[40,1152]{1,0:T(8,128)(2,1)}, bf16[40,1152]{1,0:T(8,128)(2,1)S(1)}, u32[]{:S(2)}, u32[]{:S(2)}) %collective-permute-start.35) | collective-permute-done | bytes 92192 | tf_op jit(solution)/shard_map/ppermute | solution.py:122
  72.1 2.5 %unpack.1 = (bf16[256,1024]{1,0:T(8,128)(2,1)}, bf16[1,256]{1,0:T(2,128)(2,1)}) custom-call(bf16[320,256]{1,0:T(8,128)(2,1)} %get-tuple-element.21.select_ref, bf16[40,1152]{1,0:T(8,128)(2,1)} %get-tuple-element.30.refs_0_, bf16[40,1152]{1,0:T(8,128)(2,1)} %copy-done, bf16[40,1152]{1,0:T(8,128)(2,1)} %copy-done.1, bf16[40,1152]{1,0:T(8,128)(2,1)} %copy-done.2, ...), custom_call_target="tpu_custom_call" | custom-call | tf_op jit(solution)/shard_map/unpack/pallas_call | solution.py:145
  (134 shorter events, 10.5 us)
Async XLA Ops:
  3.8 8.8 %collective-permute-start = (bf16[40,1152]{1,0:T(8,128)(2,1)}, bf16[40,1152]{1,0:T(8,128)(2,1)S(1)}, u32[]{:S(2)}, u32[]{:S(2)}) collective-permute-start(bf16[40,1152]{1,0:T(8,128)(2,1)} %get-tuple-element.23), channel_id=1, source_target_pairs={{0,4},{4,0},{8,12},{12,8},{16,20},{20,16},{24,28},{28,24},{1,5},{5... | collective-permute-start | bytes 276488 | tf_op jit(solution)/shard_map/ppermute | solution.py:122
  6.7 9.5 %collective-permute-start.1 = (bf16[40,1152]{1,0:T(8,128)(2,1)}, bf16[40,1152]{1,0:T(8,128)(2,1)S(1)}, u32[]{:S(2)}, u32[]{:S(2)}) collective-permute-start(bf16[40,1152]{1,0:T(8,128)(2,1)} %get-tuple-element.24), channel_id=1, source_target_pairs={{0,8},{4,12},{8,0},{12,4},{16,24},{20,28},{24,16},{28,20},{1,9},{5... | collective-permute-start | bytes 276488 | tf_op jit(solution)/shard_map/ppermute | solution.py:122
  8.3 7.9 %collective-permute-start.2 = (bf16[40,1152]{1,0:T(8,128)(2,1)}, bf16[40,1152]{1,0:T(8,128)(2,1)S(1)}, u32[]{:S(2)}, u32[]{:S(2)}) collective-permute-start(bf16[40,1152]{1,0:T(8,128)(2,1)} %get-tuple-element.25), channel_id=1, source_target_pairs={{0,12},{4,8},{8,4},{12,0},{16,28},{20,24},{24,20},{28,16},{1,13},{... | collective-permute-start | bytes 276488 | tf_op jit(solution)/shard_map/ppermute | solution.py:122
  8.3 8.0 %collective-permute-start.3 = (bf16[40,1152]{1,0:T(8,128)(2,1)}, bf16[40,1152]{1,0:T(8,128)(2,1)S(1)}, u32[]{:S(2)}, u32[]{:S(2)}) collective-permute-start(bf16[40,1152]{1,0:T(8,128)(2,1)} %get-tuple-element.26), channel_id=1, source_target_pairs={{0,16},{4,20},{8,24},{12,28},{16,0},{20,4},{24,8},{28,12},{1,17},{... | collective-permute-start | bytes 276488 | tf_op jit(solution)/shard_map/ppermute | solution.py:122
  11.3 14.7 %collective-permute-start.4 = (bf16[40,1152]{1,0:T(8,128)(2,1)}, bf16[40,1152]{1,0:T(8,128)(2,1)S(1)}, u32[]{:S(2)}, u32[]{:S(2)}) collective-permute-start(bf16[40,1152]{1,0:T(8,128)(2,1)} %get-tuple-element.27), channel_id=1, source_target_pairs={{0,20},{4,16},{8,28},{12,24},{16,4},{20,0},{24,12},{28,8},{1,21},{... | collective-permute-start | bytes 276488 | tf_op jit(solution)/shard_map/ppermute | solution.py:122
  12.6 13.4 %collective-permute-start.5 = (bf16[40,1152]{1,0:T(8,128)(2,1)}, bf16[40,1152]{1,0:T(8,128)(2,1)S(1)}, u32[]{:S(2)}, u32[]{:S(2)}) collective-permute-start(bf16[40,1152]{1,0:T(8,128)(2,1)} %get-tuple-element.28), channel_id=1, source_target_pairs={{0,24},{4,28},{8,16},{12,20},{16,8},{20,12},{24,0},{28,4},{1,25},{... | collective-permute-start | bytes 276488 | tf_op jit(solution)/shard_map/ppermute | solution.py:122
  16.2 11.3 %collective-permute-start.6 = (bf16[40,1152]{1,0:T(8,128)(2,1)}, bf16[40,1152]{1,0:T(8,128)(2,1)S(1)}, u32[]{:S(2)}, u32[]{:S(2)}) collective-permute-start(bf16[40,1152]{1,0:T(8,128)(2,1)} %get-tuple-element.29), channel_id=1, source_target_pairs={{0,28},{4,24},{8,20},{12,16},{16,12},{20,8},{24,4},{28,0},{1,29},{... | collective-permute-start | bytes 276488 | tf_op jit(solution)/shard_map/ppermute | solution.py:122
  16.2 11.5 %collective-permute-start.15 = (bf16[40,1152]{1,0:T(8,128)(2,1)}, bf16[40,1152]{1,0:T(8,128)(2,1)S(1)}, u32[]{:S(2)}, u32[]{:S(2)}) collective-permute-start(bf16[40,1152]{1,0:T(8,128)(2,1)} %get-tuple-element.22.refs_0_), channel_id=1, source_target_pairs={{0,1},{1,0},{2,3},{3,2},{4,5},{5,4},{6,7},{7,6},{8,9},{9,8},{10,11... | collective-permute-start | bytes 276488 | tf_op jit(solution)/shard_map/ppermute | solution.py:122
  16.3 11.9 %collective-permute-start.7 = (bf16[40,1152]{1,0:T(8,128)(2,1)}, bf16[40,1152]{1,0:T(8,128)(2,1)S(1)}, u32[]{:S(2)}, u32[]{:S(2)}) collective-permute-start(bf16[40,1152]{1,0:T(8,128)(2,1)} %get-tuple-element.22.refs_0_), channel_id=1, source_target_pairs={{0,2},{1,3},{2,0},{3,1},{4,6},{5,7},{6,4},{7,5},{8,10},{9,11},{10,... | collective-permute-start | bytes 276488 | tf_op jit(solution)/shard_map/ppermute | solution.py:122
  26.0 5.5 %collective-permute-start.8 = (bf16[40,1152]{1,0:T(8,128)(2,1)S(1)}, bf16[40,1152]{1,0:T(8,128)(2,1)S(1)}, u32[]{:S(2)}, u32[]{:S(2)}) collective-permute-start(bf16[40,1152]{1,0:T(8,128)(2,1)S(1)} %collective-permute-done.refs_1_), channel_id=1, source_target_pairs={{0,2},{1,3},{2,0},{3,1},{4,6},{5,7},{6,4},{7,5},{8,10},{9,11},{10,... | collective-permute-start | bytes 276488 | tf_op jit(solution)/shard_map/ppermute | solution.py:122
  27.7 5.7 %collective-permute-start.9 = (bf16[40,1152]{1,0:T(8,128)(2,1)S(1)}, bf16[40,1152]{1,0:T(8,128)(2,1)S(1)}, u32[]{:S(2)}, u32[]{:S(2)}) collective-permute-start(bf16[40,1152]{1,0:T(8,128)(2,1)S(1)} %collective-permute-done.1.refs_2_), channel_id=1, source_target_pairs={{0,2},{1,3},{2,0},{3,1},{4,6},{5,7},{6,4},{7,5},{8,10},{9,11},{10,... | collective-permute-start | bytes 276488 | tf_op jit(solution)/shard_map/ppermute | solution.py:122
  28.3 5.2 %collective-permute-start.18 = (bf16[40,1152]{1,0:T(8,128)(2,1)S(1)}, bf16[40,1152]{1,0:T(8,128)(2,1)S(1)}, u32[]{:S(2)}, u32[]{:S(2)}) collective-permute-start(bf16[40,1152]{1,0:T(8,128)(2,1)S(1)} %collective-permute-done.2.refs_3_), channel_id=1, source_target_pairs={{0,1},{1,0},{2,3},{3,2},{4,5},{5,4},{6,7},{7,6},{8,9},{9,8},{10,11... | collective-permute-start | bytes 276488 | tf_op jit(solution)/shard_map/ppermute | solution.py:122
  28.3 7.1 %collective-permute-start.10 = (bf16[40,1152]{1,0:T(8,128)(2,1)S(1)}, bf16[40,1152]{1,0:T(8,128)(2,1)S(1)}, u32[]{:S(2)}, u32[]{:S(2)}) collective-permute-start(bf16[40,1152]{1,0:T(8,128)(2,1)S(1)} %collective-permute-done.2.refs_3_), channel_id=1, source_target_pairs={{0,2},{1,3},{2,0},{3,1},{4,6},{5,7},{6,4},{7,5},{8,10},{9,11},{10,... | collective-permute-start | bytes 276488 | tf_op jit(solution)/shard_map/ppermute | solution.py:122
  31.5 5.9 %collective-permute-start.11 = (bf16[40,1152]{1,0:T(8,128)(2,1)S(1)}, bf16[40,1152]{1,0:T(8,128)(2,1)S(1)}, u32[]{:S(2)}, u32[]{:S(2)}) collective-permute-start(bf16[40,1152]{1,0:T(8,128)(2,1)S(1)} %collective-permute-done.3.refs_4_), channel_id=1, source_target_pairs={{0,2},{1,3},{2,0},{3,1},{4,6},{5,7},{6,4},{7,5},{8,10},{9,11},{10,... | collective-permute-start | bytes 276488 | tf_op jit(solution)/shard_map/ppermute | solution.py:122
  33.5 5.9 %collective-permute-start.12 = (bf16[40,1152]{1,0:T(8,128)(2,1)S(1)}, bf16[40,1152]{1,0:T(8,128)(2,1)S(1)}, u32[]{:S(2)}, u32[]{:S(2)}) collective-permute-start(bf16[40,1152]{1,0:T(8,128)(2,1)S(1)} %collective-permute-done.4.refs_5_), channel_id=1, source_target_pairs={{0,2},{1,3},{2,0},{3,1},{4,6},{5,7},{6,4},{7,5},{8,10},{9,11},{10,... | collective-permute-start | bytes 276488 | tf_op jit(solution)/shard_map/ppermute | solution.py:122
  35.4 5.9 %collective-permute-start.13 = (bf16[40,1152]{1,0:T(8,128)(2,1)S(1)}, bf16[40,1152]{1,0:T(8,128)(2,1)S(1)}, u32[]{:S(2)}, u32[]{:S(2)}) collective-permute-start(bf16[40,1152]{1,0:T(8,128)(2,1)S(1)} %collective-permute-done.5.refs_6_), channel_id=1, source_target_pairs={{0,2},{1,3},{2,0},{3,1},{4,6},{5,7},{6,4},{7,5},{8,10},{9,11},{10,... | collective-permute-start | bytes 276488 | tf_op jit(solution)/shard_map/ppermute | solution.py:122
  37.4 5.5 %collective-permute-start.14 = (bf16[40,1152]{1,0:T(8,128)(2,1)S(1)}, bf16[40,1152]{1,0:T(8,128)(2,1)S(1)}, u32[]{:S(2)}, u32[]{:S(2)}) collective-permute-start(bf16[40,1152]{1,0:T(8,128)(2,1)S(1)} %collective-permute-done.6.refs_7_), channel_id=1, source_target_pairs={{0,2},{1,3},{2,0},{3,1},{4,6},{5,7},{6,4},{7,5},{8,10},{9,11},{10,... | collective-permute-start | bytes 276488 | tf_op jit(solution)/shard_map/ppermute | solution.py:122
  50.8 6.8 %collective-permute-start.31 = (bf16[40,1152]{1,0:T(8,128)(2,1)}, bf16[40,1152]{1,0:T(8,128)(2,1)S(1)}, u32[]{:S(2)}, u32[]{:S(2)}) collective-permute-start(bf16[40,1152]{1,0:T(8,128)(2,1)} %get-tuple-element.31), channel_id=1, source_target_pairs={{0,4},{4,0},{8,12},{12,8},{16,20},{20,16},{24,28},{28,24},{1,5},{5... | collective-permute-start | bytes 276488 | tf_op jit(solution)/shard_map/ppermute | solution.py:122
  51.7 8.4 %collective-permute-start.32 = (bf16[40,1152]{1,0:T(8,128)(2,1)}, bf16[40,1152]{1,0:T(8,128)(2,1)S(1)}, u32[]{:S(2)}, u32[]{:S(2)}) collective-permute-start(bf16[40,1152]{1,0:T(8,128)(2,1)} %get-tuple-element.32), channel_id=1, source_target_pairs={{0,8},{4,12},{8,0},{12,4},{16,24},{20,28},{24,16},{28,20},{1,9},{5... | collective-permute-start | bytes 276488 | tf_op jit(solution)/shard_map/ppermute | solution.py:122
  53.5 8.5 %collective-permute-start.33 = (bf16[40,1152]{1,0:T(8,128)(2,1)}, bf16[40,1152]{1,0:T(8,128)(2,1)S(1)}, u32[]{:S(2)}, u32[]{:S(2)}) collective-permute-start(bf16[40,1152]{1,0:T(8,128)(2,1)} %get-tuple-element.33), channel_id=1, source_target_pairs={{0,12},{4,8},{8,4},{12,0},{16,28},{20,24},{24,20},{28,16},{1,13},{... | collective-permute-start | bytes 276488 | tf_op jit(solution)/shard_map/ppermute | solution.py:122
  54.4 7.7 %collective-permute-start.34 = (bf16[40,1152]{1,0:T(8,128)(2,1)}, bf16[40,1152]{1,0:T(8,128)(2,1)S(1)}, u32[]{:S(2)}, u32[]{:S(2)}) collective-permute-start(bf16[40,1152]{1,0:T(8,128)(2,1)} %get-tuple-element.34), channel_id=1, source_target_pairs={{0,16},{4,20},{8,24},{12,28},{16,0},{20,4},{24,8},{28,12},{1,17},{... | collective-permute-start | bytes 276488 | tf_op jit(solution)/shard_map/ppermute | solution.py:122
  57.3 14.1 %collective-permute-start.35 = (bf16[40,1152]{1,0:T(8,128)(2,1)}, bf16[40,1152]{1,0:T(8,128)(2,1)S(1)}, u32[]{:S(2)}, u32[]{:S(2)}) collective-permute-start(bf16[40,1152]{1,0:T(8,128)(2,1)} %get-tuple-element.35), channel_id=1, source_target_pairs={{0,20},{4,16},{8,28},{12,24},{16,4},{20,0},{24,12},{28,8},{1,21},{... | collective-permute-start | bytes 276488 | tf_op jit(solution)/shard_map/ppermute | solution.py:122
  57.6 13.8 %collective-permute-start.36 = (bf16[40,1152]{1,0:T(8,128)(2,1)}, bf16[40,1152]{1,0:T(8,128)(2,1)S(1)}, u32[]{:S(2)}, u32[]{:S(2)}) collective-permute-start(bf16[40,1152]{1,0:T(8,128)(2,1)} %get-tuple-element.36), channel_id=1, source_target_pairs={{0,24},{4,28},{8,16},{12,20},{16,8},{20,12},{24,0},{28,4},{1,25},{... | collective-permute-start | bytes 276488 | tf_op jit(solution)/shard_map/ppermute | solution.py:122
  60.1 11.3 %collective-permute-start.37 = (bf16[40,1152]{1,0:T(8,128)(2,1)}, bf16[40,1152]{1,0:T(8,128)(2,1)S(1)}, u32[]{:S(2)}, u32[]{:S(2)}) collective-permute-start(bf16[40,1152]{1,0:T(8,128)(2,1)} %get-tuple-element.37), channel_id=1, source_target_pairs={{0,28},{4,24},{8,20},{12,16},{16,12},{20,8},{24,4},{28,0},{1,29},{... | collective-permute-start | bytes 276488 | tf_op jit(solution)/shard_map/ppermute | solution.py:122
  (53 other events, 425.5 us)

commit v2 on v1

v2 whole, which is shorter than its diff:
```python
import functools

import jax
import jax.numpy as jnp
from jax import lax
from jax.experimental import pallas as pl
from jax.experimental.pallas import tpu as pltpu
from jax.sharding import PartitionSpec as P

CAP = 40
LANES = 128
VMEM = pl.BlockSpec(memory_space=pltpu.VMEM)
ROOM = pltpu.CompilerParams(vmem_limit_bytes=24 * 2**20)


def as_column(row):
    n = row.shape[1]
    same = lax.broadcasted_iota(jnp.int32, (n, n), 0) == lax.broadcasted_iota(jnp.int32, (n, n), 1)
    return jnp.sum(jnp.where(same, jnp.broadcast_to(row, (n, n)), 0.0), axis=1, keepdims=True)


def slot_mask(slots):
    row = lax.broadcasted_iota(jnp.int32, (slots, LANES), 0)
    return lax.rem(row, CAP) == lax.broadcasted_iota(jnp.int32, (slots, LANES), 1)


def spread(rows_of_pieces, pieces):
    slots = pieces * CAP
    owner = lax.div(lax.broadcasted_iota(jnp.int32, (slots, pieces), 0), CAP)
    pick = jnp.where(owner == lax.broadcasted_iota(jnp.int32, (slots, pieces), 1), 1.0, 0.0)
    wide = jnp.dot(
        pick.astype(jnp.bfloat16), rows_of_pieces.astype(jnp.bfloat16), preferred_element_type=jnp.float32
    )
    return jnp.where(slot_mask(slots), wide, 0.0)


def gather_lanes(column, pieces):
    wide = jnp.where(slot_mask(pieces * CAP), column, 0.0)
    return [jnp.sum(wide[p * CAP : (p + 1) * CAP], axis=0, keepdims=True) for p in range(pieces)]


def pack_kernel(groups, codes_ref, scales_ref, cluster_ref, select_ref, *out_refs):
    rows, width = codes_ref.shape
    nblk = scales_ref.shape[0]
    step = width // nblk
    scales = scales_ref[...].T
    parts = []
    total = None
    for b in range(nblk):
        x = codes_ref[:, b * step : (b + 1) * step].astype(jnp.float32) * scales[:, b : b + 1]
        parts.append(x)
        square = x * x
        total = square if total is None else total + square
    inv = lax.rsqrt(jnp.sum(total, axis=1, keepdims=True) / width + 1e-06)
    cluster = cluster_ref[...]
    owner = lax.rem(cluster, groups)
    step_row = lax.bitwise_xor(owner, lax.axis_index("grp"))
    step_f = step_row.astype(jnp.float32)
    step_col = as_column(step_f)
    before = lax.broadcasted_iota(jnp.int32, (rows, rows), 0) < lax.broadcasted_iota(
        jnp.int32, (rows, rows), 1
    )
    rank = jnp.sum(
        jnp.where(before & (step_col == step_f), 1.0, 0.0), axis=0, keepdims=True
    ).astype(jnp.int32)
    target = step_row * CAP + rank
    slots = groups * CAP
    hit = lax.broadcasted_iota(jnp.int32, (slots, rows), 0) == target
    select = jnp.where(hit, 1.0, 0.0).astype(jnp.bfloat16)
    select_ref[...] = select
    tags = jnp.sum(jnp.where(hit, cluster.astype(jnp.float32) + 1.0, 0.0), axis=1, keepdims=True)
    for s, tag_row in enumerate(gather_lanes(tags, groups)):
        out_refs[s][nblk * CAP :, :] = jnp.broadcast_to(tag_row - 1.0, (8, LANES)).astype(jnp.bfloat16)
    for b in range(nblk):
        e = (parts[b] * inv).astype(jnp.bfloat16)
        packed = jnp.dot(select, e, preferred_element_type=jnp.float32).astype(jnp.bfloat16)
        for s in range(groups):
            out_refs[s][b * CAP : (b + 1) * CAP, :] = packed[s * CAP : (s + 1) * CAP]


def smooth_kernel(groups, places, nblk, *refs):
    inputs, pieces = len(places), groups * lax.axis_size("mem")
    in_refs, out_refs = refs[:inputs], refs[inputs : inputs + groups]
    keys_ref, tags_ref = refs[inputs + groups :]
    size = nblk * CAP + 8
    width = nblk * LANES
    for ref, blocks in zip(in_refs, places):
        for k, p in enumerate(blocks):
            if p is None:
                continue
            at = k * size
            for b in range(nblk):
                keys_ref[b, p * CAP : (p + 1) * CAP, :] = ref[at + b * CAP : at + (b + 1) * CAP, :]
            tags_ref[p : p + 1, :] = ref[at + nblk * CAP : at + nblk * CAP + 1, :].astype(jnp.float32)
    slots, count = groups * CAP, pieces * CAP
    keys = jnp.concatenate([keys_ref[b] for b in range(nblk)], axis=1)
    queries = keys[:slots]
    tags = spread(tags_ref[...], pieces)
    ktags = lax.dot_general(
        jnp.ones((8, LANES), jnp.bfloat16),
        tags.astype(jnp.bfloat16),
        (((1,), (1,)), ((), ())),
        preferred_element_type=jnp.float32,
    )[:1]
    qtags = jnp.sum(tags[:slots], axis=1, keepdims=True)
    sims = (
        lax.dot_general(
            queries, keys, (((1,), (1,)), ((), ())), preferred_element_type=jnp.float32
        )
        / width
    )
    keep = (
        (qtags == ktags)
        & (qtags >= 0.0)
        & (
            lax.broadcasted_iota(jnp.int32, (slots, count), 0)
            != lax.broadcasted_iota(jnp.int32, (slots, count), 1)
        )
    )
    weights = jnp.where(keep, jnp.exp(8.0 * (sims - 1.0)), 0.0)
    den = 1.0 + jnp.sum(weights, axis=1, keepdims=True)
    num = jnp.dot(weights.astype(jnp.bfloat16), keys, preferred_element_type=jnp.float32)
    result = ((queries.astype(jnp.float32) + num) / den).astype(jnp.bfloat16)
    for s, mass_row in enumerate(gather_lanes(jnp.log(den), groups)):
        for b in range(nblk):
            out_refs[s][b * CAP : (b + 1) * CAP, :] = result[
                s * CAP : (s + 1) * CAP, b * LANES : (b + 1) * LANES
            ]
        out_refs[s][nblk * CAP :, :] = jnp.broadcast_to(mass_row, (8, LANES)).astype(jnp.bfloat16)


def unpack_kernel(steps, nblk, select_ref, *refs):
    groups = len(steps)
    in_refs, (smoothed_ref, mass_ref, back_ref, masses_ref) = refs[:groups], refs[groups:]
    for s, ref in zip(steps, in_refs):
        for b in range(nblk):
            back_ref[b, s * CAP : (s + 1) * CAP, :] = ref[b * CAP : (b + 1) * CAP, :]
        masses_ref[s : s + 1, :] = ref[nblk * CAP : nblk * CAP + 1, :].astype(jnp.float32)
    select = select_ref[...]
    over_slots = (((0,), (0,)), ((), ()))
    back = jnp.concatenate([back_ref[b] for b in range(nblk)], axis=1)
    smoothed_ref[...] = lax.dot_general(
        select, back, over_slots, preferred_element_type=jnp.float32
    ).astype(jnp.bfloat16)
    masses = spread(masses_ref[...], groups).astype(jnp.bfloat16)
    mass = lax.dot_general(masses, select, over_slots, preferred_element_type=jnp.float32)
    mass_ref[...] = jnp.sum(mass, axis=0, keepdims=True).astype(jnp.bfloat16)


def gate(value, *after):
    if not after:
        return value
    return lax.optimization_barrier((value, *after))[0]


def on_chip(values):
    return [pltpu.with_memory_space_constraint(v, pltpu.VMEM) for v in values]


def local(codes, scales, cluster_id):
    rows, width = codes.shape
    nblk = scales.shape[1]
    groups, members = lax.axis_size("grp"), lax.axis_size("mem")
    slots = groups * CAP
    size = nblk * CAP + 8
    piece = pltpu.VMEM((size, LANES), jnp.bfloat16)
    half, sides = groups // 2, members // 2
    near, far = list(range(1, half)), list(range(half, groups))

    def swap(value, axis, step):
        count = lax.axis_size(axis)
        return lax.ppermute(value, axis, [(i, i ^ step) for i in range(count)])

    def join(values):
        return jnp.concatenate(values) if len(values) > 1 else values[0]

    select, *outbox = pl.pallas_call(
        functools.partial(pack_kernel, groups),
        out_shape=[pltpu.VMEM((slots, rows), jnp.bfloat16)] + [piece] * groups,
        in_specs=[VMEM] * 3,
        out_specs=[VMEM] * (1 + groups),
        compiler_params=ROOM,
        name="pack",
    )(codes, scales.T, cluster_id.reshape(1, rows))

    held = []

    def hold(value, where):
        held.append((value, where))
        return held[-1]

    def across(parts, *after):
        joined = gate(join([v for v, _ in parts]), *after)
        where = [w for _, ws in parts for w in ws]
        return [
            (swap(joined, "mem", step), [(s, step // 2) for s, _ in where]) for step in range(2, members, 2)
        ], joined

    def partner(parts, *after):
        joined = gate(join([v for v, _ in parts]), *after)
        return (swap(joined, "mem", 1), [(s, i + sides) for _, ws in parts for s, i in ws])

    def grp(s, *after):
        return (swap(gate(outbox[s], *after), "grp", s), [(s, 0)])

    early, late = far[: half // 2], far[half // 2 :]
    got = {0: (outbox[0], [(0, 0)])}
    for s in early[:1] + near + early[1:]:
        got[s] = grp(s)
    ready = [got[s] for s in [0] + near]
    first, joined = across(ready)
    for s in late:
        got[s] = grp(s, joined)
    second, _ = across([got[s] for s in early])
    third, last = across([got[s] for s in late])
    held = [got[s] for s in early[:1] + near + early[1:] + late] + first + second + third + [got[0]]
    held += [partner(ready + [got[s] for s in early]), partner(first)]
    held += [partner([got[s] for s in late] + second)]
    held += [partner([h]) for h in third]

    steps = [s for pair in zip(far, near + [0]) for s in pair]
    places = [[i * groups + steps.index(s) for s, i in where] for _, where in held]
    pieces = groups * members
    results = pl.pallas_call(
        functools.partial(smooth_kernel, groups, places, nblk),
        out_shape=[piece] * groups,
        in_specs=[VMEM] * len(held),
        out_specs=[VMEM] * groups,
        scratch_shapes=[
            pltpu.VMEM((nblk, pieces * CAP, LANES), jnp.bfloat16),
            pltpu.VMEM((pieces, LANES), jnp.float32),
        ],
        compiler_params=ROOM,
        name="smooth",
    )(*on_chip([v for v, _ in held]))
    result = dict(zip(steps, results))
    back = {s: swap(result[s], "grp", s) if s else result[s] for s in steps}
    done = steps
    smoothed, mass = pl.pallas_call(
        functools.partial(unpack_kernel, done, nblk),
        out_shape=[
            jax.ShapeDtypeStruct((rows, width), jnp.bfloat16),
            jax.ShapeDtypeStruct((1, rows), jnp.bfloat16),
        ],
        in_specs=[VMEM] * (1 + groups),
        out_specs=[VMEM] * 2,
        scratch_shapes=[
            pltpu.VMEM((nblk, slots, LANES), jnp.bfloat16),
            pltpu.VMEM((groups, LANES), jnp.float32),
        ],
        compiler_params=ROOM,
        name="unpack",
    )(*on_chip([select] + [back[s] for s in done]))
    return (smoothed, mass.reshape(rows))


def solution(mesh):
    placed = (P(("grp", "mem"), None), P(("grp", "mem"), None), P(("grp", "mem")))
    return jax.shard_map(
        local,
        mesh=mesh,
        in_specs=placed,
        out_specs=(P(("grp", "mem"), None), P(("grp", "mem"))),
        check_vma=False,
    )
```

time: 76.6 us -> 57.5 us (0.75)
  starting transfers between devices: 37.3 us -> 25.9 us
  Pallas kernels: 10.5 us -> 4.92 us
  waiting for transfers between devices: 24.1 us -> 22.5 us
    ppermute x38 -> x21, starting transfers between devices: 37.3 us -> 25.9 us  [swap(): return lax.ppermute(value, axis, [(i, i ^ step) for i in range(count)])]
    pallas_call x3, Pallas kernels: 10.5 us -> 4.92 us  [the longest x1 2.33 us: local(): pl.pallas_call(functools.partial(smooth_kernel, groups, places, nblk), ou...]
    ppermute x38 -> x21, waiting for transfers between devices: 24.1 us -> 22.5 us  [swap(): return lax.ppermute(value, axis, [(i, i ^ step) for i in range(count)])]
    unnamed x78 -> x11, local copies, waits for them, and re-layouts: 2.28 us -> 2.52 us
  transfers between devices with their start and end apart: 38 -> 21, of which waited for: 13 -> 10; matrix products, arithmetic and copies ran while one was open for 0% -> 0% of each run, Pallas kernels for 0% -> 0%
where the time goes in v2:
time: 57.5 us; the launch traced here: 57.2 us
  starting transfers between devices  25.9 us (45%)
  waiting for transfers between devices  22.5 us (39%)
  Pallas kernels  4.92 us (9%)
  local copies, waits for them, and re-layouts  2.54 us (4%)
  between operations  0.76 us (1%)
  other arithmetic  0.58 us (1%)
    ppermute x21, starting transfers between devices, swap(): return lax.ppermute(value, axis, [(i, i ^ step) for i in range(count)])  25.9 us
    ppermute x21, waiting for transfers between devices, swap(): return lax.ppermute(value, axis, [(i, i ^ step) for i in range(count)])  22.5 us
    unnamed x11, local copies, waits for them, and re-layouts  2.52 us
    pallas_call x1, Pallas kernels, local(): pl.pallas_call(functools.partial(smooth_kernel, groups, places, nblk), ou...  2.33 us
    pallas_call x1, Pallas kernels, local(): pl.pallas_call(functools.partial(unpack_kernel, done, nblk), out_shape=[j...  1.32 us
    pallas_call x1, Pallas kernels, local(): pl.pallas_call(functools.partial(pack_kernel, groups), out_shape=[pltpu.V...  1.27 us
  transfers between devices with their start and end apart: 21, of which 10 were waited for; matrix products, arithmetic and copies ran while one was open for 0% of the time, Pallas kernels for 0%

profile of v2, /device:TPU:0, one launch (start us, length us, event | category | flops | bytes accessed | tf_op | source)
XLA Modules:
  0.0 57.2 jit_solution(6877121089849410586)
XLA Ops:
  1.3 1.0 %copy-done = bf16[256,1024]{1,0:T(8,128)(2,1)S(1)} copy-done((bf16[256,1024]{1,0:T(8,128)(2,1)S(1)}, bf16[256,1024]{1,0:T(8,128)(2,1)}, u32[]{:S(2)}) %copy-start) | copy-done | bytes 524312
  3.0 1.3 %pack.1 = (bf16[320,256]{1,0:T(8,128)(2,1)S(1)}, bf16[328,128]{1,0:T(8,128)(2,1)S(1)}, bf16[328,128]{1,0:T(8,128)(2,1)S(1)}, bf16[328,128]{1,0:T(8,128)(2,1)S(1)...) custom-call(bf16[256,1024]{1,0:T(8,128)(2,1)S(1)} %copy-done, ...), custom_call_target="tpu_custom_call" | custom-call | tf_op jit(solution)/shard_map/pack/pallas_call | solution.py:177
  4.3 4.1 %collective-permute-start = (bf16[328,128]{1,0:T(8,128)(2,1)S(1)}, bf16[328,128]{1,0:T(8,128)(2,1)S(1)}, u32[]{:S(2)}, u32[]{:S(2)}) collective-permute-start(bf16[328,128]{1,0:T(8,128)(2,1)S(1)} %get-tuple-element.24), channel_id=1, source_target_pairs={{0,16},{4,20},{8,24},{12,28},{16,0},{20,4},{24,8},{28,12},{1,17},{... | collective-permute-start | bytes 251912 | tf_op jit(solution)/shard_map/ppermute | solution.py:172
  8.4 1.5 %collective-permute-start.1 = (bf16[328,128]{1,0:T(8,128)(2,1)S(1)}, bf16[328,128]{1,0:T(8,128)(2,1)S(1)}, u32[]{:S(2)}, u32[]{:S(2)}) collective-permute-start(bf16[328,128]{1,0:T(8,128)(2,1)S(1)} %get-tuple-element.25), channel_id=1, source_target_pairs={{0,4},{4,0},{8,12},{12,8},{16,20},{20,16},{24,28},{28,24},{1,5},{5... | collective-permute-start | bytes 251912 | tf_op jit(solution)/shard_map/ppermute | solution.py:172
  9.9 1.6 %collective-permute-start.2 = (bf16[328,128]{1,0:T(8,128)(2,1)S(1)}, bf16[328,128]{1,0:T(8,128)(2,1)S(1)}, u32[]{:S(2)}, u32[]{:S(2)}) collective-permute-start(bf16[328,128]{1,0:T(8,128)(2,1)S(1)} %get-tuple-element.26), channel_id=1, source_target_pairs={{0,8},{4,12},{8,0},{12,4},{16,24},{20,28},{24,16},{28,20},{1,9},{5... | collective-permute-start | bytes 251912 | tf_op jit(solution)/shard_map/ppermute | solution.py:172
  11.9 1.3 %collective-permute-start.4 = (bf16[328,128]{1,0:T(8,128)(2,1)S(1)}, bf16[328,128]{1,0:T(8,128)(2,1)S(1)}, u32[]{:S(2)}, u32[]{:S(2)}) collective-permute-start(bf16[328,128]{1,0:T(8,128)(2,1)S(1)} %get-tuple-element.28), channel_id=1, source_target_pairs={{0,20},{4,16},{8,28},{12,24},{16,4},{20,0},{24,12},{28,8},{1,21},{... | collective-permute-start | bytes 251912 | tf_op jit(solution)/shard_map/ppermute | solution.py:172
  13.2 6.1 %collective-permute-done.4.refs_4_ = bf16[328,128]{1,0:T(8,128)(2,1)S(1)} collective-permute-done((bf16[328,128]{1,0:T(8,128)(2,1)S(1)}, bf16[328,128]{1,0:T(8,128)(2,1)S(1)}, u32[]{:S(2)}, u32[]{:S(2)}) %collective-permute-start.4) | collective-permute-done | bytes 84000 | tf_op jit(solution)/shard_map/ppermute | solution.py:172
  19.4 1.6 %collective-permute-start.8 = (bf16[656,128]{1,0:T(8,128)(2,1)S(1)}, bf16[656,128]{1,0:T(8,128)(2,1)S(1)}, u32[]{:S(2)}, u32[]{:S(2)}) collective-permute-start(bf16[656,128]{1,0:T(8,128)(2,1)S(1)} %pad_maximum_fusion.1), channel_id=1, source_target_pairs={{0,2},{1,3},{2,0},{3,1},{4,6},{5,7},{6,4},{7,5},{8,10},{9,11},{10,... | collective-permute-start | bytes 503816 | tf_op jit(solution)/shard_map/ppermute | solution.py:172
  22.4 2.8 %collective-permute-start.6 = (bf16[328,128]{1,0:T(8,128)(2,1)S(1)}, bf16[328,128]{1,0:T(8,128)(2,1)S(1)}, u32[]{:S(2)}, u32[]{:S(2)}) collective-permute-start(bf16[328,128]{1,0:T(8,128)(2,1)S(1)} %get-tuple-element.33), channel_id=1, source_target_pairs={{0,28},{4,24},{8,20},{12,16},{16,12},{20,8},{24,4},{28,0},{1,29},{... | collective-permute-start | bytes 251912 | tf_op jit(solution)/shard_map/ppermute | solution.py:172
  25.4 2.6 %collective-permute-done.5.refs_5_ = bf16[328,128]{1,0:T(8,128)(2,1)S(1)} collective-permute-done((bf16[328,128]{1,0:T(8,128)(2,1)S(1)}, bf16[328,128]{1,0:T(8,128)(2,1)S(1)}, u32[]{:S(2)}, u32[]{:S(2)}) %collective-permute-start.5) | collective-permute-done | bytes 84000 | tf_op jit(solution)/shard_map/ppermute | solution.py:172
  28.0 1.6 %collective-permute-done.6.refs_6_ = bf16[328,128]{1,0:T(8,128)(2,1)S(1)} collective-permute-done((bf16[328,128]{1,0:T(8,128)(2,1)S(1)}, bf16[328,128]{1,0:T(8,128)(2,1)S(1)}, u32[]{:S(2)}, u32[]{:S(2)}) %collective-permute-start.6) | collective-permute-done | bytes 84000 | tf_op jit(solution)/shard_map/ppermute | solution.py:172
  29.7 1.6 %collective-permute-start.9 = (bf16[656,128]{1,0:T(8,128)(2,1)S(1)}, bf16[656,128]{1,0:T(8,128)(2,1)S(1)}, u32[]{:S(2)}, u32[]{:S(2)}) collective-permute-start(bf16[656,128]{1,0:T(8,128)(2,1)S(1)} %pad_maximum_fusion.2), channel_id=1, source_target_pairs={{0,2},{1,3},{2,0},{3,1},{4,6},{5,7},{6,4},{7,5},{8,10},{9,11},{10,... | collective-permute-start | bytes 503816 | tf_op jit(solution)/shard_map/ppermute | solution.py:172
  31.9 3.2 %collective-permute-done.9.refs_9_ = bf16[656,128]{1,0:T(8,128)(2,1)S(1)} collective-permute-done((bf16[656,128]{1,0:T(8,128)(2,1)S(1)}, bf16[656,128]{1,0:T(8,128)(2,1)S(1)}, u32[]{:S(2)}, u32[]{:S(2)}) %collective-permute-start.9) | collective-permute-done | bytes 167968 | tf_op jit(solution)/shard_map/ppermute | solution.py:172
  35.1 1.4 %collective-permute-done.13.refs_14_ = bf16[656,128]{1,0:T(8,128)(2,1)S(1)} collective-permute-done((bf16[656,128]{1,0:T(8,128)(2,1)S(1)}, bf16[656,128]{1,0:T(8,128)(2,1)S(1)}, u32[]{:S(2)}, u32[]{:S(2)}) %collective-permute-start.13) | collective-permute-done | bytes 167968 | tf_op jit(solution)/shard_map/ppermute | solution.py:172
  36.5 2.3 %smooth.1 = (bf16[328,128]{1,0:T(8,128)(2,1)S(1)}, bf16[328,128]{1,0:T(8,128)(2,1)S(1)}, bf16[328,128]{1,0:T(8,128)(2,1)S(1)}, bf16[328,128]{1,0:T(8,128)(2,1)S(...) custom-call(bf16[328,128]{1,0:T(8,128)(2,1)S(1)} %collective-permute, ...), custom_call_target="tpu_custom_call" | custom-call | tf_op jit(solution)/shard_map/smooth/pallas_call | solution.py:224
  40.1 3.2 %collective-permute-start.16 = (bf16[328,128]{1,0:T(8,128)(2,1)S(1)}, bf16[328,128]{1,0:T(8,128)(2,1)S(1)}, u32[]{:S(2)}, u32[]{:S(2)}) collective-permute-start(bf16[328,128]{1,0:T(8,128)(2,1)S(1)} %get-tuple-element.36), channel_id=1, source_target_pairs={{0,20},{4,16},{8,28},{12,24},{16,4},{20,0},{24,12},{28,8},{1,21},{... | collective-permute-start | bytes 251912 | tf_op jit(solution)/shard_map/ppermute | solution.py:172
  44.0 2.3 %collective-permute-start.18 = (bf16[328,128]{1,0:T(8,128)(2,1)S(1)}, bf16[328,128]{1,0:T(8,128)(2,1)S(1)}, u32[]{:S(2)}, u32[]{:S(2)}) collective-permute-start(bf16[328,128]{1,0:T(8,128)(2,1)S(1)} %get-tuple-element.38), channel_id=1, source_target_pairs={{0,24},{4,28},{8,16},{12,20},{16,8},{20,12},{24,0},{28,4},{1,25},{... | collective-permute-start | bytes 251912 | tf_op jit(solution)/shard_map/ppermute | solution.py:172
  46.3 1.3 %collective-permute-done.14.refs_0_ = bf16[328,128]{1,0:T(8,128)(2,1)S(1)} collective-permute-done((bf16[328,128]{1,0:T(8,128)(2,1)S(1)}, bf16[328,128]{1,0:T(8,128)(2,1)S(1)}, u32[]{:S(2)}, u32[]{:S(2)}) %collective-permute-start.14) | collective-permute-done | bytes 84000 | tf_op jit(solution)/shard_map/ppermute | solution.py:172
  47.6 1.7 %collective-permute-start.20 = (bf16[328,128]{1,0:T(8,128)(2,1)S(1)}, bf16[328,128]{1,0:T(8,128)(2,1)S(1)}, u32[]{:S(2)}, u32[]{:S(2)}) collective-permute-start(bf16[328,128]{1,0:T(8,128)(2,1)S(1)} %get-tuple-element.40), channel_id=1, source_target_pairs={{0,28},{4,24},{8,20},{12,16},{16,12},{20,8},{24,4},{28,0},{1,29},{... | collective-permute-start | bytes 251912 | tf_op jit(solution)/shard_map/ppermute | solution.py:172
  49.2 1.7 %collective-permute-done.16.refs_2_ = bf16[328,128]{1,0:T(8,128)(2,1)S(1)} collective-permute-done((bf16[328,128]{1,0:T(8,128)(2,1)S(1)}, bf16[328,128]{1,0:T(8,128)(2,1)S(1)}, u32[]{:S(2)}, u32[]{:S(2)}) %collective-permute-start.16) | collective-permute-done | bytes 84000 | tf_op jit(solution)/shard_map/ppermute | solution.py:172
  51.0 2.4 %collective-permute-done.18.refs_4_ = bf16[328,128]{1,0:T(8,128)(2,1)S(1)} collective-permute-done((bf16[328,128]{1,0:T(8,128)(2,1)S(1)}, bf16[328,128]{1,0:T(8,128)(2,1)S(1)}, u32[]{:S(2)}, u32[]{:S(2)}) %collective-permute-start.18) | collective-permute-done | bytes 84000 | tf_op jit(solution)/shard_map/ppermute | solution.py:172
  53.4 1.1 %collective-permute-done.19.refs_5_ = bf16[328,128]{1,0:T(8,128)(2,1)S(1)} collective-permute-done((bf16[328,128]{1,0:T(8,128)(2,1)S(1)}, bf16[328,128]{1,0:T(8,128)(2,1)S(1)}, u32[]{:S(2)}, u32[]{:S(2)}) %collective-permute-start.19) | collective-permute-done | bytes 84000 | tf_op jit(solution)/shard_map/ppermute | solution.py:172
  54.5 0.9 %collective-permute-done.20.refs_6_ = bf16[328,128]{1,0:T(8,128)(2,1)S(1)} collective-permute-done((bf16[328,128]{1,0:T(8,128)(2,1)S(1)}, bf16[328,128]{1,0:T(8,128)(2,1)S(1)}, u32[]{:S(2)}, u32[]{:S(2)}) %collective-permute-start.20) | collective-permute-done | bytes 84000 | tf_op jit(solution)/shard_map/ppermute | solution.py:172
  55.4 1.3 %unpack.1 = (bf16[256,1024]{1,0:T(8,128)(2,1)}, bf16[1,256]{1,0:T(2,128)(2,1)S(1)}) custom-call(bf16[320,256]{1,0:T(8,128)(2,1)S(1)} %get-tuple-element.23.select_ref, bf16[328,128]{1,0:T(8,128)(2,1)S(1)} %collective-permute-done.14.refs_0_, bf16[328,128]{1,0:T(8,128)(2,1)S(1)} %collective-permute-done.15.refs_1_, ...), custom_call_target="tpu_custom_call" | custom-call | tf_op jit(solution)/shard_map/unpack/pallas_call | solution.py:239
  (37 shorter events, 6.4 us)
Async XLA Ops:
  0.6 0.7 %copy-start.2 = (s32[256]{0:T(256)S(1)}, s32[256]{0:T(256)}, u32[]{:S(2)}) copy-start(s32[256]{0:T(256)} %param.5) | copy-start | bytes 3076
  1.3 1.0 %copy-start = (bf16[256,1024]{1,0:T(8,128)(2,1)S(1)}, bf16[256,1024]{1,0:T(8,128)(2,1)}, u32[]{:S(2)}) copy-start(bf16[256,1024]{1,0:T(8,128)(2,1)} %codes_ref.1) | copy-start | bytes 1572868
  2.4 0.7 %copy-start.1 = (f32[256,8]{0,1:T(8,128)S(1)}, f32[256,8]{0,1:T(8,128)}, u32[]{:S(2)}) copy-start(f32[256,8]{0,1:T(8,128)} %param.4) | copy-start | bytes 24580
  4.3 8.9 %collective-permute-start = (bf16[328,128]{1,0:T(8,128)(2,1)S(1)}, bf16[328,128]{1,0:T(8,128)(2,1)S(1)}, u32[]{:S(2)}, u32[]{:S(2)}) collective-permute-start(bf16[328,128]{1,0:T(8,128)(2,1)S(1)} %get-tuple-element.24), channel_id=1, source_target_pairs={{0,16},{4,20},{8,24},{12,28},{16,0},{20,4},{24,8},{28,12},{1,17},{... | collective-permute-start | bytes 251912 | tf_op jit(solution)/shard_map/ppermute | solution.py:172
  8.4 12.5 %collective-permute-start.1 = (bf16[328,128]{1,0:T(8,128)(2,1)S(1)}, bf16[328,128]{1,0:T(8,128)(2,1)S(1)}, u32[]{:S(2)}, u32[]{:S(2)}) collective-permute-start(bf16[328,128]{1,0:T(8,128)(2,1)S(1)} %get-tuple-element.25), channel_id=1, source_target_pairs={{0,4},{4,0},{8,12},{12,8},{16,20},{20,16},{24,28},{28,24},{1,5},{5... | collective-permute-start | bytes 251912 | tf_op jit(solution)/shard_map/ppermute | solution.py:172
  9.9 11.0 %collective-permute-start.2 = (bf16[328,128]{1,0:T(8,128)(2,1)S(1)}, bf16[328,128]{1,0:T(8,128)(2,1)S(1)}, u32[]{:S(2)}, u32[]{:S(2)}) collective-permute-start(bf16[328,128]{1,0:T(8,128)(2,1)S(1)} %get-tuple-element.26), channel_id=1, source_target_pairs={{0,8},{4,12},{8,0},{12,4},{16,24},{20,28},{24,16},{28,20},{1,9},{5... | collective-permute-start | bytes 251912 | tf_op jit(solution)/shard_map/ppermute | solution.py:172
  11.5 9.5 %collective-permute-start.3 = (bf16[328,128]{1,0:T(8,128)(2,1)S(1)}, bf16[328,128]{1,0:T(8,128)(2,1)S(1)}, u32[]{:S(2)}, u32[]{:S(2)}) collective-permute-start(bf16[328,128]{1,0:T(8,128)(2,1)S(1)} %get-tuple-element.27), channel_id=1, source_target_pairs={{0,12},{4,8},{8,4},{12,0},{16,28},{20,24},{24,20},{28,16},{1,13},{... | collective-permute-start | bytes 251912 | tf_op jit(solution)/shard_map/ppermute | solution.py:172
  11.9 7.4 %collective-permute-start.4 = (bf16[328,128]{1,0:T(8,128)(2,1)S(1)}, bf16[328,128]{1,0:T(8,128)(2,1)S(1)}, u32[]{:S(2)}, u32[]{:S(2)}) collective-permute-start(bf16[328,128]{1,0:T(8,128)(2,1)S(1)} %get-tuple-element.28), channel_id=1, source_target_pairs={{0,20},{4,16},{8,28},{12,24},{16,4},{20,0},{24,12},{28,8},{1,21},{... | collective-permute-start | bytes 251912 | tf_op jit(solution)/shard_map/ppermute | solution.py:172
  19.4 11.9 %collective-permute-start.8 = (bf16[656,128]{1,0:T(8,128)(2,1)S(1)}, bf16[656,128]{1,0:T(8,128)(2,1)S(1)}, u32[]{:S(2)}, u32[]{:S(2)}) collective-permute-start(bf16[656,128]{1,0:T(8,128)(2,1)S(1)} %pad_maximum_fusion.1), channel_id=1, source_target_pairs={{0,2},{1,3},{2,0},{3,1},{4,6},{5,7},{6,4},{7,5},{8,10},{9,11},{10,... | collective-permute-start | bytes 503816 | tf_op jit(solution)/shard_map/ppermute | solution.py:172
  21.1 10.3 %collective-permute-start.7 = (bf16[1312,128]{1,0:T(8,128)(2,1)S(1)}, bf16[1312,128]{1,0:T(8,128)(2,1)S(1)}, u32[]{:S(2)}, u32[]{:S(2)}) collective-permute-start(bf16[1312,128]{1,0:T(8,128)(2,1)S(1)} %get-tuple-element.45), channel_id=1, source_target_pairs={{0,2},{1,3},{2,0},{3,1},{4,6},{5,7},{6,4},{7,5},{8,10},{9,11},{10,... | collective-permute-start | bytes 1007624 | tf_op jit(solution)/shard_map/ppermute | solution.py:172
  21.7 6.4 %collective-permute-start.5 = (bf16[328,128]{1,0:T(8,128)(2,1)S(1)}, bf16[328,128]{1,0:T(8,128)(2,1)S(1)}, u32[]{:S(2)}, u32[]{:S(2)}) collective-permute-start(bf16[328,128]{1,0:T(8,128)(2,1)S(1)} %get-tuple-element.31), channel_id=1, source_target_pairs={{0,24},{4,28},{8,16},{12,20},{16,8},{20,12},{24,0},{28,4},{1,25},{... | collective-permute-start | bytes 251912 | tf_op jit(solution)/shard_map/ppermute | solution.py:172
  22.4 7.3 %collective-permute-start.6 = (bf16[328,128]{1,0:T(8,128)(2,1)S(1)}, bf16[328,128]{1,0:T(8,128)(2,1)S(1)}, u32[]{:S(2)}, u32[]{:S(2)}) collective-permute-start(bf16[328,128]{1,0:T(8,128)(2,1)S(1)} %get-tuple-element.33), channel_id=1, source_target_pairs={{0,28},{4,24},{8,20},{12,16},{16,12},{20,8},{24,4},{28,0},{1,29},{... | collective-permute-start | bytes 251912 | tf_op jit(solution)/shard_map/ppermute | solution.py:172
  25.3 11.2 %collective-permute-start.10 = (bf16[1968,128]{1,0:T(8,128)(2,1)S(1)}, bf16[1968,128]{1,0:T(8,128)(2,1)S(1)}, u32[]{:S(2)}, u32[]{:S(2)}) collective-permute-start(bf16[1968,128]{1,0:T(8,128)(2,1)S(1)} %constant_dynamic-update-slice_fusion.4), channel_id=1, source_target_pairs={{0,1},{1,0},{2,3},{3,2},{4,5},{5,4},{6,7},{7,6},{8,9},{9,8},{10,11... | collective-permute-start | bytes 1511432 | tf_op jit(solution)/shard_map/ppermute | solution.py:172
  29.7 5.4 %collective-permute-start.9 = (bf16[656,128]{1,0:T(8,128)(2,1)S(1)}, bf16[656,128]{1,0:T(8,128)(2,1)S(1)}, u32[]{:S(2)}, u32[]{:S(2)}) collective-permute-start(bf16[656,128]{1,0:T(8,128)(2,1)S(1)} %pad_maximum_fusion.2), channel_id=1, source_target_pairs={{0,2},{1,3},{2,0},{3,1},{4,6},{5,7},{6,4},{7,5},{8,10},{9,11},{10,... | collective-permute-start | bytes 503816 | tf_op jit(solution)/shard_map/ppermute | solution.py:172
  31.3 5.2 %collective-permute-start.12 = (bf16[1312,128]{1,0:T(8,128)(2,1)S(1)}, bf16[1312,128]{1,0:T(8,128)(2,1)S(1)}, u32[]{:S(2)}, u32[]{:S(2)}) collective-permute-start(bf16[1312,128]{1,0:T(8,128)(2,1)S(1)} %pad_maximum_fusion), channel_id=1, source_target_pairs={{0,1},{1,0},{2,3},{3,2},{4,5},{5,4},{6,7},{7,6},{8,9},{9,8},{10,11... | collective-permute-start | bytes 1007624 | tf_op jit(solution)/shard_map/ppermute | solution.py:172
  31.4 5.1 %collective-permute-start.11 = (bf16[1312,128]{1,0:T(8,128)(2,1)S(1)}, bf16[1312,128]{1,0:T(8,128)(2,1)S(1)}, u32[]{:S(2)}, u32[]{:S(2)}) collective-permute-start(bf16[1312,128]{1,0:T(8,128)(2,1)S(1)} %collective-permute-done.7.refs_7_), channel_id=1, source_target_pairs={{0,1},{1,0},{2,3},{3,2},{4,5},{5,4},{6,7},{7,6},{8,9},{9,8},{10,11... | collective-permute-start | bytes 1007624 | tf_op jit(solution)/shard_map/ppermute | solution.py:172
  35.1 1.4 %collective-permute-start.13 = (bf16[656,128]{1,0:T(8,128)(2,1)S(1)}, bf16[656,128]{1,0:T(8,128)(2,1)S(1)}, u32[]{:S(2)}, u32[]{:S(2)}) collective-permute-start(bf16[656,128]{1,0:T(8,128)(2,1)S(1)} %collective-permute-done.9.refs_9_), channel_id=1, source_target_pairs={{0,1},{1,0},{2,3},{3,2},{4,5},{5,4},{6,7},{7,6},{8,9},{9,8},{10,11... | collective-permute-start | bytes 503816 | tf_op jit(solution)/shard_map/ppermute | solution.py:172
  38.9 8.7 %collective-permute-start.14 = (bf16[328,128]{1,0:T(8,128)(2,1)S(1)}, bf16[328,128]{1,0:T(8,128)(2,1)S(1)}, u32[]{:S(2)}, u32[]{:S(2)}) collective-permute-start(bf16[328,128]{1,0:T(8,128)(2,1)S(1)} %get-tuple-element.34), channel_id=1, source_target_pairs={{0,16},{4,20},{8,24},{12,28},{16,0},{20,4},{24,8},{28,12},{1,17},{... | collective-permute-start | bytes 251912 | tf_op jit(solution)/shard_map/ppermute | solution.py:172
  39.6 8.0 %collective-permute-start.15 = (bf16[328,128]{1,0:T(8,128)(2,1)S(1)}, bf16[328,128]{1,0:T(8,128)(2,1)S(1)}, u32[]{:S(2)}, u32[]{:S(2)}) collective-permute-start(bf16[328,128]{1,0:T(8,128)(2,1)S(1)} %get-tuple-element.35), channel_id=1, source_target_pairs={{0,4},{4,0},{8,12},{12,8},{16,20},{20,16},{24,28},{28,24},{1,5},{5... | collective-permute-start | bytes 251912 | tf_op jit(solution)/shard_map/ppermute | solution.py:172
  40.1 10.9 %collective-permute-start.16 = (bf16[328,128]{1,0:T(8,128)(2,1)S(1)}, bf16[328,128]{1,0:T(8,128)(2,1)S(1)}, u32[]{:S(2)}, u32[]{:S(2)}) collective-permute-start(bf16[328,128]{1,0:T(8,128)(2,1)S(1)} %get-tuple-element.36), channel_id=1, source_target_pairs={{0,20},{4,16},{8,28},{12,24},{16,4},{20,0},{24,12},{28,8},{1,21},{... | collective-permute-start | bytes 251912 | tf_op jit(solution)/shard_map/ppermute | solution.py:172
  43.3 7.7 %collective-permute-start.17 = (bf16[328,128]{1,0:T(8,128)(2,1)S(1)}, bf16[328,128]{1,0:T(8,128)(2,1)S(1)}, u32[]{:S(2)}, u32[]{:S(2)}) collective-permute-start(bf16[328,128]{1,0:T(8,128)(2,1)S(1)} %get-tuple-element.37), channel_id=1, source_target_pairs={{0,8},{4,12},{8,0},{12,4},{16,24},{20,28},{24,16},{28,20},{1,9},{5... | collective-permute-start | bytes 251912 | tf_op jit(solution)/shard_map/ppermute | solution.py:172
  44.0 9.3 %collective-permute-start.18 = (bf16[328,128]{1,0:T(8,128)(2,1)S(1)}, bf16[328,128]{1,0:T(8,128)(2,1)S(1)}, u32[]{:S(2)}, u32[]{:S(2)}) collective-permute-start(bf16[328,128]{1,0:T(8,128)(2,1)S(1)} %get-tuple-element.38), channel_id=1, source_target_pairs={{0,24},{4,28},{8,16},{12,20},{16,8},{20,12},{24,0},{28,4},{1,25},{... | collective-permute-start | bytes 251912 | tf_op jit(solution)/shard_map/ppermute | solution.py:172
  47.6 6.9 %collective-permute-start.19 = (bf16[328,128]{1,0:T(8,128)(2,1)S(1)}, bf16[328,128]{1,0:T(8,128)(2,1)S(1)}, u32[]{:S(2)}, u32[]{:S(2)}) collective-permute-start(bf16[328,128]{1,0:T(8,128)(2,1)S(1)} %get-tuple-element.39), channel_id=1, source_target_pairs={{0,12},{4,8},{8,4},{12,0},{16,28},{20,24},{24,20},{28,16},{1,13},{... | collective-permute-start | bytes 251912 | tf_op jit(solution)/shard_map/ppermute | solution.py:172
  47.6 7.8 %collective-permute-start.20 = (bf16[328,128]{1,0:T(8,128)(2,1)S(1)}, bf16[328,128]{1,0:T(8,128)(2,1)S(1)}, u32[]{:S(2)}, u32[]{:S(2)}) collective-permute-start(bf16[328,128]{1,0:T(8,128)(2,1)S(1)} %get-tuple-element.40), channel_id=1, source_target_pairs={{0,28},{4,24},{8,20},{12,16},{16,12},{20,8},{24,4},{28,0},{1,29},{... | collective-permute-start | bytes 251912 | tf_op jit(solution)/shard_map/ppermute | solution.py:172

commit v3 on v2

--- a/solution.py
+++ b/solution.py
@@ -10,6 +10,7 @@
 CAP = 40
 LANES = 128
 VMEM = pl.BlockSpec(memory_space=pltpu.VMEM)
+HBM = pl.BlockSpec(memory_space=pltpu.HBM)
 ROOM = pltpu.CompilerParams(vmem_limit_bytes=24 * 2**20)
 
 
@@ -39,19 +40,20 @@
     return [jnp.sum(wide[p * CAP : (p + 1) * CAP], axis=0, keepdims=True) for p in range(pieces)]
 
 
-def pack_kernel(groups, codes_ref, scales_ref, cluster_ref, select_ref, *out_refs):
+def pack_kernel(groups, codes_hbm, scales_hbm, cluster_hbm, select_ref, *refs):
+    out_refs, (codes_ref, scales_ref, cluster_ref, sems) = refs[:groups], refs[groups:]
+    copies = [
+        pltpu.make_async_copy(src, dst, sems.at[i])
+        for i, (src, dst) in enumerate(
+            ((cluster_hbm, cluster_ref), (scales_hbm, scales_ref), (codes_hbm, codes_ref))
+        )
+    ]
+    for copy in copies:
+        copy.start()
     rows, width = codes_ref.shape
     nblk = scales_ref.shape[0]
     step = width // nblk
-    scales = scales_ref[...].T
-    parts = []
-    total = None
-    for b in range(nblk):
-        x = codes_ref[:, b * step : (b + 1) * step].astype(jnp.float32) * scales[:, b : b + 1]
-        parts.append(x)
-        square = x * x
-        total = square if total is None else total + square
-    inv = lax.rsqrt(jnp.sum(total, axis=1, keepdims=True) / width + 1e-06)
+    copies[0].wait()
     cluster = cluster_ref[...]
     owner = lax.rem(cluster, groups)
     step_row = lax.bitwise_xor(owner, lax.axis_index("grp"))
@@ -71,6 +73,17 @@
     tags = jnp.sum(jnp.where(hit, cluster.astype(jnp.float32) + 1.0, 0.0), axis=1, keepdims=True)
     for s, tag_row in enumerate(gather_lanes(tags, groups)):
         out_refs[s][nblk * CAP :, :] = jnp.broadcast_to(tag_row - 1.0, (8, LANES)).astype(jnp.bfloat16)
+    copies[1].wait()
+    copies[2].wait()
+    scales = scales_ref[...].T
+    parts = []
+    total = None
+    for b in range(nblk):
+        x = codes_ref[:, b * step : (b + 1) * step].astype(jnp.float32) * scales[:, b : b + 1]
+        parts.append(x)
+        square = x * x
+        total = square if total is None else total + square
+    inv = lax.rsqrt(jnp.sum(total, axis=1, keepdims=True) / width + 1e-06)
     for b in range(nblk):
         e = (parts[b] * inv).astype(jnp.bfloat16)
         packed = jnp.dot(select, e, preferred_element_type=jnp.float32).astype(jnp.bfloat16)
@@ -144,13 +157,17 @@
     ).astype(jnp.bfloat16)
     masses = spread(masses_ref[...], groups).astype(jnp.bfloat16)
     mass = lax.dot_general(masses, select, over_slots, preferred_element_type=jnp.float32)
-    mass_ref[...] = jnp.sum(mass, axis=0, keepdims=True).astype(jnp.bfloat16)
+    mass_ref[...] = jnp.sum(mass, axis=0).astype(jnp.bfloat16)
 
 
 def gate(value, *after):
     if not after:
         return value
     return lax.optimization_barrier((value, *after))[0]
+
+
+def off_chip(values):
+    return [pltpu.with_memory_space_constraint(v, pltpu.HBM) for v in values]
 
 
 def on_chip(values):
@@ -177,11 +194,17 @@
     select, *outbox = pl.pallas_call(
         functools.partial(pack_kernel, groups),
         out_shape=[pltpu.VMEM((slots, rows), jnp.bfloat16)] + [piece] * groups,
-        in_specs=[VMEM] * 3,
+        in_specs=[HBM] * 3,
         out_specs=[VMEM] * (1 + groups),
+        scratch_shapes=[
+            pltpu.VMEM(codes.shape, codes.dtype),
+            pltpu.VMEM((nblk, rows), scales.dtype),
+            pltpu.VMEM((1, rows), cluster_id.dtype),
+            pltpu.SemaphoreType.DMA((3,)),
+        ],
         compiler_params=ROOM,
         name="pack",
-    )(codes, scales.T, cluster_id.reshape(1, rows))
+    )(*off_chip([codes, scales.T, cluster_id.reshape(1, rows)]))
 
     held = []
 
@@ -203,21 +226,21 @@
     def grp(s, *after):
         return (swap(gate(outbox[s], *after), "grp", s), [(s, 0)])
 
+    got = {0: (outbox[0], [(0, 0)])}
     early, late = far[: half // 2], far[half // 2 :]
-    got = {0: (outbox[0], [(0, 0)])}
-    for s in early[:1] + near + early[1:]:
+    for s in early[:1] + [1] + near[1:2] + early[1:]:
         got[s] = grp(s)
-    ready = [got[s] for s in [0] + near]
+    ready = [got[0], got[1]]
     first, joined = across(ready)
-    for s in late:
+    for s in near[2:] + late:
         got[s] = grp(s, joined)
-    second, _ = across([got[s] for s in early])
+    mid = [got[s] for s in near[1:] + early]
+    second, _ = across(mid, joined)
     third, last = across([got[s] for s in late])
-    held = [got[s] for s in early[:1] + near + early[1:] + late] + first + second + third + [got[0]]
-    held += [partner(ready + [got[s] for s in early]), partner(first)]
-    held += [partner([got[s] for s in late] + second)]
-    held += [partner([h]) for h in third]
-
+    held = [got[s] for s in early[:1] + [1] + near[1:2] + early[1:] + near[2:] + late] + first + second + third + [got[0]]
+    held += [partner(ready + mid[:1]), partner(mid[1:]), partner(first)]
+    held += [partner([got[s] for s in late])]
+    held += [partner([h]) for h in second + third]
     steps = [s for pair in zip(far, near + [0]) for s in pair]
     places = [[i * groups + steps.index(s) for s, i in where] for _, where in held]
     pieces = groups * members
@@ -240,7 +263,7 @@
         functools.partial(unpack_kernel, done, nblk),
         out_shape=[
             jax.ShapeDtypeStruct((rows, width), jnp.bfloat16),
-            jax.ShapeDtypeStruct((1, rows), jnp.bfloat16),
+            jax.ShapeDtypeStruct((rows,), jnp.bfloat16),
         ],
         in_specs=[VMEM] * (1 + groups),
         out_specs=[VMEM] * 2,
@@ -251,7 +274,7 @@
         compiler_params=ROOM,
         name="unpack",
     )(*on_chip([select] + [back[s] for s in done]))
-    return (smoothed, mass.reshape(rows))
+    return (smoothed, mass)
 
 
 def solution(mesh):

time: 57.5 us -> 52.7 us (0.917)
  waiting for transfers between devices: 22.5 us -> 18.9 us
  local copies, waits for them, and re-layouts: 2.54 us -> 0.04 us
  starting transfers between devices: 25.9 us -> 27 us
  Pallas kernels: 4.92 us -> 5.91 us
    ppermute x21 -> x23, waiting for transfers between devices: 22.5 us -> 18.9 us  [swap(): return lax.ppermute(value, axis, [(i, i ^ step) for i in range(count)])]
    unnamed x11 -> x2, local copies, waits for them, and re-layouts: 2.52 us -> 0.01 us
    ppermute x21 -> x23, starting transfers between devices: 25.9 us -> 27 us  [swap(): return lax.ppermute(value, axis, [(i, i ^ step) for i in range(count)])]
    pallas_call x1, Pallas kernels: 1.27 us -> 2.28 us  [local(): pl.pallas_call(functools.partial(pack_kernel, groups), out_shape=[pltpu.V...]
  transfers between devices with their start and end apart: 21 -> 23, of which waited for: 10 -> 10; matrix products, arithmetic and copies ran while one was open for 0% -> 0% of each run, Pallas kernels for 0% -> 0%
where the time goes in v3:
time: 52.7 us; the launch traced here: 52.6 us
  starting transfers between devices  27 us (51%)
  waiting for transfers between devices  18.9 us (36%)
  Pallas kernels  5.91 us (11%)
  between operations  0.72 us (1%)
    ppermute x23, starting transfers between devices, swap(): return lax.ppermute(value, axis, [(i, i ^ step) for i in range(count)])  27 us
    ppermute x23, waiting for transfers between devices, swap(): return lax.ppermute(value, axis, [(i, i ^ step) for i in range(count)])  18.9 us
    pallas_call x1, Pallas kernels, local(): pl.pallas_call(functools.partial(smooth_kernel, groups, places, nblk), ou...  2.31 us
    pallas_call x1, Pallas kernels, local(): pl.pallas_call(functools.partial(pack_kernel, groups), out_shape=[pltpu.V...  2.28 us
    pallas_call x1, Pallas kernels, local(): pl.pallas_call(functools.partial(unpack_kernel, done, nblk), out_shape=[j...  1.32 us
  transfers between devices with their start and end apart: 23, of which 10 were waited for; matrix products, arithmetic and copies ran while one was open for 0% of the time, Pallas kernels for 0%

profile of v3, /device:TPU:0, one launch (start us, length us, event | category | flops | bytes accessed | tf_op | source)
XLA Modules:
  0.0 52.6 jit_solution(16725719621694161608)
XLA Ops:
  0.6 2.3 %pack.1 = (bf16[320,256]{1,0:T(8,128)(2,1)S(1)}, bf16[328,128]{1,0:T(8,128)(2,1)S(1)}, bf16[328,128]{1,0:T(8,128)(2,1)S(1)}, bf16[328,128]{1,0:T(8,128)(2,1)S(1)...) custom-call(bf16[256,1024]{1,0:T(8,128)(2,1)} %codes_hbm.1, ...), custom_call_target="tpu_custom_call" | custom-call | tf_op jit(solution)/shard_map/pack/pallas_call | solution.py:194
  2.9 4.1 %collective-permute-start = (bf16[328,128]{1,0:T(8,128)(2,1)S(1)}, bf16[328,128]{1,0:T(8,128)(2,1)S(1)}, u32[]{:S(2)}, u32[]{:S(2)}) collective-permute-start(bf16[328,128]{1,0:T(8,128)(2,1)S(1)} %get-tuple-element.24), channel_id=1, source_target_pairs={{0,16},{4,20},{8,24},{12,28},{16,0},{20,4},{24,8},{28,12},{1,17},{... | collective-permute-start | bytes 251912 | tf_op jit(solution)/shard_map/ppermute | solution.py:189
  7.0 1.5 %collective-permute-start.1 = (bf16[328,128]{1,0:T(8,128)(2,1)S(1)}, bf16[328,128]{1,0:T(8,128)(2,1)S(1)}, u32[]{:S(2)}, u32[]{:S(2)}) collective-permute-start(bf16[328,128]{1,0:T(8,128)(2,1)S(1)} %get-tuple-element.25), channel_id=1, source_target_pairs={{0,4},{4,0},{8,12},{12,8},{16,20},{20,16},{24,28},{28,24},{1,5},{5... | collective-permute-start | bytes 251912 | tf_op jit(solution)/shard_map/ppermute | solution.py:189
  8.5 1.6 %collective-permute-start.2 = (bf16[328,128]{1,0:T(8,128)(2,1)S(1)}, bf16[328,128]{1,0:T(8,128)(2,1)S(1)}, u32[]{:S(2)}, u32[]{:S(2)}) collective-permute-start(bf16[328,128]{1,0:T(8,128)(2,1)S(1)} %get-tuple-element.26), channel_id=1, source_target_pairs={{0,8},{4,12},{8,0},{12,4},{16,24},{20,28},{24,16},{28,20},{1,9},{5... | collective-permute-start | bytes 251912 | tf_op jit(solution)/shard_map/ppermute | solution.py:189
  10.4 1.1 %collective-permute-done.1.refs_1_ = bf16[328,128]{1,0:T(8,128)(2,1)S(1)} collective-permute-done((bf16[328,128]{1,0:T(8,128)(2,1)S(1)}, bf16[328,128]{1,0:T(8,128)(2,1)S(1)}, u32[]{:S(2)}, u32[]{:S(2)}) %collective-permute-start.1) | collective-permute-done | bytes 84000 | tf_op jit(solution)/shard_map/ppermute | solution.py:189
  11.5 2.8 %collective-permute-start.4 = (bf16[328,128]{1,0:T(8,128)(2,1)S(1)}, bf16[328,128]{1,0:T(8,128)(2,1)S(1)}, u32[]{:S(2)}, u32[]{:S(2)}) collective-permute-start(bf16[328,128]{1,0:T(8,128)(2,1)S(1)} %get-tuple-element.30), channel_id=1, source_target_pairs={{0,12},{4,8},{8,4},{12,0},{16,28},{20,24},{24,20},{28,16},{1,13},{... | collective-permute-start | bytes 251912 | tf_op jit(solution)/shard_map/ppermute | solution.py:189
  14.3 1.5 %collective-permute-start.7 = (bf16[656,128]{1,0:T(8,128)(2,1)S(1)}, bf16[656,128]{1,0:T(8,128)(2,1)S(1)}, u32[]{:S(2)}, u32[]{:S(2)}) collective-permute-start(bf16[656,128]{1,0:T(8,128)(2,1)S(1)} %constant_dynamic-update-slice_fusion), channel_id=1, source_target_pairs={{0,2},{1,3},{2,0},{3,1},{4,6},{5,7},{6,4},{7,5},{8,10},{9,11},{10,... | collective-permute-start | bytes 503816 | tf_op jit(solution)/shard_map/ppermute | solution.py:189
  15.8 1.2 %collective-permute-start.5 = (bf16[328,128]{1,0:T(8,128)(2,1)S(1)}, bf16[328,128]{1,0:T(8,128)(2,1)S(1)}, u32[]{:S(2)}, u32[]{:S(2)}) collective-permute-start(bf16[328,128]{1,0:T(8,128)(2,1)S(1)} %get-tuple-element.32), channel_id=1, source_target_pairs={{0,24},{4,28},{8,16},{12,20},{16,8},{20,12},{24,0},{28,4},{1,25},{... | collective-permute-start | bytes 251912 | tf_op jit(solution)/shard_map/ppermute | solution.py:189
  17.0 2.4 %collective-permute-start.6 = (bf16[328,128]{1,0:T(8,128)(2,1)S(1)}, bf16[328,128]{1,0:T(8,128)(2,1)S(1)}, u32[]{:S(2)}, u32[]{:S(2)}) collective-permute-start(bf16[328,128]{1,0:T(8,128)(2,1)S(1)} %get-tuple-element.34), channel_id=1, source_target_pairs={{0,28},{4,24},{8,20},{12,16},{16,12},{20,8},{24,4},{28,0},{1,29},{... | collective-permute-start | bytes 251912 | tf_op jit(solution)/shard_map/ppermute | solution.py:189
  19.4 1.2 %collective-permute-start.8 = (bf16[1312,128]{1,0:T(8,128)(2,1)S(1)}, bf16[1312,128]{1,0:T(8,128)(2,1)S(1)}, u32[]{:S(2)}, u32[]{:S(2)}) collective-permute-start(bf16[1312,128]{1,0:T(8,128)(2,1)S(1)} %pad_maximum_fusion), channel_id=1, source_target_pairs={{0,2},{1,3},{2,0},{3,1},{4,6},{5,7},{6,4},{7,5},{8,10},{9,11},{10,... | collective-permute-start | bytes 1007624 | tf_op jit(solution)/shard_map/ppermute | solution.py:189
  20.8 1.7 %collective-permute-done.5.refs_5_ = bf16[328,128]{1,0:T(8,128)(2,1)S(1)} collective-permute-done((bf16[328,128]{1,0:T(8,128)(2,1)S(1)}, bf16[328,128]{1,0:T(8,128)(2,1)S(1)}, u32[]{:S(2)}, u32[]{:S(2)}) %collective-permute-start.5) | collective-permute-done | bytes 84000 | tf_op jit(solution)/shard_map/ppermute | solution.py:189
  22.5 1.8 %collective-permute-done.6.refs_6_ = bf16[328,128]{1,0:T(8,128)(2,1)S(1)} collective-permute-done((bf16[328,128]{1,0:T(8,128)(2,1)S(1)}, bf16[328,128]{1,0:T(8,128)(2,1)S(1)}, u32[]{:S(2)}, u32[]{:S(2)}) %collective-permute-start.6) | collective-permute-done | bytes 84000 | tf_op jit(solution)/shard_map/ppermute | solution.py:189
  25.0 1.8 %collective-permute-done.8.refs_8_ = bf16[1312,128]{1,0:T(8,128)(2,1)S(1)} collective-permute-done((bf16[1312,128]{1,0:T(8,128)(2,1)S(1)}, bf16[1312,128]{1,0:T(8,128)(2,1)S(1)}, u32[]{:S(2)}, u32[]{:S(2)}) %collective-permute-start.8) | collective-permute-done | bytes 335904 | tf_op jit(solution)/shard_map/ppermute | solution.py:189
  27.5 3.5 %collective-permute-done.9.refs_9_ = bf16[656,128]{1,0:T(8,128)(2,1)S(1)} collective-permute-done((bf16[656,128]{1,0:T(8,128)(2,1)S(1)}, bf16[656,128]{1,0:T(8,128)(2,1)S(1)}, u32[]{:S(2)}, u32[]{:S(2)}) %collective-permute-start.9) | collective-permute-done | bytes 167968 | tf_op jit(solution)/shard_map/ppermute | solution.py:189
  31.1 1.4 %collective-permute-done.15.refs_16_ = bf16[656,128]{1,0:T(8,128)(2,1)S(1)} collective-permute-done((bf16[656,128]{1,0:T(8,128)(2,1)S(1)}, bf16[656,128]{1,0:T(8,128)(2,1)S(1)}, u32[]{:S(2)}, u32[]{:S(2)}) %collective-permute-start.15) | collective-permute-done | bytes 167968 | tf_op jit(solution)/shard_map/ppermute | solution.py:189
  32.5 2.3 %smooth.1 = (bf16[328,128]{1,0:T(8,128)(2,1)S(1)}, bf16[328,128]{1,0:T(8,128)(2,1)S(1)}, bf16[328,128]{1,0:T(8,128)(2,1)S(1)}, bf16[328,128]{1,0:T(8,128)(2,1)S(...) custom-call(bf16[328,128]{1,0:T(8,128)(2,1)S(1)} %collective-permute, ...), custom_call_target="tpu_custom_call" | custom-call | tf_op jit(solution)/shard_map/smooth/pallas_call | solution.py:247
  34.8 1.2 %collective-permute-start.16 = (bf16[328,128]{1,0:T(8,128)(2,1)S(1)}, bf16[328,128]{1,0:T(8,128)(2,1)S(1)}, u32[]{:S(2)}, u32[]{:S(2)}) collective-permute-start(bf16[328,128]{1,0:T(8,128)(2,1)S(1)} %get-tuple-element.36), channel_id=1, source_target_pairs={{0,16},{4,20},{8,24},{12,28},{16,0},{20,4},{24,8},{28,12},{1,17},{... | collective-permute-start | bytes 251912 | tf_op jit(solution)/shard_map/ppermute | solution.py:189
  36.5 2.7 %collective-permute-start.18 = (bf16[328,128]{1,0:T(8,128)(2,1)S(1)}, bf16[328,128]{1,0:T(8,128)(2,1)S(1)}, u32[]{:S(2)}, u32[]{:S(2)}) collective-permute-start(bf16[328,128]{1,0:T(8,128)(2,1)S(1)} %get-tuple-element.38), channel_id=1, source_target_pairs={{0,20},{4,16},{8,28},{12,24},{16,4},{20,0},{24,12},{28,8},{1,21},{... | collective-permute-start | bytes 251912 | tf_op jit(solution)/shard_map/ppermute | solution.py:189
  39.9 1.9 %collective-permute-start.20 = (bf16[328,128]{1,0:T(8,128)(2,1)S(1)}, bf16[328,128]{1,0:T(8,128)(2,1)S(1)}, u32[]{:S(2)}, u32[]{:S(2)}) collective-permute-start(bf16[328,128]{1,0:T(8,128)(2,1)S(1)} %get-tuple-element.40), channel_id=1, source_target_pairs={{0,24},{4,28},{8,16},{12,20},{16,8},{20,12},{24,0},{28,4},{1,25},{... | collective-permute-start | bytes 251912 | tf_op jit(solution)/shard_map/ppermute | solution.py:189
  41.9 1.4 %collective-permute-done.16.refs_0_ = bf16[328,128]{1,0:T(8,128)(2,1)S(1)} collective-permute-done((bf16[328,128]{1,0:T(8,128)(2,1)S(1)}, bf16[328,128]{1,0:T(8,128)(2,1)S(1)}, u32[]{:S(2)}, u32[]{:S(2)}) %collective-permute-start.16) | collective-permute-done | bytes 84000 | tf_op jit(solution)/shard_map/ppermute | solution.py:189
  43.3 1.9 %collective-permute-start.22 = (bf16[328,128]{1,0:T(8,128)(2,1)S(1)}, bf16[328,128]{1,0:T(8,128)(2,1)S(1)}, u32[]{:S(2)}, u32[]{:S(2)}) collective-permute-start(bf16[328,128]{1,0:T(8,128)(2,1)S(1)} %get-tuple-element.42), channel_id=1, source_target_pairs={{0,28},{4,24},{8,20},{12,16},{16,12},{20,8},{24,4},{28,0},{1,29},{... | collective-permute-start | bytes 251912 | tf_op jit(solution)/shard_map/ppermute | solution.py:189
  45.2 2.1 %collective-permute-done.18.refs_2_ = bf16[328,128]{1,0:T(8,128)(2,1)S(1)} collective-permute-done((bf16[328,128]{1,0:T(8,128)(2,1)S(1)}, bf16[328,128]{1,0:T(8,128)(2,1)S(1)}, u32[]{:S(2)}, u32[]{:S(2)}) %collective-permute-start.18) | collective-permute-done | bytes 84000 | tf_op jit(solution)/shard_map/ppermute | solution.py:189
  48.4 2.9 %collective-permute-done.21.refs_5_ = bf16[328,128]{1,0:T(8,128)(2,1)S(1)} collective-permute-done((bf16[328,128]{1,0:T(8,128)(2,1)S(1)}, bf16[328,128]{1,0:T(8,128)(2,1)S(1)}, u32[]{:S(2)}, u32[]{:S(2)}) %collective-permute-start.21) | collective-permute-done | bytes 84000 | tf_op jit(solution)/shard_map/ppermute | solution.py:189
  51.3 1.3 %unpack.1 = (bf16[256,1024]{1,0:T(8,128)(2,1)}, bf16[256]{0:T(256)(128)(2,1)}) custom-call(bf16[320,256]{1,0:T(8,128)(2,1)S(1)} %get-tuple-element.23.select_ref, bf16[328,128]{1,0:T(8,128)(2,1)S(1)} %collective-permute-done.16.refs_0_, bf16[328,128]{1,0:T(8,128)(2,1)S(1)} %collective-permute-done.17.refs_1_, ...), custom_call_target="tpu_custom_call" | custom-call | tf_op jit(solution)/shard_map/unpack/pallas_call | solution.py:262
  (32 shorter events, 4.1 us)
Async XLA Ops:
  2.9 12.9 %collective-permute-start = (bf16[328,128]{1,0:T(8,128)(2,1)S(1)}, bf16[328,128]{1,0:T(8,128)(2,1)S(1)}, u32[]{:S(2)}, u32[]{:S(2)}) collective-permute-start(bf16[328,128]{1,0:T(8,128)(2,1)S(1)} %get-tuple-element.24), channel_id=1, source_target_pairs={{0,16},{4,20},{8,24},{12,28},{16,0},{20,4},{24,8},{28,12},{1,17},{... | collective-permute-start | bytes 251912 | tf_op jit(solution)/shard_map/ppermute | solution.py:189
  7.0 4.5 %collective-permute-start.1 = (bf16[328,128]{1,0:T(8,128)(2,1)S(1)}, bf16[328,128]{1,0:T(8,128)(2,1)S(1)}, u32[]{:S(2)}, u32[]{:S(2)}) collective-permute-start(bf16[328,128]{1,0:T(8,128)(2,1)S(1)} %get-tuple-element.25), channel_id=1, source_target_pairs={{0,4},{4,0},{8,12},{12,8},{16,20},{20,16},{24,28},{28,24},{1,5},{5... | collective-permute-start | bytes 251912 | tf_op jit(solution)/shard_map/ppermute | solution.py:189
  8.5 8.5 %collective-permute-start.2 = (bf16[328,128]{1,0:T(8,128)(2,1)S(1)}, bf16[328,128]{1,0:T(8,128)(2,1)S(1)}, u32[]{:S(2)}, u32[]{:S(2)}) collective-permute-start(bf16[328,128]{1,0:T(8,128)(2,1)S(1)} %get-tuple-element.26), channel_id=1, source_target_pairs={{0,8},{4,12},{8,0},{12,4},{16,24},{20,28},{24,16},{28,20},{1,9},{5... | collective-permute-start | bytes 251912 | tf_op jit(solution)/shard_map/ppermute | solution.py:189
  10.1 9.2 %collective-permute-start.3 = (bf16[328,128]{1,0:T(8,128)(2,1)S(1)}, bf16[328,128]{1,0:T(8,128)(2,1)S(1)}, u32[]{:S(2)}, u32[]{:S(2)}) collective-permute-start(bf16[328,128]{1,0:T(8,128)(2,1)S(1)} %get-tuple-element.27), channel_id=1, source_target_pairs={{0,20},{4,16},{8,28},{12,24},{16,4},{20,0},{24,12},{28,8},{1,21},{... | collective-permute-start | bytes 251912 | tf_op jit(solution)/shard_map/ppermute | solution.py:189
  11.5 7.9 %collective-permute-start.4 = (bf16[328,128]{1,0:T(8,128)(2,1)S(1)}, bf16[328,128]{1,0:T(8,128)(2,1)S(1)}, u32[]{:S(2)}, u32[]{:S(2)}) collective-permute-start(bf16[328,128]{1,0:T(8,128)(2,1)S(1)} %get-tuple-element.30), channel_id=1, source_target_pairs={{0,12},{4,8},{8,4},{12,0},{16,28},{20,24},{24,20},{28,16},{1,13},{... | collective-permute-start | bytes 251912 | tf_op jit(solution)/shard_map/ppermute | solution.py:189
  14.3 12.6 %collective-permute-start.7 = (bf16[656,128]{1,0:T(8,128)(2,1)S(1)}, bf16[656,128]{1,0:T(8,128)(2,1)S(1)}, u32[]{:S(2)}, u32[]{:S(2)}) collective-permute-start(bf16[656,128]{1,0:T(8,128)(2,1)S(1)} %constant_dynamic-update-slice_fusion), channel_id=1, source_target_pairs={{0,2},{1,3},{2,0},{3,1},{4,6},{5,7},{6,4},{7,5},{8,10},{9,11},{10,... | collective-permute-start | bytes 503816 | tf_op jit(solution)/shard_map/ppermute | solution.py:189
  15.8 6.7 %collective-permute-start.5 = (bf16[328,128]{1,0:T(8,128)(2,1)S(1)}, bf16[328,128]{1,0:T(8,128)(2,1)S(1)}, u32[]{:S(2)}, u32[]{:S(2)}) collective-permute-start(bf16[328,128]{1,0:T(8,128)(2,1)S(1)} %get-tuple-element.32), channel_id=1, source_target_pairs={{0,24},{4,28},{8,16},{12,20},{16,8},{20,12},{24,0},{28,4},{1,25},{... | collective-permute-start | bytes 251912 | tf_op jit(solution)/shard_map/ppermute | solution.py:189
  17.0 7.3 %collective-permute-start.6 = (bf16[328,128]{1,0:T(8,128)(2,1)S(1)}, bf16[328,128]{1,0:T(8,128)(2,1)S(1)}, u32[]{:S(2)}, u32[]{:S(2)}) collective-permute-start(bf16[328,128]{1,0:T(8,128)(2,1)S(1)} %get-tuple-element.34), channel_id=1, source_target_pairs={{0,28},{4,24},{8,20},{12,16},{16,12},{20,8},{24,4},{28,0},{1,29},{... | collective-permute-start | bytes 251912 | tf_op jit(solution)/shard_map/ppermute | solution.py:189
  19.4 7.4 %collective-permute-start.8 = (bf16[1312,128]{1,0:T(8,128)(2,1)S(1)}, bf16[1312,128]{1,0:T(8,128)(2,1)S(1)}, u32[]{:S(2)}, u32[]{:S(2)}) collective-permute-start(bf16[1312,128]{1,0:T(8,128)(2,1)S(1)} %pad_maximum_fusion), channel_id=1, source_target_pairs={{0,2},{1,3},{2,0},{3,1},{4,6},{5,7},{6,4},{7,5},{8,10},{9,11},{10,... | collective-permute-start | bytes 1007624 | tf_op jit(solution)/shard_map/ppermute | solution.py:189
  20.7 10.4 %collective-permute-start.10 = (bf16[984,128]{1,0:T(8,128)(2,1)S(1)}, bf16[984,128]{1,0:T(8,128)(2,1)S(1)}, u32[]{:S(2)}, u32[]{:S(2)}) collective-permute-start(bf16[984,128]{1,0:T(8,128)(2,1)S(1)} %pad_maximum_fusion.1), channel_id=1, source_target_pairs={{0,1},{1,0},{2,3},{3,2},{4,5},{5,4},{6,7},{7,6},{8,9},{9,8},{10,11... | collective-permute-start | bytes 755720 | tf_op jit(solution)/shard_map/ppermute | solution.py:189
  24.3 3.2 %collective-permute-start.13 = (bf16[656,128]{1,0:T(8,128)(2,1)S(1)}, bf16[656,128]{1,0:T(8,128)(2,1)S(1)}, u32[]{:S(2)}, u32[]{:S(2)}) collective-permute-start(bf16[656,128]{1,0:T(8,128)(2,1)S(1)} %constant_dynamic-update-slice_fusion.2), channel_id=1, source_target_pairs={{0,1},{1,0},{2,3},{3,2},{4,5},{5,4},{6,7},{7,6},{8,9},{9,8},{10,11... | collective-permute-start | bytes 503816 | tf_op jit(solution)/shard_map/ppermute | solution.py:189
  24.4 6.7 %collective-permute-start.9 = (bf16[656,128]{1,0:T(8,128)(2,1)S(1)}, bf16[656,128]{1,0:T(8,128)(2,1)S(1)}, u32[]{:S(2)}, u32[]{:S(2)}) collective-permute-start(bf16[656,128]{1,0:T(8,128)(2,1)S(1)} %constant_dynamic-update-slice_fusion.2), channel_id=1, source_target_pairs={{0,2},{1,3},{2,0},{3,1},{4,6},{5,7},{6,4},{7,5},{8,10},{9,11},{10,... | collective-permute-start | bytes 503816 | tf_op jit(solution)/shard_map/ppermute | solution.py:189
  26.8 5.6 %collective-permute-start.14 = (bf16[1312,128]{1,0:T(8,128)(2,1)S(1)}, bf16[1312,128]{1,0:T(8,128)(2,1)S(1)}, u32[]{:S(2)}, u32[]{:S(2)}) collective-permute-start(bf16[1312,128]{1,0:T(8,128)(2,1)S(1)} %collective-permute-done.8.refs_8_), channel_id=1, source_target_pairs={{0,1},{1,0},{2,3},{3,2},{4,5},{5,4},{6,7},{7,6},{8,9},{9,8},{10,11... | collective-permute-start | bytes 1007624 | tf_op jit(solution)/shard_map/ppermute | solution.py:189
  26.9 4.2 %collective-permute-start.11 = (bf16[984,128]{1,0:T(8,128)(2,1)S(1)}, bf16[984,128]{1,0:T(8,128)(2,1)S(1)}, u32[]{:S(2)}, u32[]{:S(2)}) collective-permute-start(bf16[984,128]{1,0:T(8,128)(2,1)S(1)} %pad_maximum_fusion.2), channel_id=1, source_target_pairs={{0,1},{1,0},{2,3},{3,2},{4,5},{5,4},{6,7},{7,6},{8,9},{9,8},{10,11... | collective-permute-start | bytes 755720 | tf_op jit(solution)/shard_map/ppermute | solution.py:189
  27.5 3.6 %collective-permute-start.12 = (bf16[656,128]{1,0:T(8,128)(2,1)S(1)}, bf16[656,128]{1,0:T(8,128)(2,1)S(1)}, u32[]{:S(2)}, u32[]{:S(2)}) collective-permute-start(bf16[656,128]{1,0:T(8,128)(2,1)S(1)} %collective-permute-done.7.refs_7_), channel_id=1, source_target_pairs={{0,1},{1,0},{2,3},{3,2},{4,5},{5,4},{6,7},{7,6},{8,9},{9,8},{10,11... | collective-permute-start | bytes 503816 | tf_op jit(solution)/shard_map/ppermute | solution.py:189
  31.1 1.4 %collective-permute-start.15 = (bf16[656,128]{1,0:T(8,128)(2,1)S(1)}, bf16[656,128]{1,0:T(8,128)(2,1)S(1)}, u32[]{:S(2)}, u32[]{:S(2)}) collective-permute-start(bf16[656,128]{1,0:T(8,128)(2,1)S(1)} %collective-permute-done.9.refs_9_), channel_id=1, source_target_pairs={{0,1},{1,0},{2,3},{3,2},{4,5},{5,4},{6,7},{7,6},{8,9},{9,8},{10,11... | collective-permute-start | bytes 503816 | tf_op jit(solution)/shard_map/ppermute | solution.py:189
  34.8 8.5 %collective-permute-start.16 = (bf16[328,128]{1,0:T(8,128)(2,1)S(1)}, bf16[328,128]{1,0:T(8,128)(2,1)S(1)}, u32[]{:S(2)}, u32[]{:S(2)}) collective-permute-start(bf16[328,128]{1,0:T(8,128)(2,1)S(1)} %get-tuple-element.36), channel_id=1, source_target_pairs={{0,16},{4,20},{8,24},{12,28},{16,0},{20,4},{24,8},{28,12},{1,17},{... | collective-permute-start | bytes 251912 | tf_op jit(solution)/shard_map/ppermute | solution.py:189
  36.0 7.3 %collective-permute-start.17 = (bf16[328,128]{1,0:T(8,128)(2,1)S(1)}, bf16[328,128]{1,0:T(8,128)(2,1)S(1)}, u32[]{:S(2)}, u32[]{:S(2)}) collective-permute-start(bf16[328,128]{1,0:T(8,128)(2,1)S(1)} %get-tuple-element.37), channel_id=1, source_target_pairs={{0,4},{4,0},{8,12},{12,8},{16,20},{20,16},{24,28},{28,24},{1,5},{5... | collective-permute-start | bytes 251912 | tf_op jit(solution)/shard_map/ppermute | solution.py:189
  36.5 10.8 %collective-permute-start.18 = (bf16[328,128]{1,0:T(8,128)(2,1)S(1)}, bf16[328,128]{1,0:T(8,128)(2,1)S(1)}, u32[]{:S(2)}, u32[]{:S(2)}) collective-permute-start(bf16[328,128]{1,0:T(8,128)(2,1)S(1)} %get-tuple-element.38), channel_id=1, source_target_pairs={{0,20},{4,16},{8,28},{12,24},{16,4},{20,0},{24,12},{28,8},{1,21},{... | collective-permute-start | bytes 251912 | tf_op jit(solution)/shard_map/ppermute | solution.py:189
  39.2 8.1 %collective-permute-start.19 = (bf16[328,128]{1,0:T(8,128)(2,1)S(1)}, bf16[328,128]{1,0:T(8,128)(2,1)S(1)}, u32[]{:S(2)}, u32[]{:S(2)}) collective-permute-start(bf16[328,128]{1,0:T(8,128)(2,1)S(1)} %get-tuple-element.39), channel_id=1, source_target_pairs={{0,8},{4,12},{8,0},{12,4},{16,24},{20,28},{24,16},{28,20},{1,9},{5... | collective-permute-start | bytes 251912 | tf_op jit(solution)/shard_map/ppermute | solution.py:189
  39.9 8.4 %collective-permute-start.20 = (bf16[328,128]{1,0:T(8,128)(2,1)S(1)}, bf16[328,128]{1,0:T(8,128)(2,1)S(1)}, u32[]{:S(2)}, u32[]{:S(2)}) collective-permute-start(bf16[328,128]{1,0:T(8,128)(2,1)S(1)} %get-tuple-element.40), channel_id=1, source_target_pairs={{0,24},{4,28},{8,16},{12,20},{16,8},{20,12},{24,0},{28,4},{1,25},{... | collective-permute-start | bytes 251912 | tf_op jit(solution)/shard_map/ppermute | solution.py:189
  43.3 8.0 %collective-permute-start.21 = (bf16[328,128]{1,0:T(8,128)(2,1)S(1)}, bf16[328,128]{1,0:T(8,128)(2,1)S(1)}, u32[]{:S(2)}, u32[]{:S(2)}) collective-permute-start(bf16[328,128]{1,0:T(8,128)(2,1)S(1)} %get-tuple-element.41), channel_id=1, source_target_pairs={{0,12},{4,8},{8,4},{12,0},{16,28},{20,24},{24,20},{28,16},{1,13},{... | collective-permute-start | bytes 251912 | tf_op jit(solution)/shard_map/ppermute | solution.py:189
  43.3 8.0 %collective-permute-start.22 = (bf16[328,128]{1,0:T(8,128)(2,1)S(1)}, bf16[328,128]{1,0:T(8,128)(2,1)S(1)}, u32[]{:S(2)}, u32[]{:S(2)}) collective-permute-start(bf16[328,128]{1,0:T(8,128)(2,1)S(1)} %get-tuple-element.42), channel_id=1, source_target_pairs={{0,28},{4,24},{8,20},{12,16},{16,12},{20,8},{24,4},{28,0},{1,29},{... | collective-permute-start | bytes 251912 | tf_op jit(solution)/shard_map/ppermute | solution.py:189

commit v4 on v3

--- a/solution.py
+++ b/solution.py
@@ -84,11 +84,15 @@
         square = x * x
         total = square if total is None else total + square
     inv = lax.rsqrt(jnp.sum(total, axis=1, keepdims=True) / width + 1e-06)
-    for b in range(nblk):
-        e = (parts[b] * inv).astype(jnp.bfloat16)
+    for at in range(0, nblk, 8):
+        e = jnp.concatenate([(x * inv).astype(jnp.bfloat16) for x in parts[at : at + 8]], axis=1)
         packed = jnp.dot(select, e, preferred_element_type=jnp.float32).astype(jnp.bfloat16)
-        for s in range(groups):
-            out_refs[s][b * CAP : (b + 1) * CAP, :] = packed[s * CAP : (s + 1) * CAP]
+        for k in range(e.shape[1] // step):
+            b = at + k
+            for s in range(groups):
+                out_refs[s][b * CAP : (b + 1) * CAP, :] = packed[
+                    s * CAP : (s + 1) * CAP, k * step : (k + 1) * step
+                ]
 
 
 def smooth_kernel(groups, places, nblk, *refs):
@@ -120,7 +124,6 @@
         lax.dot_general(
             queries, keys, (((1,), (1,)), ((), ())), preferred_element_type=jnp.float32
         )
-        / width
     )
     keep = (
         (qtags == ktags)
@@ -130,10 +133,10 @@
             != lax.broadcasted_iota(jnp.int32, (slots, count), 1)
         )
     )
-    weights = jnp.where(keep, jnp.exp(8.0 * (sims - 1.0)), 0.0)
+    weights = jnp.where(keep, jnp.exp(sims * (8.0 / width) - 8.0), 0.0)
     den = 1.0 + jnp.sum(weights, axis=1, keepdims=True)
     num = jnp.dot(weights.astype(jnp.bfloat16), keys, preferred_element_type=jnp.float32)
-    result = ((queries.astype(jnp.float32) + num) / den).astype(jnp.bfloat16)
+    result = ((queries.astype(jnp.float32) + num) * (1.0 / den)).astype(jnp.bfloat16)
     for s, mass_row in enumerate(gather_lanes(jnp.log(den), groups)):
         for b in range(nblk):
             out_refs[s][b * CAP : (b + 1) * CAP, :] = result[

time: 52.7 us -> 52.6 us (level)
  no operation moved by 1% of the time
where the time goes in v4:
time: 52.6 us; the launch traced here: 52.4 us
  starting transfers between devices  26.9 us (51%)
  waiting for transfers between devices  18.9 us (36%)
  Pallas kernels  5.73 us (11%)
  between operations  0.72 us (1%)
    ppermute x23, starting transfers between devices, swap(): return lax.ppermute(value, axis, [(i, i ^ step) for i in range(count)])  26.9 us
    ppermute x23, waiting for transfers between devices, swap(): return lax.ppermute(value, axis, [(i, i ^ step) for i in range(count)])  18.9 us
    pallas_call x1, Pallas kernels, local(): pl.pallas_call(functools.partial(smooth_kernel, groups, places, nblk), ou...  2.3 us
    pallas_call x1, Pallas kernels, local(): pl.pallas_call(functools.partial(pack_kernel, groups), out_shape=[pltpu.V...  2.11 us
    pallas_call x1, Pallas kernels, local(): pl.pallas_call(functools.partial(unpack_kernel, done, nblk), out_shape=[j...  1.32 us
  transfers between devices with their start and end apart: 23, of which 10 were waited for; matrix products, arithmetic and copies ran while one was open for 0% of the time, Pallas kernels for 0%

profile of v4, /device:TPU:0, one launch (start us, length us, event | category | flops | bytes accessed | tf_op | source)
XLA Modules:
  0.0 52.4 jit_solution(8959840519180012278)
XLA Ops:
  0.6 2.1 %pack.1 = (bf16[320,256]{1,0:T(8,128)(2,1)S(1)}, bf16[328,128]{1,0:T(8,128)(2,1)S(1)}, bf16[328,128]{1,0:T(8,128)(2,1)S(1)}, bf16[328,128]{1,0:T(8,128)(2,1)S(1)...) custom-call(bf16[256,1024]{1,0:T(8,128)(2,1)} %codes_hbm.1, ...), custom_call_target="tpu_custom_call" | custom-call | tf_op jit(solution)/shard_map/pack/pallas_call | solution.py:197
  2.7 4.1 %collective-permute-start = (bf16[328,128]{1,0:T(8,128)(2,1)S(1)}, bf16[328,128]{1,0:T(8,128)(2,1)S(1)}, u32[]{:S(2)}, u32[]{:S(2)}) collective-permute-start(bf16[328,128]{1,0:T(8,128)(2,1)S(1)} %get-tuple-element.24), channel_id=1, source_target_pairs={{0,16},{4,20},{8,24},{12,28},{16,0},{20,4},{24,8},{28,12},{1,17},{... | collective-permute-start | bytes 251912 | tf_op jit(solution)/shard_map/ppermute | solution.py:192
  6.8 1.5 %collective-permute-start.1 = (bf16[328,128]{1,0:T(8,128)(2,1)S(1)}, bf16[328,128]{1,0:T(8,128)(2,1)S(1)}, u32[]{:S(2)}, u32[]{:S(2)}) collective-permute-start(bf16[328,128]{1,0:T(8,128)(2,1)S(1)} %get-tuple-element.25), channel_id=1, source_target_pairs={{0,4},{4,0},{8,12},{12,8},{16,20},{20,16},{24,28},{28,24},{1,5},{5... | collective-permute-start | bytes 251912 | tf_op jit(solution)/shard_map/ppermute | solution.py:192
  8.4 1.6 %collective-permute-start.2 = (bf16[328,128]{1,0:T(8,128)(2,1)S(1)}, bf16[328,128]{1,0:T(8,128)(2,1)S(1)}, u32[]{:S(2)}, u32[]{:S(2)}) collective-permute-start(bf16[328,128]{1,0:T(8,128)(2,1)S(1)} %get-tuple-element.26), channel_id=1, source_target_pairs={{0,8},{4,12},{8,0},{12,4},{16,24},{20,28},{24,16},{28,20},{1,9},{5... | collective-permute-start | bytes 251912 | tf_op jit(solution)/shard_map/ppermute | solution.py:192
  11.3 2.8 %collective-permute-start.4 = (bf16[328,128]{1,0:T(8,128)(2,1)S(1)}, bf16[328,128]{1,0:T(8,128)(2,1)S(1)}, u32[]{:S(2)}, u32[]{:S(2)}) collective-permute-start(bf16[328,128]{1,0:T(8,128)(2,1)S(1)} %get-tuple-element.30), channel_id=1, source_target_pairs={{0,12},{4,8},{8,4},{12,0},{16,28},{20,24},{24,20},{28,16},{1,13},{... | collective-permute-start | bytes 251912 | tf_op jit(solution)/shard_map/ppermute | solution.py:192
  14.1 1.5 %collective-permute-start.7 = (bf16[656,128]{1,0:T(8,128)(2,1)S(1)}, bf16[656,128]{1,0:T(8,128)(2,1)S(1)}, u32[]{:S(2)}, u32[]{:S(2)}) collective-permute-start(bf16[656,128]{1,0:T(8,128)(2,1)S(1)} %constant_dynamic-update-slice_fusion), channel_id=1, source_target_pairs={{0,2},{1,3},{2,0},{3,1},{4,6},{5,7},{6,4},{7,5},{8,10},{9,11},{10,... | collective-permute-start | bytes 503816 | tf_op jit(solution)/shard_map/ppermute | solution.py:192
  15.6 1.2 %collective-permute-start.5 = (bf16[328,128]{1,0:T(8,128)(2,1)S(1)}, bf16[328,128]{1,0:T(8,128)(2,1)S(1)}, u32[]{:S(2)}, u32[]{:S(2)}) collective-permute-start(bf16[328,128]{1,0:T(8,128)(2,1)S(1)} %get-tuple-element.32), channel_id=1, source_target_pairs={{0,24},{4,28},{8,16},{12,20},{16,8},{20,12},{24,0},{28,4},{1,25},{... | collective-permute-start | bytes 251912 | tf_op jit(solution)/shard_map/ppermute | solution.py:192
  16.8 2.4 %collective-permute-start.6 = (bf16[328,128]{1,0:T(8,128)(2,1)S(1)}, bf16[328,128]{1,0:T(8,128)(2,1)S(1)}, u32[]{:S(2)}, u32[]{:S(2)}) collective-permute-start(bf16[328,128]{1,0:T(8,128)(2,1)S(1)} %get-tuple-element.34), channel_id=1, source_target_pairs={{0,28},{4,24},{8,20},{12,16},{16,12},{20,8},{24,4},{28,0},{1,29},{... | collective-permute-start | bytes 251912 | tf_op jit(solution)/shard_map/ppermute | solution.py:192
  19.2 1.2 %collective-permute-start.8 = (bf16[1312,128]{1,0:T(8,128)(2,1)S(1)}, bf16[1312,128]{1,0:T(8,128)(2,1)S(1)}, u32[]{:S(2)}, u32[]{:S(2)}) collective-permute-start(bf16[1312,128]{1,0:T(8,128)(2,1)S(1)} %pad_maximum_fusion), channel_id=1, source_target_pairs={{0,2},{1,3},{2,0},{3,1},{4,6},{5,7},{6,4},{7,5},{8,10},{9,11},{10,... | collective-permute-start | bytes 1007624 | tf_op jit(solution)/shard_map/ppermute | solution.py:192
  20.6 1.7 %collective-permute-done.5.refs_5_ = bf16[328,128]{1,0:T(8,128)(2,1)S(1)} collective-permute-done((bf16[328,128]{1,0:T(8,128)(2,1)S(1)}, bf16[328,128]{1,0:T(8,128)(2,1)S(1)}, u32[]{:S(2)}, u32[]{:S(2)}) %collective-permute-start.5) | collective-permute-done | bytes 84000 | tf_op jit(solution)/shard_map/ppermute | solution.py:192
  22.3 1.8 %collective-permute-done.6.refs_6_ = bf16[328,128]{1,0:T(8,128)(2,1)S(1)} collective-permute-done((bf16[328,128]{1,0:T(8,128)(2,1)S(1)}, bf16[328,128]{1,0:T(8,128)(2,1)S(1)}, u32[]{:S(2)}, u32[]{:S(2)}) %collective-permute-start.6) | collective-permute-done | bytes 84000 | tf_op jit(solution)/shard_map/ppermute | solution.py:192
  24.8 1.8 %collective-permute-done.8.refs_8_ = bf16[1312,128]{1,0:T(8,128)(2,1)S(1)} collective-permute-done((bf16[1312,128]{1,0:T(8,128)(2,1)S(1)}, bf16[1312,128]{1,0:T(8,128)(2,1)S(1)}, u32[]{:S(2)}, u32[]{:S(2)}) %collective-permute-start.8) | collective-permute-done | bytes 335904 | tf_op jit(solution)/shard_map/ppermute | solution.py:192
  27.4 3.5 %collective-permute-done.9.refs_9_ = bf16[656,128]{1,0:T(8,128)(2,1)S(1)} collective-permute-done((bf16[656,128]{1,0:T(8,128)(2,1)S(1)}, bf16[656,128]{1,0:T(8,128)(2,1)S(1)}, u32[]{:S(2)}, u32[]{:S(2)}) %collective-permute-start.9) | collective-permute-done | bytes 167968 | tf_op jit(solution)/shard_map/ppermute | solution.py:192
  30.9 1.4 %collective-permute-done.15.refs_16_ = bf16[656,128]{1,0:T(8,128)(2,1)S(1)} collective-permute-done((bf16[656,128]{1,0:T(8,128)(2,1)S(1)}, bf16[656,128]{1,0:T(8,128)(2,1)S(1)}, u32[]{:S(2)}, u32[]{:S(2)}) %collective-permute-start.15) | collective-permute-done | bytes 167968 | tf_op jit(solution)/shard_map/ppermute | solution.py:192
  32.3 2.3 %smooth.1 = (bf16[328,128]{1,0:T(8,128)(2,1)S(1)}, bf16[328,128]{1,0:T(8,128)(2,1)S(1)}, bf16[328,128]{1,0:T(8,128)(2,1)S(1)}, bf16[328,128]{1,0:T(8,128)(2,1)S(...) custom-call(bf16[328,128]{1,0:T(8,128)(2,1)S(1)} %collective-permute, ...), custom_call_target="tpu_custom_call" | custom-call | tf_op jit(solution)/shard_map/smooth/pallas_call | solution.py:250
  34.6 1.2 %collective-permute-start.16 = (bf16[328,128]{1,0:T(8,128)(2,1)S(1)}, bf16[328,128]{1,0:T(8,128)(2,1)S(1)}, u32[]{:S(2)}, u32[]{:S(2)}) collective-permute-start(bf16[328,128]{1,0:T(8,128)(2,1)S(1)} %get-tuple-element.36), channel_id=1, source_target_pairs={{0,16},{4,20},{8,24},{12,28},{16,0},{20,4},{24,8},{28,12},{1,17},{... | collective-permute-start | bytes 251912 | tf_op jit(solution)/shard_map/ppermute | solution.py:192
  36.3 2.7 %collective-permute-start.18 = (bf16[328,128]{1,0:T(8,128)(2,1)S(1)}, bf16[328,128]{1,0:T(8,128)(2,1)S(1)}, u32[]{:S(2)}, u32[]{:S(2)}) collective-permute-start(bf16[328,128]{1,0:T(8,128)(2,1)S(1)} %get-tuple-element.38), channel_id=1, source_target_pairs={{0,20},{4,16},{8,28},{12,24},{16,4},{20,0},{24,12},{28,8},{1,21},{... | collective-permute-start | bytes 251912 | tf_op jit(solution)/shard_map/ppermute | solution.py:192
  39.7 1.9 %collective-permute-start.20 = (bf16[328,128]{1,0:T(8,128)(2,1)S(1)}, bf16[328,128]{1,0:T(8,128)(2,1)S(1)}, u32[]{:S(2)}, u32[]{:S(2)}) collective-permute-start(bf16[328,128]{1,0:T(8,128)(2,1)S(1)} %get-tuple-element.40), channel_id=1, source_target_pairs={{0,24},{4,28},{8,16},{12,20},{16,8},{20,12},{24,0},{28,4},{1,25},{... | collective-permute-start | bytes 251912 | tf_op jit(solution)/shard_map/ppermute | solution.py:192
  41.7 1.4 %collective-permute-done.16.refs_0_ = bf16[328,128]{1,0:T(8,128)(2,1)S(1)} collective-permute-done((bf16[328,128]{1,0:T(8,128)(2,1)S(1)}, bf16[328,128]{1,0:T(8,128)(2,1)S(1)}, u32[]{:S(2)}, u32[]{:S(2)}) %collective-permute-start.16) | collective-permute-done | bytes 84000 | tf_op jit(solution)/shard_map/ppermute | solution.py:192
  43.1 1.8 %collective-permute-start.22 = (bf16[328,128]{1,0:T(8,128)(2,1)S(1)}, bf16[328,128]{1,0:T(8,128)(2,1)S(1)}, u32[]{:S(2)}, u32[]{:S(2)}) collective-permute-start(bf16[328,128]{1,0:T(8,128)(2,1)S(1)} %get-tuple-element.42), channel_id=1, source_target_pairs={{0,28},{4,24},{8,20},{12,16},{16,12},{20,8},{24,4},{28,0},{1,29},{... | collective-permute-start | bytes 251912 | tf_op jit(solution)/shard_map/ppermute | solution.py:192
  45.0 2.2 %collective-permute-done.18.refs_2_ = bf16[328,128]{1,0:T(8,128)(2,1)S(1)} collective-permute-done((bf16[328,128]{1,0:T(8,128)(2,1)S(1)}, bf16[328,128]{1,0:T(8,128)(2,1)S(1)}, u32[]{:S(2)}, u32[]{:S(2)}) %collective-permute-start.18) | collective-permute-done | bytes 84000 | tf_op jit(solution)/shard_map/ppermute | solution.py:192
  47.1 1.1 %collective-permute-done.20.refs_4_ = bf16[328,128]{1,0:T(8,128)(2,1)S(1)} collective-permute-done((bf16[328,128]{1,0:T(8,128)(2,1)S(1)}, bf16[328,128]{1,0:T(8,128)(2,1)S(1)}, u32[]{:S(2)}, u32[]{:S(2)}) %collective-permute-start.20) | collective-permute-done | bytes 84000 | tf_op jit(solution)/shard_map/ppermute | solution.py:192
  48.3 2.8 %collective-permute-done.21.refs_5_ = bf16[328,128]{1,0:T(8,128)(2,1)S(1)} collective-permute-done((bf16[328,128]{1,0:T(8,128)(2,1)S(1)}, bf16[328,128]{1,0:T(8,128)(2,1)S(1)}, u32[]{:S(2)}, u32[]{:S(2)}) %collective-permute-start.21) | collective-permute-done | bytes 84000 | tf_op jit(solution)/shard_map/ppermute | solution.py:192
  51.1 1.3 %unpack.1 = (bf16[256,1024]{1,0:T(8,128)(2,1)}, bf16[256]{0:T(256)(128)(2,1)}) custom-call(bf16[320,256]{1,0:T(8,128)(2,1)S(1)} %get-tuple-element.23.select_ref, bf16[328,128]{1,0:T(8,128)(2,1)S(1)} %collective-permute-done.16.refs_0_, bf16[328,128]{1,0:T(8,128)(2,1)S(1)} %collective-permute-done.17.refs_1_, ...), custom_call_target="tpu_custom_call" | custom-call | tf_op jit(solution)/shard_map/unpack/pallas_call | solution.py:265
  (32 shorter events, 4.1 us)
Async XLA Ops:
  2.7 12.9 %collective-permute-start = (bf16[328,128]{1,0:T(8,128)(2,1)S(1)}, bf16[328,128]{1,0:T(8,128)(2,1)S(1)}, u32[]{:S(2)}, u32[]{:S(2)}) collective-permute-start(bf16[328,128]{1,0:T(8,128)(2,1)S(1)} %get-tuple-element.24), channel_id=1, source_target_pairs={{0,16},{4,20},{8,24},{12,28},{16,0},{20,4},{24,8},{28,12},{1,17},{... | collective-permute-start | bytes 251912 | tf_op jit(solution)/shard_map/ppermute | solution.py:192
  6.8 4.5 %collective-permute-start.1 = (bf16[328,128]{1,0:T(8,128)(2,1)S(1)}, bf16[328,128]{1,0:T(8,128)(2,1)S(1)}, u32[]{:S(2)}, u32[]{:S(2)}) collective-permute-start(bf16[328,128]{1,0:T(8,128)(2,1)S(1)} %get-tuple-element.25), channel_id=1, source_target_pairs={{0,4},{4,0},{8,12},{12,8},{16,20},{20,16},{24,28},{28,24},{1,5},{5... | collective-permute-start | bytes 251912 | tf_op jit(solution)/shard_map/ppermute | solution.py:192
  8.4 8.5 %collective-permute-start.2 = (bf16[328,128]{1,0:T(8,128)(2,1)S(1)}, bf16[328,128]{1,0:T(8,128)(2,1)S(1)}, u32[]{:S(2)}, u32[]{:S(2)}) collective-permute-start(bf16[328,128]{1,0:T(8,128)(2,1)S(1)} %get-tuple-element.26), channel_id=1, source_target_pairs={{0,8},{4,12},{8,0},{12,4},{16,24},{20,28},{24,16},{28,20},{1,9},{5... | collective-permute-start | bytes 251912 | tf_op jit(solution)/shard_map/ppermute | solution.py:192
  9.9 9.3 %collective-permute-start.3 = (bf16[328,128]{1,0:T(8,128)(2,1)S(1)}, bf16[328,128]{1,0:T(8,128)(2,1)S(1)}, u32[]{:S(2)}, u32[]{:S(2)}) collective-permute-start(bf16[328,128]{1,0:T(8,128)(2,1)S(1)} %get-tuple-element.27), channel_id=1, source_target_pairs={{0,20},{4,16},{8,28},{12,24},{16,4},{20,0},{24,12},{28,8},{1,21},{... | collective-permute-start | bytes 251912 | tf_op jit(solution)/shard_map/ppermute | solution.py:192
  11.3 7.9 %collective-permute-start.4 = (bf16[328,128]{1,0:T(8,128)(2,1)S(1)}, bf16[328,128]{1,0:T(8,128)(2,1)S(1)}, u32[]{:S(2)}, u32[]{:S(2)}) collective-permute-start(bf16[328,128]{1,0:T(8,128)(2,1)S(1)} %get-tuple-element.30), channel_id=1, source_target_pairs={{0,12},{4,8},{8,4},{12,0},{16,28},{20,24},{24,20},{28,16},{1,13},{... | collective-permute-start | bytes 251912 | tf_op jit(solution)/shard_map/ppermute | solution.py:192
  14.1 12.6 %collective-permute-start.7 = (bf16[656,128]{1,0:T(8,128)(2,1)S(1)}, bf16[656,128]{1,0:T(8,128)(2,1)S(1)}, u32[]{:S(2)}, u32[]{:S(2)}) collective-permute-start(bf16[656,128]{1,0:T(8,128)(2,1)S(1)} %constant_dynamic-update-slice_fusion), channel_id=1, source_target_pairs={{0,2},{1,3},{2,0},{3,1},{4,6},{5,7},{6,4},{7,5},{8,10},{9,11},{10,... | collective-permute-start | bytes 503816 | tf_op jit(solution)/shard_map/ppermute | solution.py:192
  15.6 6.7 %collective-permute-start.5 = (bf16[328,128]{1,0:T(8,128)(2,1)S(1)}, bf16[328,128]{1,0:T(8,128)(2,1)S(1)}, u32[]{:S(2)}, u32[]{:S(2)}) collective-permute-start(bf16[328,128]{1,0:T(8,128)(2,1)S(1)} %get-tuple-element.32), channel_id=1, source_target_pairs={{0,24},{4,28},{8,16},{12,20},{16,8},{20,12},{24,0},{28,4},{1,25},{... | collective-permute-start | bytes 251912 | tf_op jit(solution)/shard_map/ppermute | solution.py:192
  16.8 7.3 %collective-permute-start.6 = (bf16[328,128]{1,0:T(8,128)(2,1)S(1)}, bf16[328,128]{1,0:T(8,128)(2,1)S(1)}, u32[]{:S(2)}, u32[]{:S(2)}) collective-permute-start(bf16[328,128]{1,0:T(8,128)(2,1)S(1)} %get-tuple-element.34), channel_id=1, source_target_pairs={{0,28},{4,24},{8,20},{12,16},{16,12},{20,8},{24,4},{28,0},{1,29},{... | collective-permute-start | bytes 251912 | tf_op jit(solution)/shard_map/ppermute | solution.py:192
  19.2 7.4 %collective-permute-start.8 = (bf16[1312,128]{1,0:T(8,128)(2,1)S(1)}, bf16[1312,128]{1,0:T(8,128)(2,1)S(1)}, u32[]{:S(2)}, u32[]{:S(2)}) collective-permute-start(bf16[1312,128]{1,0:T(8,128)(2,1)S(1)} %pad_maximum_fusion), channel_id=1, source_target_pairs={{0,2},{1,3},{2,0},{3,1},{4,6},{5,7},{6,4},{7,5},{8,10},{9,11},{10,... | collective-permute-start | bytes 1007624 | tf_op jit(solution)/shard_map/ppermute | solution.py:192
  20.5 10.4 %collective-permute-start.10 = (bf16[984,128]{1,0:T(8,128)(2,1)S(1)}, bf16[984,128]{1,0:T(8,128)(2,1)S(1)}, u32[]{:S(2)}, u32[]{:S(2)}) collective-permute-start(bf16[984,128]{1,0:T(8,128)(2,1)S(1)} %pad_maximum_fusion.1), channel_id=1, source_target_pairs={{0,1},{1,0},{2,3},{3,2},{4,5},{5,4},{6,7},{7,6},{8,9},{9,8},{10,11... | collective-permute-start | bytes 755720 | tf_op jit(solution)/shard_map/ppermute | solution.py:192
  24.1 3.2 %collective-permute-start.13 = (bf16[656,128]{1,0:T(8,128)(2,1)S(1)}, bf16[656,128]{1,0:T(8,128)(2,1)S(1)}, u32[]{:S(2)}, u32[]{:S(2)}) collective-permute-start(bf16[656,128]{1,0:T(8,128)(2,1)S(1)} %constant_dynamic-update-slice_fusion.2), channel_id=1, source_target_pairs={{0,1},{1,0},{2,3},{3,2},{4,5},{5,4},{6,7},{7,6},{8,9},{9,8},{10,11... | collective-permute-start | bytes 503816 | tf_op jit(solution)/shard_map/ppermute | solution.py:192
  24.2 6.7 %collective-permute-start.9 = (bf16[656,128]{1,0:T(8,128)(2,1)S(1)}, bf16[656,128]{1,0:T(8,128)(2,1)S(1)}, u32[]{:S(2)}, u32[]{:S(2)}) collective-permute-start(bf16[656,128]{1,0:T(8,128)(2,1)S(1)} %constant_dynamic-update-slice_fusion.2), channel_id=1, source_target_pairs={{0,2},{1,3},{2,0},{3,1},{4,6},{5,7},{6,4},{7,5},{8,10},{9,11},{10,... | collective-permute-start | bytes 503816 | tf_op jit(solution)/shard_map/ppermute | solution.py:192
  26.7 5.6 %collective-permute-start.14 = (bf16[1312,128]{1,0:T(8,128)(2,1)S(1)}, bf16[1312,128]{1,0:T(8,128)(2,1)S(1)}, u32[]{:S(2)}, u32[]{:S(2)}) collective-permute-start(bf16[1312,128]{1,0:T(8,128)(2,1)S(1)} %collective-permute-done.8.refs_8_), channel_id=1, source_target_pairs={{0,1},{1,0},{2,3},{3,2},{4,5},{5,4},{6,7},{7,6},{8,9},{9,8},{10,11... | collective-permute-start | bytes 1007624 | tf_op jit(solution)/shard_map/ppermute | solution.py:192
  26.7 4.2 %collective-permute-start.11 = (bf16[984,128]{1,0:T(8,128)(2,1)S(1)}, bf16[984,128]{1,0:T(8,128)(2,1)S(1)}, u32[]{:S(2)}, u32[]{:S(2)}) collective-permute-start(bf16[984,128]{1,0:T(8,128)(2,1)S(1)} %pad_maximum_fusion.2), channel_id=1, source_target_pairs={{0,1},{1,0},{2,3},{3,2},{4,5},{5,4},{6,7},{7,6},{8,9},{9,8},{10,11... | collective-permute-start | bytes 755720 | tf_op jit(solution)/shard_map/ppermute | solution.py:192
  27.3 3.6 %collective-permute-start.12 = (bf16[656,128]{1,0:T(8,128)(2,1)S(1)}, bf16[656,128]{1,0:T(8,128)(2,1)S(1)}, u32[]{:S(2)}, u32[]{:S(2)}) collective-permute-start(bf16[656,128]{1,0:T(8,128)(2,1)S(1)} %collective-permute-done.7.refs_7_), channel_id=1, source_target_pairs={{0,1},{1,0},{2,3},{3,2},{4,5},{5,4},{6,7},{7,6},{8,9},{9,8},{10,11... | collective-permute-start | bytes 503816 | tf_op jit(solution)/shard_map/ppermute | solution.py:192
  30.9 1.4 %collective-permute-start.15 = (bf16[656,128]{1,0:T(8,128)(2,1)S(1)}, bf16[656,128]{1,0:T(8,128)(2,1)S(1)}, u32[]{:S(2)}, u32[]{:S(2)}) collective-permute-start(bf16[656,128]{1,0:T(8,128)(2,1)S(1)} %collective-permute-done.9.refs_9_), channel_id=1, source_target_pairs={{0,1},{1,0},{2,3},{3,2},{4,5},{5,4},{6,7},{7,6},{8,9},{9,8},{10,11... | collective-permute-start | bytes 503816 | tf_op jit(solution)/shard_map/ppermute | solution.py:192
  34.6 8.5 %collective-permute-start.16 = (bf16[328,128]{1,0:T(8,128)(2,1)S(1)}, bf16[328,128]{1,0:T(8,128)(2,1)S(1)}, u32[]{:S(2)}, u32[]{:S(2)}) collective-permute-start(bf16[328,128]{1,0:T(8,128)(2,1)S(1)} %get-tuple-element.36), channel_id=1, source_target_pairs={{0,16},{4,20},{8,24},{12,28},{16,0},{20,4},{24,8},{28,12},{1,17},{... | collective-permute-start | bytes 251912 | tf_op jit(solution)/shard_map/ppermute | solution.py:192
  35.8 7.3 %collective-permute-start.17 = (bf16[328,128]{1,0:T(8,128)(2,1)S(1)}, bf16[328,128]{1,0:T(8,128)(2,1)S(1)}, u32[]{:S(2)}, u32[]{:S(2)}) collective-permute-start(bf16[328,128]{1,0:T(8,128)(2,1)S(1)} %get-tuple-element.37), channel_id=1, source_target_pairs={{0,4},{4,0},{8,12},{12,8},{16,20},{20,16},{24,28},{28,24},{1,5},{5... | collective-permute-start | bytes 251912 | tf_op jit(solution)/shard_map/ppermute | solution.py:192
  36.3 10.8 %collective-permute-start.18 = (bf16[328,128]{1,0:T(8,128)(2,1)S(1)}, bf16[328,128]{1,0:T(8,128)(2,1)S(1)}, u32[]{:S(2)}, u32[]{:S(2)}) collective-permute-start(bf16[328,128]{1,0:T(8,128)(2,1)S(1)} %get-tuple-element.38), channel_id=1, source_target_pairs={{0,20},{4,16},{8,28},{12,24},{16,4},{20,0},{24,12},{28,8},{1,21},{... | collective-permute-start | bytes 251912 | tf_op jit(solution)/shard_map/ppermute | solution.py:192
  39.1 8.1 %collective-permute-start.19 = (bf16[328,128]{1,0:T(8,128)(2,1)S(1)}, bf16[328,128]{1,0:T(8,128)(2,1)S(1)}, u32[]{:S(2)}, u32[]{:S(2)}) collective-permute-start(bf16[328,128]{1,0:T(8,128)(2,1)S(1)} %get-tuple-element.39), channel_id=1, source_target_pairs={{0,8},{4,12},{8,0},{12,4},{16,24},{20,28},{24,16},{28,20},{1,9},{5... | collective-permute-start | bytes 251912 | tf_op jit(solution)/shard_map/ppermute | solution.py:192
  39.7 8.5 %collective-permute-start.20 = (bf16[328,128]{1,0:T(8,128)(2,1)S(1)}, bf16[328,128]{1,0:T(8,128)(2,1)S(1)}, u32[]{:S(2)}, u32[]{:S(2)}) collective-permute-start(bf16[328,128]{1,0:T(8,128)(2,1)S(1)} %get-tuple-element.40), channel_id=1, source_target_pairs={{0,24},{4,28},{8,16},{12,20},{16,8},{20,12},{24,0},{28,4},{1,25},{... | collective-permute-start | bytes 251912 | tf_op jit(solution)/shard_map/ppermute | solution.py:192
  43.1 8.0 %collective-permute-start.21 = (bf16[328,128]{1,0:T(8,128)(2,1)S(1)}, bf16[328,128]{1,0:T(8,128)(2,1)S(1)}, u32[]{:S(2)}, u32[]{:S(2)}) collective-permute-start(bf16[328,128]{1,0:T(8,128)(2,1)S(1)} %get-tuple-element.41), channel_id=1, source_target_pairs={{0,12},{4,8},{8,4},{12,0},{16,28},{20,24},{24,20},{28,16},{1,13},{... | collective-permute-start | bytes 251912 | tf_op jit(solution)/shard_map/ppermute | solution.py:192
  43.1 8.0 %collective-permute-start.22 = (bf16[328,128]{1,0:T(8,128)(2,1)S(1)}, bf16[328,128]{1,0:T(8,128)(2,1)S(1)}, u32[]{:S(2)}, u32[]{:S(2)}) collective-permute-start(bf16[328,128]{1,0:T(8,128)(2,1)S(1)} %get-tuple-element.42), channel_id=1, source_target_pairs={{0,28},{4,24},{8,20},{12,16},{16,12},{20,8},{24,4},{28,0},{1,29},{... | collective-permute-start | bytes 251912 | tf_op jit(solution)/shard_map/ppermute | solution.py:192

commit v5 on v4

--- a/solution.py
+++ b/solution.py
@@ -241,7 +241,7 @@
     second, _ = across(mid, joined)
     third, last = across([got[s] for s in late])
     held = [got[s] for s in early[:1] + [1] + near[1:2] + early[1:] + near[2:] + late] + first + second + third + [got[0]]
-    held += [partner(ready + mid[:1]), partner(mid[1:]), partner(first)]
+    held += [partner(ready + mid[:1]), partner(mid[1:] + first)]
     held += [partner([got[s] for s in late])]
     held += [partner([h]) for h in second + third]
     steps = [s for pair in zip(far, near + [0]) for s in pair]

time: 52.6 us -> 52.3 us (level)
    ppermute x23 -> x22, waiting for transfers between devices: 18.9 us -> 18.6 us  [swap(): return lax.ppermute(value, axis, [(i, i ^ step) for i in range(count)])]
    ppermute x23 -> x22, starting transfers between devices: 26.9 us -> 27.1 us  [swap(): return lax.ppermute(value, axis, [(i, i ^ step) for i in range(count)])]
  transfers between devices with their start and end apart: 23 -> 22, of which waited for: 10 -> 10; matrix products, arithmetic and copies ran while one was open for 0% -> 0% of each run, Pallas kernels for 0% -> 0%
where the time goes in v5:
time: 52.3 us; the launch traced here: 52.2 us
  starting transfers between devices  27.1 us (52%)
  waiting for transfers between devices  18.6 us (36%)
  Pallas kernels  5.72 us (11%)
  between operations  0.71 us (1%)
    ppermute x22, starting transfers between devices, swap(): return lax.ppermute(value, axis, [(i, i ^ step) for i in range(count)])  27.1 us
    ppermute x22, waiting for transfers between devices, swap(): return lax.ppermute(value, axis, [(i, i ^ step) for i in range(count)])  18.6 us
    pallas_call x1, Pallas kernels, local(): pl.pallas_call(functools.partial(smooth_kernel, groups, places, nblk), ou...  2.29 us
    pallas_call x1, Pallas kernels, local(): pl.pallas_call(functools.partial(pack_kernel, groups), out_shape=[pltpu.V...  2.11 us
    pallas_call x1, Pallas kernels, local(): pl.pallas_call(functools.partial(unpack_kernel, done, nblk), out_shape=[j...  1.32 us
  transfers between devices with their start and end apart: 22, of which 10 were waited for; matrix products, arithmetic and copies ran while one was open for 0% of the time, Pallas kernels for 0%

profile of v5, /device:TPU:0, one launch (start us, length us, event | category | flops | bytes accessed | tf_op | source)
XLA Modules:
  0.0 52.2 jit_solution(1182419874273820)
XLA Ops:
  0.6 2.1 %pack.1 = (bf16[320,256]{1,0:T(8,128)(2,1)S(1)}, bf16[328,128]{1,0:T(8,128)(2,1)S(1)}, bf16[328,128]{1,0:T(8,128)(2,1)S(1)}, bf16[328,128]{1,0:T(8,128)(2,1)S(1)...) custom-call(bf16[256,1024]{1,0:T(8,128)(2,1)} %codes_hbm.1, ...), custom_call_target="tpu_custom_call" | custom-call | tf_op jit(solution)/shard_map/pack/pallas_call | solution.py:197
  2.7 4.1 %collective-permute-start = (bf16[328,128]{1,0:T(8,128)(2,1)S(1)}, bf16[328,128]{1,0:T(8,128)(2,1)S(1)}, u32[]{:S(2)}, u32[]{:S(2)}) collective-permute-start(bf16[328,128]{1,0:T(8,128)(2,1)S(1)} %get-tuple-element.24), channel_id=1, source_target_pairs={{0,16},{4,20},{8,24},{12,28},{16,0},{20,4},{24,8},{28,12},{1,17},{... | collective-permute-start | bytes 251912 | tf_op jit(solution)/shard_map/ppermute | solution.py:192
  6.8 1.5 %collective-permute-start.1 = (bf16[328,128]{1,0:T(8,128)(2,1)S(1)}, bf16[328,128]{1,0:T(8,128)(2,1)S(1)}, u32[]{:S(2)}, u32[]{:S(2)}) collective-permute-start(bf16[328,128]{1,0:T(8,128)(2,1)S(1)} %get-tuple-element.25), channel_id=1, source_target_pairs={{0,4},{4,0},{8,12},{12,8},{16,20},{20,16},{24,28},{28,24},{1,5},{5... | collective-permute-start | bytes 251912 | tf_op jit(solution)/shard_map/ppermute | solution.py:192
  8.4 1.6 %collective-permute-start.2 = (bf16[328,128]{1,0:T(8,128)(2,1)S(1)}, bf16[328,128]{1,0:T(8,128)(2,1)S(1)}, u32[]{:S(2)}, u32[]{:S(2)}) collective-permute-start(bf16[328,128]{1,0:T(8,128)(2,1)S(1)} %get-tuple-element.26), channel_id=1, source_target_pairs={{0,8},{4,12},{8,0},{12,4},{16,24},{20,28},{24,16},{28,20},{1,9},{5... | collective-permute-start | bytes 251912 | tf_op jit(solution)/shard_map/ppermute | solution.py:192
  11.3 2.8 %collective-permute-start.4 = (bf16[328,128]{1,0:T(8,128)(2,1)S(1)}, bf16[328,128]{1,0:T(8,128)(2,1)S(1)}, u32[]{:S(2)}, u32[]{:S(2)}) collective-permute-start(bf16[328,128]{1,0:T(8,128)(2,1)S(1)} %get-tuple-element.30), channel_id=1, source_target_pairs={{0,12},{4,8},{8,4},{12,0},{16,28},{20,24},{24,20},{28,16},{1,13},{... | collective-permute-start | bytes 251912 | tf_op jit(solution)/shard_map/ppermute | solution.py:192
  14.1 1.5 %collective-permute-start.7 = (bf16[656,128]{1,0:T(8,128)(2,1)S(1)}, bf16[656,128]{1,0:T(8,128)(2,1)S(1)}, u32[]{:S(2)}, u32[]{:S(2)}) collective-permute-start(bf16[656,128]{1,0:T(8,128)(2,1)S(1)} %constant_dynamic-update-slice_fusion), channel_id=1, source_target_pairs={{0,2},{1,3},{2,0},{3,1},{4,6},{5,7},{6,4},{7,5},{8,10},{9,11},{10,... | collective-permute-start | bytes 503816 | tf_op jit(solution)/shard_map/ppermute | solution.py:192
  15.6 1.2 %collective-permute-start.5 = (bf16[328,128]{1,0:T(8,128)(2,1)S(1)}, bf16[328,128]{1,0:T(8,128)(2,1)S(1)}, u32[]{:S(2)}, u32[]{:S(2)}) collective-permute-start(bf16[328,128]{1,0:T(8,128)(2,1)S(1)} %get-tuple-element.32), channel_id=1, source_target_pairs={{0,24},{4,28},{8,16},{12,20},{16,8},{20,12},{24,0},{28,4},{1,25},{... | collective-permute-start | bytes 251912 | tf_op jit(solution)/shard_map/ppermute | solution.py:192
  16.8 2.4 %collective-permute-start.6 = (bf16[328,128]{1,0:T(8,128)(2,1)S(1)}, bf16[328,128]{1,0:T(8,128)(2,1)S(1)}, u32[]{:S(2)}, u32[]{:S(2)}) collective-permute-start(bf16[328,128]{1,0:T(8,128)(2,1)S(1)} %get-tuple-element.34), channel_id=1, source_target_pairs={{0,28},{4,24},{8,20},{12,16},{16,12},{20,8},{24,4},{28,0},{1,29},{... | collective-permute-start | bytes 251912 | tf_op jit(solution)/shard_map/ppermute | solution.py:192
  19.2 1.2 %collective-permute-start.8 = (bf16[1312,128]{1,0:T(8,128)(2,1)S(1)}, bf16[1312,128]{1,0:T(8,128)(2,1)S(1)}, u32[]{:S(2)}, u32[]{:S(2)}) collective-permute-start(bf16[1312,128]{1,0:T(8,128)(2,1)S(1)} %pad_maximum_fusion.1), channel_id=1, source_target_pairs={{0,2},{1,3},{2,0},{3,1},{4,6},{5,7},{6,4},{7,5},{8,10},{9,11},{10,... | collective-permute-start | bytes 1007624 | tf_op jit(solution)/shard_map/ppermute | solution.py:192
  20.5 1.8 %collective-permute-done.5.refs_5_ = bf16[328,128]{1,0:T(8,128)(2,1)S(1)} collective-permute-done((bf16[328,128]{1,0:T(8,128)(2,1)S(1)}, bf16[328,128]{1,0:T(8,128)(2,1)S(1)}, u32[]{:S(2)}, u32[]{:S(2)}) %collective-permute-start.5) | collective-permute-done | bytes 84000 | tf_op jit(solution)/shard_map/ppermute | solution.py:192
  22.4 1.7 %collective-permute-done.6.refs_6_ = bf16[328,128]{1,0:T(8,128)(2,1)S(1)} collective-permute-done((bf16[328,128]{1,0:T(8,128)(2,1)S(1)}, bf16[328,128]{1,0:T(8,128)(2,1)S(1)}, u32[]{:S(2)}, u32[]{:S(2)}) %collective-permute-start.6) | collective-permute-done | bytes 84000 | tf_op jit(solution)/shard_map/ppermute | solution.py:192
  24.7 2.9 %collective-permute-done.8.refs_8_ = bf16[1312,128]{1,0:T(8,128)(2,1)S(1)} collective-permute-done((bf16[1312,128]{1,0:T(8,128)(2,1)S(1)}, bf16[1312,128]{1,0:T(8,128)(2,1)S(1)}, u32[]{:S(2)}, u32[]{:S(2)}) %collective-permute-start.8) | collective-permute-done | bytes 335904 | tf_op jit(solution)/shard_map/ppermute | solution.py:192
  28.3 1.9 %collective-permute-done.9.refs_9_ = bf16[656,128]{1,0:T(8,128)(2,1)S(1)} collective-permute-done((bf16[656,128]{1,0:T(8,128)(2,1)S(1)}, bf16[656,128]{1,0:T(8,128)(2,1)S(1)}, u32[]{:S(2)}, u32[]{:S(2)}) %collective-permute-start.9) | collective-permute-done | bytes 167968 | tf_op jit(solution)/shard_map/ppermute | solution.py:192
  30.3 1.4 %collective-permute-done.14.refs_15_ = bf16[656,128]{1,0:T(8,128)(2,1)S(1)} collective-permute-done((bf16[656,128]{1,0:T(8,128)(2,1)S(1)}, bf16[656,128]{1,0:T(8,128)(2,1)S(1)}, u32[]{:S(2)}, u32[]{:S(2)}) %collective-permute-start.14) | collective-permute-done | bytes 167968 | tf_op jit(solution)/shard_map/ppermute | solution.py:192
  31.7 2.3 %smooth.1 = (bf16[328,128]{1,0:T(8,128)(2,1)S(1)}, bf16[328,128]{1,0:T(8,128)(2,1)S(1)}, bf16[328,128]{1,0:T(8,128)(2,1)S(1)}, bf16[328,128]{1,0:T(8,128)(2,1)S(...) custom-call(bf16[328,128]{1,0:T(8,128)(2,1)S(1)} %collective-permute, ...), custom_call_target="tpu_custom_call" | custom-call | tf_op jit(solution)/shard_map/smooth/pallas_call | solution.py:250
  34.0 1.2 %collective-permute-start.15 = (bf16[328,128]{1,0:T(8,128)(2,1)S(1)}, bf16[328,128]{1,0:T(8,128)(2,1)S(1)}, u32[]{:S(2)}, u32[]{:S(2)}) collective-permute-start(bf16[328,128]{1,0:T(8,128)(2,1)S(1)} %get-tuple-element.36), channel_id=1, source_target_pairs={{0,16},{4,20},{8,24},{12,28},{16,0},{20,4},{24,8},{28,12},{1,17},{... | collective-permute-start | bytes 251912 | tf_op jit(solution)/shard_map/ppermute | solution.py:192
  35.6 2.8 %collective-permute-start.17 = (bf16[328,128]{1,0:T(8,128)(2,1)S(1)}, bf16[328,128]{1,0:T(8,128)(2,1)S(1)}, u32[]{:S(2)}, u32[]{:S(2)}) collective-permute-start(bf16[328,128]{1,0:T(8,128)(2,1)S(1)} %get-tuple-element.38), channel_id=1, source_target_pairs={{0,20},{4,16},{8,28},{12,24},{16,4},{20,0},{24,12},{28,8},{1,21},{... | collective-permute-start | bytes 251912 | tf_op jit(solution)/shard_map/ppermute | solution.py:192
  38.9 2.3 %collective-permute-start.19 = (bf16[328,128]{1,0:T(8,128)(2,1)S(1)}, bf16[328,128]{1,0:T(8,128)(2,1)S(1)}, u32[]{:S(2)}, u32[]{:S(2)}) collective-permute-start(bf16[328,128]{1,0:T(8,128)(2,1)S(1)} %get-tuple-element.40), channel_id=1, source_target_pairs={{0,24},{4,28},{8,16},{12,20},{16,8},{20,12},{24,0},{28,4},{1,25},{... | collective-permute-start | bytes 251912 | tf_op jit(solution)/shard_map/ppermute | solution.py:192
  41.2 1.3 %collective-permute-done.15.refs_0_ = bf16[328,128]{1,0:T(8,128)(2,1)S(1)} collective-permute-done((bf16[328,128]{1,0:T(8,128)(2,1)S(1)}, bf16[328,128]{1,0:T(8,128)(2,1)S(1)}, u32[]{:S(2)}, u32[]{:S(2)}) %collective-permute-start.15) | collective-permute-done | bytes 84000 | tf_op jit(solution)/shard_map/ppermute | solution.py:192
  42.5 1.9 %collective-permute-start.21 = (bf16[328,128]{1,0:T(8,128)(2,1)S(1)}, bf16[328,128]{1,0:T(8,128)(2,1)S(1)}, u32[]{:S(2)}, u32[]{:S(2)}) collective-permute-start(bf16[328,128]{1,0:T(8,128)(2,1)S(1)} %get-tuple-element.42), channel_id=1, source_target_pairs={{0,28},{4,24},{8,20},{12,16},{16,12},{20,8},{24,4},{28,0},{1,29},{... | collective-permute-start | bytes 251912 | tf_op jit(solution)/shard_map/ppermute | solution.py:192
  44.4 1.9 %collective-permute-done.17.refs_2_ = bf16[328,128]{1,0:T(8,128)(2,1)S(1)} collective-permute-done((bf16[328,128]{1,0:T(8,128)(2,1)S(1)}, bf16[328,128]{1,0:T(8,128)(2,1)S(1)}, u32[]{:S(2)}, u32[]{:S(2)}) %collective-permute-start.17) | collective-permute-done | bytes 84000 | tf_op jit(solution)/shard_map/ppermute | solution.py:192
  46.3 1.8 %collective-permute-done.19.refs_4_ = bf16[328,128]{1,0:T(8,128)(2,1)S(1)} collective-permute-done((bf16[328,128]{1,0:T(8,128)(2,1)S(1)}, bf16[328,128]{1,0:T(8,128)(2,1)S(1)}, u32[]{:S(2)}, u32[]{:S(2)}) %collective-permute-start.19) | collective-permute-done | bytes 84000 | tf_op jit(solution)/shard_map/ppermute | solution.py:192
  48.1 2.8 %collective-permute-done.20.refs_5_ = bf16[328,128]{1,0:T(8,128)(2,1)S(1)} collective-permute-done((bf16[328,128]{1,0:T(8,128)(2,1)S(1)}, bf16[328,128]{1,0:T(8,128)(2,1)S(1)}, u32[]{:S(2)}, u32[]{:S(2)}) %collective-permute-start.20) | collective-permute-done | bytes 84000 | tf_op jit(solution)/shard_map/ppermute | solution.py:192
  50.8 1.3 %unpack.1 = (bf16[256,1024]{1,0:T(8,128)(2,1)}, bf16[256]{0:T(256)(128)(2,1)}) custom-call(bf16[320,256]{1,0:T(8,128)(2,1)S(1)} %get-tuple-element.23.select_ref, bf16[328,128]{1,0:T(8,128)(2,1)S(1)} %collective-permute-done.15.refs_0_, bf16[328,128]{1,0:T(8,128)(2,1)S(1)} %collective-permute-done.16.refs_1_, ...), custom_call_target="tpu_custom_call" | custom-call | tf_op jit(solution)/shard_map/unpack/pallas_call | solution.py:265
  (30 shorter events, 3.8 us)
Async XLA Ops:
  2.7 12.9 %collective-permute-start = (bf16[328,128]{1,0:T(8,128)(2,1)S(1)}, bf16[328,128]{1,0:T(8,128)(2,1)S(1)}, u32[]{:S(2)}, u32[]{:S(2)}) collective-permute-start(bf16[328,128]{1,0:T(8,128)(2,1)S(1)} %get-tuple-element.24), channel_id=1, source_target_pairs={{0,16},{4,20},{8,24},{12,28},{16,0},{20,4},{24,8},{28,12},{1,17},{... | collective-permute-start | bytes 251912 | tf_op jit(solution)/shard_map/ppermute | solution.py:192
  6.8 4.5 %collective-permute-start.1 = (bf16[328,128]{1,0:T(8,128)(2,1)S(1)}, bf16[328,128]{1,0:T(8,128)(2,1)S(1)}, u32[]{:S(2)}, u32[]{:S(2)}) collective-permute-start(bf16[328,128]{1,0:T(8,128)(2,1)S(1)} %get-tuple-element.25), channel_id=1, source_target_pairs={{0,4},{4,0},{8,12},{12,8},{16,20},{20,16},{24,28},{28,24},{1,5},{5... | collective-permute-start | bytes 251912 | tf_op jit(solution)/shard_map/ppermute | solution.py:192
  8.4 8.5 %collective-permute-start.2 = (bf16[328,128]{1,0:T(8,128)(2,1)S(1)}, bf16[328,128]{1,0:T(8,128)(2,1)S(1)}, u32[]{:S(2)}, u32[]{:S(2)}) collective-permute-start(bf16[328,128]{1,0:T(8,128)(2,1)S(1)} %get-tuple-element.26), channel_id=1, source_target_pairs={{0,8},{4,12},{8,0},{12,4},{16,24},{20,28},{24,16},{28,20},{1,9},{5... | collective-permute-start | bytes 251912 | tf_op jit(solution)/shard_map/ppermute | solution.py:192
  9.9 9.3 %collective-permute-start.3 = (bf16[328,128]{1,0:T(8,128)(2,1)S(1)}, bf16[328,128]{1,0:T(8,128)(2,1)S(1)}, u32[]{:S(2)}, u32[]{:S(2)}) collective-permute-start(bf16[328,128]{1,0:T(8,128)(2,1)S(1)} %get-tuple-element.27), channel_id=1, source_target_pairs={{0,20},{4,16},{8,28},{12,24},{16,4},{20,0},{24,12},{28,8},{1,21},{... | collective-permute-start | bytes 251912 | tf_op jit(solution)/shard_map/ppermute | solution.py:192
  11.3 7.9 %collective-permute-start.4 = (bf16[328,128]{1,0:T(8,128)(2,1)S(1)}, bf16[328,128]{1,0:T(8,128)(2,1)S(1)}, u32[]{:S(2)}, u32[]{:S(2)}) collective-permute-start(bf16[328,128]{1,0:T(8,128)(2,1)S(1)} %get-tuple-element.30), channel_id=1, source_target_pairs={{0,12},{4,8},{8,4},{12,0},{16,28},{20,24},{24,20},{28,16},{1,13},{... | collective-permute-start | bytes 251912 | tf_op jit(solution)/shard_map/ppermute | solution.py:192
  14.1 8.2 %collective-permute-start.7 = (bf16[656,128]{1,0:T(8,128)(2,1)S(1)}, bf16[656,128]{1,0:T(8,128)(2,1)S(1)}, u32[]{:S(2)}, u32[]{:S(2)}) collective-permute-start(bf16[656,128]{1,0:T(8,128)(2,1)S(1)} %constant_dynamic-update-slice_fusion), channel_id=1, source_target_pairs={{0,2},{1,3},{2,0},{3,1},{4,6},{5,7},{6,4},{7,5},{8,10},{9,11},{10,... | collective-permute-start | bytes 503816 | tf_op jit(solution)/shard_map/ppermute | solution.py:192
  15.6 6.7 %collective-permute-start.5 = (bf16[328,128]{1,0:T(8,128)(2,1)S(1)}, bf16[328,128]{1,0:T(8,128)(2,1)S(1)}, u32[]{:S(2)}, u32[]{:S(2)}) collective-permute-start(bf16[328,128]{1,0:T(8,128)(2,1)S(1)} %get-tuple-element.32), channel_id=1, source_target_pairs={{0,24},{4,28},{8,16},{12,20},{16,8},{20,12},{24,0},{28,4},{1,25},{... | collective-permute-start | bytes 251912 | tf_op jit(solution)/shard_map/ppermute | solution.py:192
  16.8 7.3 %collective-permute-start.6 = (bf16[328,128]{1,0:T(8,128)(2,1)S(1)}, bf16[328,128]{1,0:T(8,128)(2,1)S(1)}, u32[]{:S(2)}, u32[]{:S(2)}) collective-permute-start(bf16[328,128]{1,0:T(8,128)(2,1)S(1)} %get-tuple-element.34), channel_id=1, source_target_pairs={{0,28},{4,24},{8,20},{12,16},{16,12},{20,8},{24,4},{28,0},{1,29},{... | collective-permute-start | bytes 251912 | tf_op jit(solution)/shard_map/ppermute | solution.py:192
  19.2 8.4 %collective-permute-start.8 = (bf16[1312,128]{1,0:T(8,128)(2,1)S(1)}, bf16[1312,128]{1,0:T(8,128)(2,1)S(1)}, u32[]{:S(2)}, u32[]{:S(2)}) collective-permute-start(bf16[1312,128]{1,0:T(8,128)(2,1)S(1)} %pad_maximum_fusion.1), channel_id=1, source_target_pairs={{0,2},{1,3},{2,0},{3,1},{4,6},{5,7},{6,4},{7,5},{8,10},{9,11},{10,... | collective-permute-start | bytes 1007624 | tf_op jit(solution)/shard_map/ppermute | solution.py:192
  22.3 9.3 %collective-permute-start.11 = (bf16[1640,128]{1,0:T(8,128)(2,1)S(1)}, bf16[1640,128]{1,0:T(8,128)(2,1)S(1)}, u32[]{:S(2)}, u32[]{:S(2)}) collective-permute-start(bf16[1640,128]{1,0:T(8,128)(2,1)S(1)} %pad_maximum_fusion), channel_id=1, source_target_pairs={{0,1},{1,0},{2,3},{3,2},{4,5},{5,4},{6,7},{7,6},{8,9},{9,8},{10,11... | collective-permute-start | bytes 1259528 | tf_op jit(solution)/shard_map/ppermute | solution.py:192
  24.1 6.2 %collective-permute-start.9 = (bf16[656,128]{1,0:T(8,128)(2,1)S(1)}, bf16[656,128]{1,0:T(8,128)(2,1)S(1)}, u32[]{:S(2)}, u32[]{:S(2)}) collective-permute-start(bf16[656,128]{1,0:T(8,128)(2,1)S(1)} %constant_dynamic-update-slice_fusion.2), channel_id=1, source_target_pairs={{0,2},{1,3},{2,0},{3,1},{4,6},{5,7},{6,4},{7,5},{8,10},{9,11},{10,... | collective-permute-start | bytes 503816 | tf_op jit(solution)/shard_map/ppermute | solution.py:192
  27.7 4.0 %collective-permute-start.13 = (bf16[1312,128]{1,0:T(8,128)(2,1)S(1)}, bf16[1312,128]{1,0:T(8,128)(2,1)S(1)}, u32[]{:S(2)}, u32[]{:S(2)}) collective-permute-start(bf16[1312,128]{1,0:T(8,128)(2,1)S(1)} %collective-permute-done.8.refs_8_), channel_id=1, source_target_pairs={{0,1},{1,0},{2,3},{3,2},{4,5},{5,4},{6,7},{7,6},{8,9},{9,8},{10,11... | collective-permute-start | bytes 1007624 | tf_op jit(solution)/shard_map/ppermute | solution.py:192
  27.7 2.6 %collective-permute-start.10 = (bf16[984,128]{1,0:T(8,128)(2,1)S(1)}, bf16[984,128]{1,0:T(8,128)(2,1)S(1)}, u32[]{:S(2)}, u32[]{:S(2)}) collective-permute-start(bf16[984,128]{1,0:T(8,128)(2,1)S(1)} %pad_maximum_fusion.2), channel_id=1, source_target_pairs={{0,1},{1,0},{2,3},{3,2},{4,5},{5,4},{6,7},{7,6},{8,9},{9,8},{10,11... | collective-permute-start | bytes 755720 | tf_op jit(solution)/shard_map/ppermute | solution.py:192
  28.3 2.0 %collective-permute-start.12 = (bf16[656,128]{1,0:T(8,128)(2,1)S(1)}, bf16[656,128]{1,0:T(8,128)(2,1)S(1)}, u32[]{:S(2)}, u32[]{:S(2)}) collective-permute-start(bf16[656,128]{1,0:T(8,128)(2,1)S(1)} %constant_dynamic-update-slice_fusion.2), channel_id=1, source_target_pairs={{0,1},{1,0},{2,3},{3,2},{4,5},{5,4},{6,7},{7,6},{8,9},{9,8},{10,11... | collective-permute-start | bytes 503816 | tf_op jit(solution)/shard_map/ppermute | solution.py:192
  30.3 1.4 %collective-permute-start.14 = (bf16[656,128]{1,0:T(8,128)(2,1)S(1)}, bf16[656,128]{1,0:T(8,128)(2,1)S(1)}, u32[]{:S(2)}, u32[]{:S(2)}) collective-permute-start(bf16[656,128]{1,0:T(8,128)(2,1)S(1)} %collective-permute-done.9.refs_9_), channel_id=1, source_target_pairs={{0,1},{1,0},{2,3},{3,2},{4,5},{5,4},{6,7},{7,6},{8,9},{9,8},{10,11... | collective-permute-start | bytes 503816 | tf_op jit(solution)/shard_map/ppermute | solution.py:192
  34.0 8.5 %collective-permute-start.15 = (bf16[328,128]{1,0:T(8,128)(2,1)S(1)}, bf16[328,128]{1,0:T(8,128)(2,1)S(1)}, u32[]{:S(2)}, u32[]{:S(2)}) collective-permute-start(bf16[328,128]{1,0:T(8,128)(2,1)S(1)} %get-tuple-element.36), channel_id=1, source_target_pairs={{0,16},{4,20},{8,24},{12,28},{16,0},{20,4},{24,8},{28,12},{1,17},{... | collective-permute-start | bytes 251912 | tf_op jit(solution)/shard_map/ppermute | solution.py:192
  35.2 7.3 %collective-permute-start.16 = (bf16[328,128]{1,0:T(8,128)(2,1)S(1)}, bf16[328,128]{1,0:T(8,128)(2,1)S(1)}, u32[]{:S(2)}, u32[]{:S(2)}) collective-permute-start(bf16[328,128]{1,0:T(8,128)(2,1)S(1)} %get-tuple-element.37), channel_id=1, source_target_pairs={{0,4},{4,0},{8,12},{12,8},{16,20},{20,16},{24,28},{28,24},{1,5},{5... | collective-permute-start | bytes 251912 | tf_op jit(solution)/shard_map/ppermute | solution.py:192
  35.6 10.7 %collective-permute-start.17 = (bf16[328,128]{1,0:T(8,128)(2,1)S(1)}, bf16[328,128]{1,0:T(8,128)(2,1)S(1)}, u32[]{:S(2)}, u32[]{:S(2)}) collective-permute-start(bf16[328,128]{1,0:T(8,128)(2,1)S(1)} %get-tuple-element.38), channel_id=1, source_target_pairs={{0,20},{4,16},{8,28},{12,24},{16,4},{20,0},{24,12},{28,8},{1,21},{... | collective-permute-start | bytes 251912 | tf_op jit(solution)/shard_map/ppermute | solution.py:192
  38.4 7.9 %collective-permute-start.18 = (bf16[328,128]{1,0:T(8,128)(2,1)S(1)}, bf16[328,128]{1,0:T(8,128)(2,1)S(1)}, u32[]{:S(2)}, u32[]{:S(2)}) collective-permute-start(bf16[328,128]{1,0:T(8,128)(2,1)S(1)} %get-tuple-element.39), channel_id=1, source_target_pairs={{0,8},{4,12},{8,0},{12,4},{16,24},{20,28},{24,16},{28,20},{1,9},{5... | collective-permute-start | bytes 251912 | tf_op jit(solution)/shard_map/ppermute | solution.py:192
  38.9 9.2 %collective-permute-start.19 = (bf16[328,128]{1,0:T(8,128)(2,1)S(1)}, bf16[328,128]{1,0:T(8,128)(2,1)S(1)}, u32[]{:S(2)}, u32[]{:S(2)}) collective-permute-start(bf16[328,128]{1,0:T(8,128)(2,1)S(1)} %get-tuple-element.40), channel_id=1, source_target_pairs={{0,24},{4,28},{8,16},{12,20},{16,8},{20,12},{24,0},{28,4},{1,25},{... | collective-permute-start | bytes 251912 | tf_op jit(solution)/shard_map/ppermute | solution.py:192
  42.5 8.4 %collective-permute-start.20 = (bf16[328,128]{1,0:T(8,128)(2,1)S(1)}, bf16[328,128]{1,0:T(8,128)(2,1)S(1)}, u32[]{:S(2)}, u32[]{:S(2)}) collective-permute-start(bf16[328,128]{1,0:T(8,128)(2,1)S(1)} %get-tuple-element.41), channel_id=1, source_target_pairs={{0,12},{4,8},{8,4},{12,0},{16,28},{20,24},{24,20},{28,16},{1,13},{... | collective-permute-start | bytes 251912 | tf_op jit(solution)/shard_map/ppermute | solution.py:192
  42.5 8.3 %collective-permute-start.21 = (bf16[328,128]{1,0:T(8,128)(2,1)S(1)}, bf16[328,128]{1,0:T(8,128)(2,1)S(1)}, u32[]{:S(2)}, u32[]{:S(2)}) collective-permute-start(bf16[328,128]{1,0:T(8,128)(2,1)S(1)} %get-tuple-element.42), channel_id=1, source_target_pairs={{0,28},{4,24},{8,20},{12,16},{16,12},{20,8},{24,4},{28,0},{1,29},{... | collective-permute-start | bytes 251912 | tf_op jit(solution)/shard_map/ppermute | solution.py:192

commit v6 on v5

--- a/solution.py
+++ b/solution.py
@@ -186,6 +186,7 @@
     piece = pltpu.VMEM((size, LANES), jnp.bfloat16)
     half, sides = groups // 2, members // 2
     near, far = list(range(1, half)), list(range(half, groups))
+    far = far[:-2] + far[:-3:-1]
 
     def swap(value, axis, step):
         count = lax.axis_size(axis)

time: 52.3 us -> 52.1 us (level)
  no operation moved by 1% of the time
where the time goes in v6:
time: 52.1 us; the launch traced here: 51.9 us
  starting transfers between devices  26.9 us (52%)
  waiting for transfers between devices  18.5 us (36%)
  Pallas kernels  5.71 us (11%)
  between operations  0.71 us (1%)
    ppermute x22, starting transfers between devices, swap(): return lax.ppermute(value, axis, [(i, i ^ step) for i in range(count)])  26.9 us
    ppermute x22, waiting for transfers between devices, swap(): return lax.ppermute(value, axis, [(i, i ^ step) for i in range(count)])  18.5 us
    pallas_call x1, Pallas kernels, local(): pl.pallas_call(functools.partial(smooth_kernel, groups, places, nblk), ou...  2.29 us
    pallas_call x1, Pallas kernels, local(): pl.pallas_call(functools.partial(pack_kernel, groups), out_shape=[pltpu.V...  2.11 us
    pallas_call x1, Pallas kernels, local(): pl.pallas_call(functools.partial(unpack_kernel, done, nblk), out_shape=[j...  1.32 us
  transfers between devices with their start and end apart: 22, of which 10 were waited for; matrix products, arithmetic and copies ran while one was open for 0% of the time, Pallas kernels for 0%

profile of v6, /device:TPU:0, one launch (start us, length us, event | category | flops | bytes accessed | tf_op | source)
XLA Modules:
  0.0 51.9 jit_solution(5578339475946453058)
XLA Ops:
  0.6 2.1 %pack.1 = (bf16[320,256]{1,0:T(8,128)(2,1)S(1)}, bf16[328,128]{1,0:T(8,128)(2,1)S(1)}, bf16[328,128]{1,0:T(8,128)(2,1)S(1)}, bf16[328,128]{1,0:T(8,128)(2,1)S(1)...) custom-call(bf16[256,1024]{1,0:T(8,128)(2,1)} %codes_hbm.1, ...), custom_call_target="tpu_custom_call" | custom-call | tf_op jit(solution)/shard_map/pack/pallas_call | solution.py:198
  2.7 4.1 %collective-permute-start = (bf16[328,128]{1,0:T(8,128)(2,1)S(1)}, bf16[328,128]{1,0:T(8,128)(2,1)S(1)}, u32[]{:S(2)}, u32[]{:S(2)}) collective-permute-start(bf16[328,128]{1,0:T(8,128)(2,1)S(1)} %get-tuple-element.24), channel_id=1, source_target_pairs={{0,16},{4,20},{8,24},{12,28},{16,0},{20,4},{24,8},{28,12},{1,17},{... | collective-permute-start | bytes 251912 | tf_op jit(solution)/shard_map/ppermute | solution.py:193
  6.8 1.5 %collective-permute-start.1 = (bf16[328,128]{1,0:T(8,128)(2,1)S(1)}, bf16[328,128]{1,0:T(8,128)(2,1)S(1)}, u32[]{:S(2)}, u32[]{:S(2)}) collective-permute-start(bf16[328,128]{1,0:T(8,128)(2,1)S(1)} %get-tuple-element.25), channel_id=1, source_target_pairs={{0,4},{4,0},{8,12},{12,8},{16,20},{20,16},{24,28},{28,24},{1,5},{5... | collective-permute-start | bytes 251912 | tf_op jit(solution)/shard_map/ppermute | solution.py:193
  8.4 1.6 %collective-permute-start.2 = (bf16[328,128]{1,0:T(8,128)(2,1)S(1)}, bf16[328,128]{1,0:T(8,128)(2,1)S(1)}, u32[]{:S(2)}, u32[]{:S(2)}) collective-permute-start(bf16[328,128]{1,0:T(8,128)(2,1)S(1)} %get-tuple-element.26), channel_id=1, source_target_pairs={{0,8},{4,12},{8,0},{12,4},{16,24},{20,28},{24,16},{28,20},{1,9},{5... | collective-permute-start | bytes 251912 | tf_op jit(solution)/shard_map/ppermute | solution.py:193
  10.2 1.1 %collective-permute-done.1.refs_1_ = bf16[328,128]{1,0:T(8,128)(2,1)S(1)} collective-permute-done((bf16[328,128]{1,0:T(8,128)(2,1)S(1)}, bf16[328,128]{1,0:T(8,128)(2,1)S(1)}, u32[]{:S(2)}, u32[]{:S(2)}) %collective-permute-start.1) | collective-permute-done | bytes 84000 | tf_op jit(solution)/shard_map/ppermute | solution.py:193
  11.3 2.8 %collective-permute-start.4 = (bf16[328,128]{1,0:T(8,128)(2,1)S(1)}, bf16[328,128]{1,0:T(8,128)(2,1)S(1)}, u32[]{:S(2)}, u32[]{:S(2)}) collective-permute-start(bf16[328,128]{1,0:T(8,128)(2,1)S(1)} %get-tuple-element.30), channel_id=1, source_target_pairs={{0,12},{4,8},{8,4},{12,0},{16,28},{20,24},{24,20},{28,16},{1,13},{... | collective-permute-start | bytes 251912 | tf_op jit(solution)/shard_map/ppermute | solution.py:193
  14.1 1.5 %collective-permute-start.7 = (bf16[656,128]{1,0:T(8,128)(2,1)S(1)}, bf16[656,128]{1,0:T(8,128)(2,1)S(1)}, u32[]{:S(2)}, u32[]{:S(2)}) collective-permute-start(bf16[656,128]{1,0:T(8,128)(2,1)S(1)} %constant_dynamic-update-slice_fusion), channel_id=1, source_target_pairs={{0,2},{1,3},{2,0},{3,1},{4,6},{5,7},{6,4},{7,5},{8,10},{9,11},{10,... | collective-permute-start | bytes 503816 | tf_op jit(solution)/shard_map/ppermute | solution.py:193
  15.6 1.2 %collective-permute-start.5 = (bf16[328,128]{1,0:T(8,128)(2,1)S(1)}, bf16[328,128]{1,0:T(8,128)(2,1)S(1)}, u32[]{:S(2)}, u32[]{:S(2)}) collective-permute-start(bf16[328,128]{1,0:T(8,128)(2,1)S(1)} %get-tuple-element.32), channel_id=1, source_target_pairs={{0,28},{4,24},{8,20},{12,16},{16,12},{20,8},{24,4},{28,0},{1,29},{... | collective-permute-start | bytes 251912 | tf_op jit(solution)/shard_map/ppermute | solution.py:193
  16.8 2.4 %collective-permute-start.6 = (bf16[328,128]{1,0:T(8,128)(2,1)S(1)}, bf16[328,128]{1,0:T(8,128)(2,1)S(1)}, u32[]{:S(2)}, u32[]{:S(2)}) collective-permute-start(bf16[328,128]{1,0:T(8,128)(2,1)S(1)} %get-tuple-element.34), channel_id=1, source_target_pairs={{0,24},{4,28},{8,16},{12,20},{16,8},{20,12},{24,0},{28,4},{1,25},{... | collective-permute-start | bytes 251912 | tf_op jit(solution)/shard_map/ppermute | solution.py:193
  19.8 3.0 %collective-permute-done.5.refs_5_ = bf16[328,128]{1,0:T(8,128)(2,1)S(1)} collective-permute-done((bf16[328,128]{1,0:T(8,128)(2,1)S(1)}, bf16[328,128]{1,0:T(8,128)(2,1)S(1)}, u32[]{:S(2)}, u32[]{:S(2)}) %collective-permute-start.5) | collective-permute-done | bytes 84000 | tf_op jit(solution)/shard_map/ppermute | solution.py:193
  23.2 1.5 %collective-permute-start.9 = (bf16[656,128]{1,0:T(8,128)(2,1)S(1)}, bf16[656,128]{1,0:T(8,128)(2,1)S(1)}, u32[]{:S(2)}, u32[]{:S(2)}) collective-permute-start(bf16[656,128]{1,0:T(8,128)(2,1)S(1)} %constant_dynamic-update-slice_fusion.2), channel_id=1, source_target_pairs={{0,2},{1,3},{2,0},{3,1},{4,6},{5,7},{6,4},{7,5},{8,10},{9,11},{10,... | collective-permute-start | bytes 503816 | tf_op jit(solution)/shard_map/ppermute | solution.py:193
  24.7 2.5 %collective-permute-done.8.refs_8_ = bf16[1312,128]{1,0:T(8,128)(2,1)S(1)} collective-permute-done((bf16[1312,128]{1,0:T(8,128)(2,1)S(1)}, bf16[1312,128]{1,0:T(8,128)(2,1)S(1)}, u32[]{:S(2)}, u32[]{:S(2)}) %collective-permute-start.8) | collective-permute-done | bytes 335904 | tf_op jit(solution)/shard_map/ppermute | solution.py:193
  27.8 2.4 %collective-permute-done.9.refs_9_ = bf16[656,128]{1,0:T(8,128)(2,1)S(1)} collective-permute-done((bf16[656,128]{1,0:T(8,128)(2,1)S(1)}, bf16[656,128]{1,0:T(8,128)(2,1)S(1)}, u32[]{:S(2)}, u32[]{:S(2)}) %collective-permute-start.9) | collective-permute-done | bytes 167968 | tf_op jit(solution)/shard_map/ppermute | solution.py:193
  30.3 1.4 %collective-permute-done.14.refs_15_ = bf16[656,128]{1,0:T(8,128)(2,1)S(1)} collective-permute-done((bf16[656,128]{1,0:T(8,128)(2,1)S(1)}, bf16[656,128]{1,0:T(8,128)(2,1)S(1)}, u32[]{:S(2)}, u32[]{:S(2)}) %collective-permute-start.14) | collective-permute-done | bytes 167968 | tf_op jit(solution)/shard_map/ppermute | solution.py:193
  31.7 2.3 %smooth.1 = (bf16[328,128]{1,0:T(8,128)(2,1)S(1)}, bf16[328,128]{1,0:T(8,128)(2,1)S(1)}, bf16[328,128]{1,0:T(8,128)(2,1)S(1)}, bf16[328,128]{1,0:T(8,128)(2,1)S(...) custom-call(bf16[328,128]{1,0:T(8,128)(2,1)S(1)} %collective-permute, ...), custom_call_target="tpu_custom_call" | custom-call | tf_op jit(solution)/shard_map/smooth/pallas_call | solution.py:251
  34.4 1.2 %collective-permute-start.16 = (bf16[328,128]{1,0:T(8,128)(2,1)S(1)}, bf16[328,128]{1,0:T(8,128)(2,1)S(1)}, u32[]{:S(2)}, u32[]{:S(2)}) collective-permute-start(bf16[328,128]{1,0:T(8,128)(2,1)S(1)} %get-tuple-element.37), channel_id=1, source_target_pairs={{0,4},{4,0},{8,12},{12,8},{16,20},{20,16},{24,28},{28,24},{1,5},{5... | collective-permute-start | bytes 251912 | tf_op jit(solution)/shard_map/ppermute | solution.py:193
  35.6 2.8 %collective-permute-start.17 = (bf16[328,128]{1,0:T(8,128)(2,1)S(1)}, bf16[328,128]{1,0:T(8,128)(2,1)S(1)}, u32[]{:S(2)}, u32[]{:S(2)}) collective-permute-start(bf16[328,128]{1,0:T(8,128)(2,1)S(1)} %get-tuple-element.38), channel_id=1, source_target_pairs={{0,20},{4,16},{8,28},{12,24},{16,4},{20,0},{24,12},{28,8},{1,21},{... | collective-permute-start | bytes 251912 | tf_op jit(solution)/shard_map/ppermute | solution.py:193
  38.9 2.0 %collective-permute-start.19 = (bf16[328,128]{1,0:T(8,128)(2,1)S(1)}, bf16[328,128]{1,0:T(8,128)(2,1)S(1)}, u32[]{:S(2)}, u32[]{:S(2)}) collective-permute-start(bf16[328,128]{1,0:T(8,128)(2,1)S(1)} %get-tuple-element.40), channel_id=1, source_target_pairs={{0,28},{4,24},{8,20},{12,16},{16,12},{20,8},{24,4},{28,0},{1,29},{... | collective-permute-start | bytes 251912 | tf_op jit(solution)/shard_map/ppermute | solution.py:193
  40.9 1.6 %collective-permute-done.15.refs_0_ = bf16[328,128]{1,0:T(8,128)(2,1)S(1)} collective-permute-done((bf16[328,128]{1,0:T(8,128)(2,1)S(1)}, bf16[328,128]{1,0:T(8,128)(2,1)S(1)}, u32[]{:S(2)}, u32[]{:S(2)}) %collective-permute-start.15) | collective-permute-done | bytes 84000 | tf_op jit(solution)/shard_map/ppermute | solution.py:193
  43.2 1.0 %collective-permute-start.21 = (bf16[328,128]{1,0:T(8,128)(2,1)S(1)}, bf16[328,128]{1,0:T(8,128)(2,1)S(1)}, u32[]{:S(2)}, u32[]{:S(2)}) collective-permute-start(bf16[328,128]{1,0:T(8,128)(2,1)S(1)} %get-tuple-element.42), channel_id=1, source_target_pairs={{0,24},{4,28},{8,16},{12,20},{16,8},{20,12},{24,0},{28,4},{1,25},{... | collective-permute-start | bytes 251912 | tf_op jit(solution)/shard_map/ppermute | solution.py:193
  44.3 1.7 %collective-permute-done.17.refs_2_ = bf16[328,128]{1,0:T(8,128)(2,1)S(1)} collective-permute-done((bf16[328,128]{1,0:T(8,128)(2,1)S(1)}, bf16[328,128]{1,0:T(8,128)(2,1)S(1)}, u32[]{:S(2)}, u32[]{:S(2)}) %collective-permute-start.17) | collective-permute-done | bytes 84000 | tf_op jit(solution)/shard_map/ppermute | solution.py:193
  46.0 1.7 %collective-permute-done.19.refs_4_ = bf16[328,128]{1,0:T(8,128)(2,1)S(1)} collective-permute-done((bf16[328,128]{1,0:T(8,128)(2,1)S(1)}, bf16[328,128]{1,0:T(8,128)(2,1)S(1)}, u32[]{:S(2)}, u32[]{:S(2)}) %collective-permute-start.19) | collective-permute-done | bytes 84000 | tf_op jit(solution)/shard_map/ppermute | solution.py:193
  47.7 2.9 %collective-permute-done.20.refs_5_ = bf16[328,128]{1,0:T(8,128)(2,1)S(1)} collective-permute-done((bf16[328,128]{1,0:T(8,128)(2,1)S(1)}, bf16[328,128]{1,0:T(8,128)(2,1)S(1)}, u32[]{:S(2)}, u32[]{:S(2)}) %collective-permute-start.20) | collective-permute-done | bytes 84000 | tf_op jit(solution)/shard_map/ppermute | solution.py:193
  50.6 1.3 %unpack.1 = (bf16[256,1024]{1,0:T(8,128)(2,1)}, bf16[256]{0:T(256)(128)(2,1)}) custom-call(bf16[320,256]{1,0:T(8,128)(2,1)S(1)} %get-tuple-element.23.select_ref, bf16[328,128]{1,0:T(8,128)(2,1)S(1)} %collective-permute-done.15.refs_0_, bf16[328,128]{1,0:T(8,128)(2,1)S(1)} %collective-permute-done.16.refs_1_, ...), custom_call_target="tpu_custom_call" | custom-call | tf_op jit(solution)/shard_map/unpack/pallas_call | solution.py:266
  (30 shorter events, 3.6 us)
Async XLA Ops:
  2.7 12.9 %collective-permute-start = (bf16[328,128]{1,0:T(8,128)(2,1)S(1)}, bf16[328,128]{1,0:T(8,128)(2,1)S(1)}, u32[]{:S(2)}, u32[]{:S(2)}) collective-permute-start(bf16[328,128]{1,0:T(8,128)(2,1)S(1)} %get-tuple-element.24), channel_id=1, source_target_pairs={{0,16},{4,20},{8,24},{12,28},{16,0},{20,4},{24,8},{28,12},{1,17},{... | collective-permute-start | bytes 251912 | tf_op jit(solution)/shard_map/ppermute | solution.py:193
  6.8 4.5 %collective-permute-start.1 = (bf16[328,128]{1,0:T(8,128)(2,1)S(1)}, bf16[328,128]{1,0:T(8,128)(2,1)S(1)}, u32[]{:S(2)}, u32[]{:S(2)}) collective-permute-start(bf16[328,128]{1,0:T(8,128)(2,1)S(1)} %get-tuple-element.25), channel_id=1, source_target_pairs={{0,4},{4,0},{8,12},{12,8},{16,20},{20,16},{24,28},{28,24},{1,5},{5... | collective-permute-start | bytes 251912 | tf_op jit(solution)/shard_map/ppermute | solution.py:193
  8.4 8.4 %collective-permute-start.2 = (bf16[328,128]{1,0:T(8,128)(2,1)S(1)}, bf16[328,128]{1,0:T(8,128)(2,1)S(1)}, u32[]{:S(2)}, u32[]{:S(2)}) collective-permute-start(bf16[328,128]{1,0:T(8,128)(2,1)S(1)} %get-tuple-element.26), channel_id=1, source_target_pairs={{0,8},{4,12},{8,0},{12,4},{16,24},{20,28},{24,16},{28,20},{1,9},{5... | collective-permute-start | bytes 251912 | tf_op jit(solution)/shard_map/ppermute | solution.py:193
  9.9 9.3 %collective-permute-start.3 = (bf16[328,128]{1,0:T(8,128)(2,1)S(1)}, bf16[328,128]{1,0:T(8,128)(2,1)S(1)}, u32[]{:S(2)}, u32[]{:S(2)}) collective-permute-start(bf16[328,128]{1,0:T(8,128)(2,1)S(1)} %get-tuple-element.27), channel_id=1, source_target_pairs={{0,20},{4,16},{8,28},{12,24},{16,4},{20,0},{24,12},{28,8},{1,21},{... | collective-permute-start | bytes 251912 | tf_op jit(solution)/shard_map/ppermute | solution.py:193
  11.3 7.9 %collective-permute-start.4 = (bf16[328,128]{1,0:T(8,128)(2,1)S(1)}, bf16[328,128]{1,0:T(8,128)(2,1)S(1)}, u32[]{:S(2)}, u32[]{:S(2)}) collective-permute-start(bf16[328,128]{1,0:T(8,128)(2,1)S(1)} %get-tuple-element.30), channel_id=1, source_target_pairs={{0,12},{4,8},{8,4},{12,0},{16,28},{20,24},{24,20},{28,16},{1,13},{... | collective-permute-start | bytes 251912 | tf_op jit(solution)/shard_map/ppermute | solution.py:193
  14.1 8.8 %collective-permute-start.7 = (bf16[656,128]{1,0:T(8,128)(2,1)S(1)}, bf16[656,128]{1,0:T(8,128)(2,1)S(1)}, u32[]{:S(2)}, u32[]{:S(2)}) collective-permute-start(bf16[656,128]{1,0:T(8,128)(2,1)S(1)} %constant_dynamic-update-slice_fusion), channel_id=1, source_target_pairs={{0,2},{1,3},{2,0},{3,1},{4,6},{5,7},{6,4},{7,5},{8,10},{9,11},{10,... | collective-permute-start | bytes 503816 | tf_op jit(solution)/shard_map/ppermute | solution.py:193
  15.6 7.3 %collective-permute-start.5 = (bf16[328,128]{1,0:T(8,128)(2,1)S(1)}, bf16[328,128]{1,0:T(8,128)(2,1)S(1)}, u32[]{:S(2)}, u32[]{:S(2)}) collective-permute-start(bf16[328,128]{1,0:T(8,128)(2,1)S(1)} %get-tuple-element.32), channel_id=1, source_target_pairs={{0,28},{4,24},{8,20},{12,16},{16,12},{20,8},{24,4},{28,0},{1,29},{... | collective-permute-start | bytes 251912 | tf_op jit(solution)/shard_map/ppermute | solution.py:193
  16.8 6.4 %collective-permute-start.6 = (bf16[328,128]{1,0:T(8,128)(2,1)S(1)}, bf16[328,128]{1,0:T(8,128)(2,1)S(1)}, u32[]{:S(2)}, u32[]{:S(2)}) collective-permute-start(bf16[328,128]{1,0:T(8,128)(2,1)S(1)} %get-tuple-element.34), channel_id=1, source_target_pairs={{0,24},{4,28},{8,16},{12,20},{16,8},{20,12},{24,0},{28,4},{1,25},{... | collective-permute-start | bytes 251912 | tf_op jit(solution)/shard_map/ppermute | solution.py:193
  19.2 7.9 %collective-permute-start.8 = (bf16[1312,128]{1,0:T(8,128)(2,1)S(1)}, bf16[1312,128]{1,0:T(8,128)(2,1)S(1)}, u32[]{:S(2)}, u32[]{:S(2)}) collective-permute-start(bf16[1312,128]{1,0:T(8,128)(2,1)S(1)} %pad_maximum_fusion.1), channel_id=1, source_target_pairs={{0,2},{1,3},{2,0},{3,1},{4,6},{5,7},{6,4},{7,5},{8,10},{9,11},{10,... | collective-permute-start | bytes 1007624 | tf_op jit(solution)/shard_map/ppermute | solution.py:193
  22.9 8.7 %collective-permute-start.11 = (bf16[1640,128]{1,0:T(8,128)(2,1)S(1)}, bf16[1640,128]{1,0:T(8,128)(2,1)S(1)}, u32[]{:S(2)}, u32[]{:S(2)}) collective-permute-start(bf16[1640,128]{1,0:T(8,128)(2,1)S(1)} %pad_maximum_fusion), channel_id=1, source_target_pairs={{0,1},{1,0},{2,3},{3,2},{4,5},{5,4},{6,7},{7,6},{8,9},{9,8},{10,11... | collective-permute-start | bytes 1259528 | tf_op jit(solution)/shard_map/ppermute | solution.py:193
  23.2 7.0 %collective-permute-start.9 = (bf16[656,128]{1,0:T(8,128)(2,1)S(1)}, bf16[656,128]{1,0:T(8,128)(2,1)S(1)}, u32[]{:S(2)}, u32[]{:S(2)}) collective-permute-start(bf16[656,128]{1,0:T(8,128)(2,1)S(1)} %constant_dynamic-update-slice_fusion.2), channel_id=1, source_target_pairs={{0,2},{1,3},{2,0},{3,1},{4,6},{5,7},{6,4},{7,5},{8,10},{9,11},{10,... | collective-permute-start | bytes 503816 | tf_op jit(solution)/shard_map/ppermute | solution.py:193
  27.2 4.5 %collective-permute-start.13 = (bf16[1312,128]{1,0:T(8,128)(2,1)S(1)}, bf16[1312,128]{1,0:T(8,128)(2,1)S(1)}, u32[]{:S(2)}, u32[]{:S(2)}) collective-permute-start(bf16[1312,128]{1,0:T(8,128)(2,1)S(1)} %collective-permute-done.8.refs_8_), channel_id=1, source_target_pairs={{0,1},{1,0},{2,3},{3,2},{4,5},{5,4},{6,7},{7,6},{8,9},{9,8},{10,11... | collective-permute-start | bytes 1007624 | tf_op jit(solution)/shard_map/ppermute | solution.py:193
  27.2 3.1 %collective-permute-start.10 = (bf16[984,128]{1,0:T(8,128)(2,1)S(1)}, bf16[984,128]{1,0:T(8,128)(2,1)S(1)}, u32[]{:S(2)}, u32[]{:S(2)}) collective-permute-start(bf16[984,128]{1,0:T(8,128)(2,1)S(1)} %pad_maximum_fusion.2), channel_id=1, source_target_pairs={{0,1},{1,0},{2,3},{3,2},{4,5},{5,4},{6,7},{7,6},{8,9},{9,8},{10,11... | collective-permute-start | bytes 755720 | tf_op jit(solution)/shard_map/ppermute | solution.py:193
  27.8 2.5 %collective-permute-start.12 = (bf16[656,128]{1,0:T(8,128)(2,1)S(1)}, bf16[656,128]{1,0:T(8,128)(2,1)S(1)}, u32[]{:S(2)}, u32[]{:S(2)}) collective-permute-start(bf16[656,128]{1,0:T(8,128)(2,1)S(1)} %constant_dynamic-update-slice_fusion.2), channel_id=1, source_target_pairs={{0,1},{1,0},{2,3},{3,2},{4,5},{5,4},{6,7},{7,6},{8,9},{9,8},{10,11... | collective-permute-start | bytes 503816 | tf_op jit(solution)/shard_map/ppermute | solution.py:193
  30.3 1.4 %collective-permute-start.14 = (bf16[656,128]{1,0:T(8,128)(2,1)S(1)}, bf16[656,128]{1,0:T(8,128)(2,1)S(1)}, u32[]{:S(2)}, u32[]{:S(2)}) collective-permute-start(bf16[656,128]{1,0:T(8,128)(2,1)S(1)} %collective-permute-done.9.refs_9_), channel_id=1, source_target_pairs={{0,1},{1,0},{2,3},{3,2},{4,5},{5,4},{6,7},{7,6},{8,9},{9,8},{10,11... | collective-permute-start | bytes 503816 | tf_op jit(solution)/shard_map/ppermute | solution.py:193
  34.0 8.5 %collective-permute-start.15 = (bf16[328,128]{1,0:T(8,128)(2,1)S(1)}, bf16[328,128]{1,0:T(8,128)(2,1)S(1)}, u32[]{:S(2)}, u32[]{:S(2)}) collective-permute-start(bf16[328,128]{1,0:T(8,128)(2,1)S(1)} %get-tuple-element.36), channel_id=1, source_target_pairs={{0,16},{4,20},{8,24},{12,28},{16,0},{20,4},{24,8},{28,12},{1,17},{... | collective-permute-start | bytes 251912 | tf_op jit(solution)/shard_map/ppermute | solution.py:193
  34.4 8.8 %collective-permute-start.16 = (bf16[328,128]{1,0:T(8,128)(2,1)S(1)}, bf16[328,128]{1,0:T(8,128)(2,1)S(1)}, u32[]{:S(2)}, u32[]{:S(2)}) collective-permute-start(bf16[328,128]{1,0:T(8,128)(2,1)S(1)} %get-tuple-element.37), channel_id=1, source_target_pairs={{0,4},{4,0},{8,12},{12,8},{16,20},{20,16},{24,28},{28,24},{1,5},{5... | collective-permute-start | bytes 251912 | tf_op jit(solution)/shard_map/ppermute | solution.py:193
  35.6 10.4 %collective-permute-start.17 = (bf16[328,128]{1,0:T(8,128)(2,1)S(1)}, bf16[328,128]{1,0:T(8,128)(2,1)S(1)}, u32[]{:S(2)}, u32[]{:S(2)}) collective-permute-start(bf16[328,128]{1,0:T(8,128)(2,1)S(1)} %get-tuple-element.38), channel_id=1, source_target_pairs={{0,20},{4,16},{8,28},{12,24},{16,4},{20,0},{24,12},{28,8},{1,21},{... | collective-permute-start | bytes 251912 | tf_op jit(solution)/shard_map/ppermute | solution.py:193
  38.4 7.6 %collective-permute-start.18 = (bf16[328,128]{1,0:T(8,128)(2,1)S(1)}, bf16[328,128]{1,0:T(8,128)(2,1)S(1)}, u32[]{:S(2)}, u32[]{:S(2)}) collective-permute-start(bf16[328,128]{1,0:T(8,128)(2,1)S(1)} %get-tuple-element.39), channel_id=1, source_target_pairs={{0,8},{4,12},{8,0},{12,4},{16,24},{20,28},{24,16},{28,20},{1,9},{5... | collective-permute-start | bytes 251912 | tf_op jit(solution)/shard_map/ppermute | solution.py:193
  38.9 8.8 %collective-permute-start.19 = (bf16[328,128]{1,0:T(8,128)(2,1)S(1)}, bf16[328,128]{1,0:T(8,128)(2,1)S(1)}, u32[]{:S(2)}, u32[]{:S(2)}) collective-permute-start(bf16[328,128]{1,0:T(8,128)(2,1)S(1)} %get-tuple-element.40), channel_id=1, source_target_pairs={{0,28},{4,24},{8,20},{12,16},{16,12},{20,8},{24,4},{28,0},{1,29},{... | collective-permute-start | bytes 251912 | tf_op jit(solution)/shard_map/ppermute | solution.py:193
  42.5 8.1 %collective-permute-start.20 = (bf16[328,128]{1,0:T(8,128)(2,1)S(1)}, bf16[328,128]{1,0:T(8,128)(2,1)S(1)}, u32[]{:S(2)}, u32[]{:S(2)}) collective-permute-start(bf16[328,128]{1,0:T(8,128)(2,1)S(1)} %get-tuple-element.41), channel_id=1, source_target_pairs={{0,12},{4,8},{8,4},{12,0},{16,28},{20,24},{24,20},{28,16},{1,13},{... | collective-permute-start | bytes 251912 | tf_op jit(solution)/shard_map/ppermute | solution.py:193
  43.2 7.4 %collective-permute-start.21 = (bf16[328,128]{1,0:T(8,128)(2,1)S(1)}, bf16[328,128]{1,0:T(8,128)(2,1)S(1)}, u32[]{:S(2)}, u32[]{:S(2)}) collective-permute-start(bf16[328,128]{1,0:T(8,128)(2,1)S(1)} %get-tuple-element.42), channel_id=1, source_target_pairs={{0,24},{4,28},{8,16},{12,20},{16,8},{20,12},{24,0},{28,4},{1,25},{... | collective-permute-start | bytes 251912 | tf_op jit(solution)/shard_map/ppermute | solution.py:193
